TPU v7x, 512 devices: a whole 4x8x8 slice. The times are simulated.
512 devices in a mesh: expert: 128 (over y, z, core), rep: 4 (over x).
Axes of the slice: x: 4, y: 8, z: 8, core: 2. Of those that a mesh axis runs over, the one named last changes fastest.
Arguments:
- tokens: bfloat16 [16384, 1024], P('expert', 'rep'), may hold values from -6 to 6
- cotangent: bfloat16 [16384, 1024], P('expert', 'rep'), may hold values from -1.796875 to 1.796875
- expert_ids: int32 [16384, 2], P('expert'), may hold values from 0 to 127, all different within a row; in each aligned block of 128 rows (0 to 127, 128 to 255, ...) at most 4 rows name the same one
- gate_values: float32 [16384, 2], P('expert'), may hold values from 0.1 to 0.9
- inner_weight: bfloat16 [128, 1024, 4096], P('expert', None, 'rep'), may hold values from -0.1875 to 0.1875
- outer_weight: bfloat16 [128, 4096, 1024], P('expert', 'rep'), may hold values from -0.09375 to 0.09375
Outputs:
- output: bfloat16 [16384, 1024], P('expert', 'rep')
- input_grads: bfloat16 [16384, 1024], P('expert', 'rep')
- gate_grads: float32 [16384, 2], P('expert')
Inputs may be any that keep to these rules, and one draw needn't show every extreme that they name: `expert_ids`: each token names 2 different experts. Among the 128 tokens of one block no expert is named more than 4 times, a bound that some block reaches.
All inputs are finite; a program needn't handle non-finite values.
Results may differ from a plain program's by a relative error of at most 0.012.
Values may be sent and summed in bfloat16 or wider, within the bound.
No kernel may reach another device: no remote copies, remote signals or barrier semaphores. Data moves between devices by JAX's collectives and lax.ppermute only.
A program may use at most 64 MiB of HBM per device.

v0:
```python
import jax
import jax.numpy as jnp
from jax import lax
from jax.sharding import PartitionSpec as P

TOP = 2


SQRT_TWO_PI = 0.7978845608028654
CUBIC = 0.044715


def in_one_piece(arrays, axis, split_dim, concat_dim, along):
    ends, at = ([], 0)
    for a in arrays[:-1]:
        at += a.shape[along]
        ends.append(at)
    both = jnp.concatenate(arrays, axis=along)
    return tuple(
        jnp.split(
            lax.all_to_all(both, axis, split_axis=split_dim, concat_axis=concat_dim, tiled=True),
            ends,
            axis=along,
        )
    )


def copy_for_each(x, axis):
    peers = lax.axis_size(axis)
    return lax.all_to_all(jnp.broadcast_to(x[None], (peers, *x.shape)), axis, 0, 0, tiled=True)


def laid_out(parts, dim):
    shape = list(parts.shape[1:])
    shape[dim] *= parts.shape[0]
    return jnp.moveaxis(parts, 0, dim).reshape(shape)


def gather_directly(x, axis, dim):
    parts = copy_for_each(x, axis)
    return laid_out(parts, dim)


def side_by_side(arrays, axis, dim, along):
    ends, at = ([], 0)
    for a in arrays[:-1]:
        at += a.shape[along]
        ends.append(at)
    both = jnp.concatenate(arrays, axis=along)
    return tuple(jnp.split(gather_directly(both, axis, dim), ends, axis=along))


def in_blocks(x, dim, peers):
    shape = x.shape
    parts = x.reshape(*shape[:dim], peers, shape[dim] // peers, *shape[dim + 1 :])
    return jnp.moveaxis(parts, dim, 0)


def sum_at_owner(x, axis, dim):
    parts = in_blocks(x, dim, lax.axis_size(axis))
    arrived = lax.all_to_all(parts, axis, split_axis=0, concat_axis=0, tiled=True)
    return arrived.astype(jnp.float32).sum(axis=0)


def of_everyone(x, axis):
    everything = copy_for_each(x, axis)
    return jnp.sum(everything, axis=0)


def gelu_pair(preact):
    argument = SQRT_TWO_PI * (preact + CUBIC * preact * preact * preact)
    tangent = jnp.tanh(argument)
    result = 0.5 * preact * (1.0 + tangent)
    derivative = 0.5 * (1.0 + tangent) + 0.5 * preact * (1.0 - tangent * tangent) * SQRT_TWO_PI * (
        1.0 + 3.0 * CUBIC * preact * preact
    )
    return (result, derivative)


def slot_tables(expert_ids, experts, capacity):
    flat_ids = expert_ids.reshape(-1)
    matches = (flat_ids[:, None] == jnp.arange(experts, dtype=jnp.int32)[None, :]).astype(jnp.int32)
    ranked = jnp.sum((jnp.cumsum(matches, axis=0) - 1) * matches, axis=1)
    target = (flat_ids * capacity + ranked).reshape(expert_ids.shape[0], expert_ids.shape[1]).T
    slot_index = jnp.arange(experts * capacity, dtype=jnp.int32)
    return (slot_index[None, :, None] == target[:, None, :]).astype(jnp.bfloat16)


def build_slots(slot_table, gate_values, token_part, cot_part):
    slot_rows = jnp.dot(
        jnp.sum(slot_table, axis=0), token_part, preferred_element_type=jnp.float32
    ).astype(jnp.bfloat16)
    cot_float = cot_part.astype(jnp.float32)
    grad_acc = jnp.zeros((slot_table.shape[1], token_part.shape[1]), jnp.float32)
    for member in range(TOP):
        scaled = (gate_values[:, member : member + 1] * cot_float).astype(jnp.bfloat16)
        grad_acc = grad_acc + jnp.dot(
            slot_table[member], scaled, preferred_element_type=jnp.float32
        )
    return (slot_rows, grad_acc.astype(jnp.bfloat16))


def per_device(tokens, cotangent, expert_ids, gate_values, inner_weight, outer_weight):
    quarter = tokens.shape[1]
    experts = lax.axis_size("expert") * inner_weight.shape[0]
    capacity = 2 * tokens.shape[0] * TOP // experts
    slot_table = slot_tables(expert_ids, experts, capacity)
    cot_wide = cotangent.astype(jnp.float32)
    slot_rows, slot_grads = build_slots(slot_table, gate_values, tokens, cotangent)
    part_rows, part_grads = in_one_piece(
        (
            slot_rows.reshape(experts, capacity, quarter),
            slot_grads.reshape(experts, capacity, quarter),
        ),
        "expert",
        0,
        0,
        1,
    )
    arrived_rows, arrived_grads = side_by_side((part_rows, part_grads), "rep", 2, 0)
    feature_width = arrived_rows.shape[2]
    expert_rows = arrived_rows.reshape(-1, feature_width)
    expert_grads = arrived_grads.reshape(-1, feature_width)
    slot_count = expert_rows.shape[0]
    inner_block = inner_weight[0]
    outer_block = outer_weight[0]
    preact = jnp.dot(expert_rows, inner_block, preferred_element_type=jnp.float32)
    result, derivative = gelu_pair(preact)
    hidden = result.astype(jnp.bfloat16)
    back_hidden = lax.dot_general(
        expert_grads, outer_block, (((1,), (1,)), ((), ())), preferred_element_type=jnp.float32
    )
    back_pre = (back_hidden * derivative).astype(jnp.bfloat16)
    term_out = lax.dot_general(
        outer_block, hidden, (((0,), (1,)), ((), ())), preferred_element_type=jnp.float32
    )
    term_in = lax.dot_general(
        inner_block, back_pre, (((1,), (1,)), ((), ())), preferred_element_type=jnp.float32
    )
    joined = jnp.concatenate([term_out, term_in], axis=1)
    summed = sum_at_owner(
        joined.astype(jnp.bfloat16).astype(jnp.float32).astype(jnp.bfloat16), "rep", 0
    )
    expert_out = summed[:, :slot_count].T.astype(jnp.bfloat16)
    slot_input = summed[:, slot_count:].T.astype(jnp.bfloat16)
    back_out, back_input = in_one_piece(
        (expert_out.reshape(-1, capacity, quarter), slot_input.reshape(-1, capacity, quarter)),
        "expert",
        0,
        0,
        1,
    )
    back_out = back_out.reshape(-1, quarter)
    back_input = back_input.reshape(-1, quarter)
    combined = jnp.zeros((tokens.shape[0], quarter), jnp.float32)
    in_total = jnp.zeros((tokens.shape[0], quarter), jnp.float32)
    columns = []
    for member in range(TOP):
        picked = lax.dot_general(
            slot_table[member],
            back_out,
            (((0,), (0,)), ((), ())),
            preferred_element_type=jnp.float32,
        )
        combined = combined + gate_values[:, member : member + 1] * picked
        columns.append(jnp.sum(cot_wide * picked, axis=1))
        in_total = in_total + lax.dot_general(
            slot_table[member],
            back_input,
            (((0,), (0,)), ((), ())),
            preferred_element_type=jnp.float32,
        )
    output = combined.astype(jnp.bfloat16)
    input_grads = in_total.astype(jnp.bfloat16)
    gate_grads = of_everyone(jnp.stack(columns, axis=1), "rep")
    return (output, input_grads, gate_grads)


def solution(mesh):
    placed = (
        P("expert", "rep"),
        P("expert", "rep"),
        P("expert", None),
        P("expert", None),
        P("expert", None, "rep"),
        P("expert", "rep", None),
    )
    return jax.shard_map(
        per_device,
        mesh=mesh,
        in_specs=placed,
        out_specs=(P("expert", "rep"), P("expert", "rep"), P("expert", None)),
        check_vma=False,
    )
```

profile of v0, /device:TPU:8, one launch (start us, length us, event | category | flops | bytes accessed | tf_op | source)
XLA Modules:
  0.0 160.2 jit_solution(10295055551137416852)
XLA Ops:
  0.7 1.0 copy.40
  1.6 0.1 eq.43
  1.7 0.1 eq.39
  1.9 0.1 copy.42
  2.0 0.2 fusion.39
  2.4 0.2 fusion.40
  2.5 0.1 reduce_sum.60
  2.7 0.7 add_bitcast_fusion
  3.4 0.1 iota_compare_fusion
  3.6 0.8 slice_bitcast_fusion.11
  4.4 1.0 convolution_convert_fusion
  5.4 0.1 reshape.66
  5.5 0.3 fusion.33
  5.8 0.3 fusion.23
  6.1 0.1 reshape.67
  6.2 0.3 pad_maximum_fusion.1
  6.4 37.5 %all_to_all.25 = bf16[128,8,256]{2,1,0:T(8,128)(2,1)S(1)} all-to-all(bf16[128,8,256]{2,1,0:T(8,128)(2,1)S(1)} %pad_maximum_fusion.1), channel_id=1, replica_groups=mesh['expert'=128,'rep'=4] {'expert'}, dimensions={0} | all-to-all | bytes 1048576 | tf_op jit(solution)/shard_map/all_to_all | solution.py:21
  43.9 0.2 fusion.58
  44.1 0.3 pad_maximum_fusion.2
  44.4 0.5 broadcast_in_dim.4
  45.0 29.5 %all_to_all.26 = bf16[4,256,4,256]{3,2,1,0:T(4,128)(2,1)S(1)} all-to-all(bf16[4,256,4,256]{3,2,1,0:T(4,128)(2,1)S(1)} %broadcast_in_dim.4), channel_id=1, replica_groups=mesh['expert'=128,'rep'=4] {'rep'}, dimensions={0} | all-to-all | bytes 4194304 | tf_op jit(solution)/shard_map/all_to_all | solution.py:30
  74.5 0.7 fusion.56
  75.2 1.4 copy.46
  76.6 0.2 copy.52
  76.8 1.4 copy.45
  78.2 0.2 copy.51
  78.4 1.3 fusion.13
  79.7 0.3 copy-done.3
  80.0 2.4 %fusion.18 = bf16[512,1024]{1,0:T(8,128)(2,1)} fusion(bf16[1,1024,1024]{2,1,0:T(8,128)(2,1)S(1)} %copy-done.3, f32[512,1024]{1,0:T(8,128)S(1)} %fusion.13), kind=kOutput, calls=%fused_computation.20 | convolution fusion | flops 1078984704 | bytes 5242880 | tf_op jit(solution)/shard_map/dot_general | solution.py:134
  82.4 5.9 %fusion.15 = bf16[512,1024]{1,0:T(8,128)(2,1)} fusion(bf16[1,1024,1024]{2,1,0:T(8,128)(2,1)S(1)} %copy-done, f32[512,1024]{1,0:T(8,128)} %copy-done.4, bf16[512,1024]{1,0:T(8,128)(2,1)S(1)} %bitcast.76, bf16[1,1024,1024]{2,1,0:T(8,128)(2,1)} %param.11), kind=kOutput, calls=%fused_computation.19 | convolution fusion | flops 2157969408 | bytes 8388608 | tf_op jit(solution)/shard_map/dot_general | solution.py:137
  88.3 1.7 %copy_bitcast_fusion = (bf16[4,256,512]{1,2,0:T(8,128)(2,1)S(1)}, bf16[4,256,512]{1,2,0:T(8,128)(2,1)S(1)}) fusion(bf16[64,4,8,256]{3,2,1,0:T(8,128)(2,1)} %bitcast.79, bf16[64,4,8,256]{3,2,1,0:T(8,128)(2,1)} %bitcast.78), kind=kLoop, calls=%fused_computation.26 | loop fusion | bytes 4194304 | tf_op jit(solution)/shard_map/concatenate | solution.py:140
  90.0 0.1 pad_maximum_fusion
  90.1 27.8 %all_to_all.27 = bf16[4,256,1024]{1,2,0:T(8,128)(2,1)} all-to-all(bf16[4,256,1024]{1,2,0:T(8,128)(2,1)S(1)} %pad_maximum_fusion), channel_id=1, replica_groups=mesh['expert'=128,'rep'=4] {'rep'}, dimensions={0} | all-to-all | bytes 4194304 | tf_op jit(solution)/shard_map/all_to_all | solution.py:61
  117.9 2.2 %reduce.1 = bf16[256,1024]{0,1:T(8,128)(2,1)S(1)} reduce(bf16[4,256,1024]{1,2,0:T(8,128)(2,1)} %all_to_all.27, bf16[]{:T(256)} %constant.8.clone.1), dimensions={0}, to_apply=%region_4.5.clone | reduce | flops 786432 | bytes 2621442 | tf_op jit(solution)/shard_map/reduce_sum | solution.py:62
  120.2 0.1 reshape.70
  120.2 0.1 reshape.71
  120.3 0.3 pad_maximum_fusion.3
  120.6 28.0 %all_to_all.28 = bf16[128,8,256]{2,1,0:T(8,128)(2,1)S(1)} all-to-all(bf16[128,8,256]{2,1,0:T(8,128)(2,1)S(1)} %pad_maximum_fusion.3), channel_id=1, replica_groups=mesh['expert'=128,'rep'=4] {'expert'}, dimensions={0} | all-to-all | bytes 1048576 | tf_op jit(solution)/shard_map/all_to_all | solution.py:21
  148.6 0.2 fusion.57
  148.8 0.1 reshape.73
  148.9 0.3 fusion.31
  149.2 0.3 fusion.34
  149.5 1.0 fusion.37
  150.5 0.6 broadcast_in_dim.5
  151.1 3.2 %all-to-all-start.4 = ((f32[4,128,2]{1,2,0:T(2,128)}), f32[4,128,2]{1,2,0:T(2,128)S(1)}, u32[]{:S(2)}, u32[]{:S(2)}) async-start(f32[4,128,2]{1,2,0:T(2,128)} %broadcast_in_dim.5), calls=%async_computation.4 | async-start | bytes 8192 | tf_op jit(solution)/shard_map/all_to_all | solution.py:30
  154.3 0.9 fusion.24
  155.2 4.4 %all-to-all-done.4 = f32[4,128,2]{1,2,0:T(2,128)S(1)} async-done(((f32[4,128,2]{1,2,0:T(2,128)}), f32[4,128,2]{1,2,0:T(2,128)S(1)}, u32[]{:S(2)}, u32[]{:S(2)}) %all-to-all-start.4) | async-done | bytes 4128 | tf_op jit(solution)/shard_map/all_to_all | solution.py:30
  159.6 0.6 reduce_sum.65
  (19 shorter events, 0.4 us)
Async XLA Ops:
  0.6 77.8 %copy-start = (bf16[1,1024,1024]{2,1,0:T(8,128)(2,1)S(1)}, bf16[1,1024,1024]{2,1,0:T(8,128)(2,1)}, u32[]{:S(2)}) copy-start(bf16[1,1024,1024]{2,1,0:T(8,128)(2,1)} %param.10) | copy-start | bytes 6291460
  0.6 4.8 %copy-start.1 = (bf16[128,256]{1,0:T(8,128)(2,1)S(1)}, bf16[128,256]{1,0:T(8,128)(2,1)}, u32[]{:S(2)}) copy-start(bf16[128,256]{1,0:T(8,128)(2,1)} %param.7) | copy-start | bytes 196612
  78.4 1.6 copy-start.3
  80.0 2.4 %copy-start.4 = (f32[512,1024]{1,0:T(8,128)}, f32[512,1024]{1,0:T(8,128)S(1)}, u32[]{:S(2)}) copy-start(f32[512,1024]{1,0:T(8,128)S(1)} %fusion.13) | copy-start | bytes 6291460
  120.6 28.9 %copy-start.2 = (bf16[128,256]{1,0:T(8,128)(2,1)S(1)}, bf16[128,256]{1,0:T(8,128)(2,1)}, u32[]{:S(2)}) copy-start(bf16[128,256]{1,0:T(8,128)(2,1)} %param.7) | copy-start | bytes 196612
  151.1 8.5 %all-to-all-start.4 = ((f32[4,128,2]{1,2,0:T(2,128)}), f32[4,128,2]{1,2,0:T(2,128)S(1)}, u32[]{:S(2)}, u32[]{:S(2)}) async-start(f32[4,128,2]{1,2,0:T(2,128)} %broadcast_in_dim.5), calls=%async_computation.4 | async-start | bytes 8192 | tf_op jit(solution)/shard_map/all_to_all | solution.py:30
where the time goes:
time: 161 us; the launch traced here: 160 us
  blocking collectives  123 us (76%)
  matrix products  13.6 us (8%)
  local copies, waits for them, and re-layouts  10.1 us (6%)
  other arithmetic  5.1 us (3%)
  waiting for transfers between devices  4.36 us (3%)
  starting transfers between devices  3.24 us (2%)
    all_to_all x2, blocking collectives, in_one_piece(): lax.all_to_all(both, axis, split_axis=split_dim, concat_axis=concat_dim,...  65.5 us
    all_to_all x1, blocking collectives, copy_for_each(): lax.all_to_all(jnp.broadcast_to(x[None], (peers, *x.shape)), axis, 0, 0,...  29.5 us
    all_to_all x1, blocking collectives, sum_at_owner(): lax.all_to_all(parts, axis, split_axis=0, concat_axis=0, tiled=True)  27.8 us
    dot_general x1, matrix products, per_device(): lax.dot_general(inner_block, back_pre, (((1,), (1,)), ((), ())), preferre...  5.91 us
    all_to_all x1, waiting for transfers between devices, copy_for_each(): lax.all_to_all(jnp.broadcast_to(x[None], (peers, *x.shape)), axis, 0, 0,...  4.36 us
    split x3, local copies, waits for them, and re-layouts, side_by_side(): return tuple(jnp.split(gather_directly(both, axis, dim), ends, axis=along))  3.43 us
    all_to_all x1, starting transfers between devices, copy_for_each(): lax.all_to_all(jnp.broadcast_to(x[None], (peers, *x.shape)), axis, 0, 0,...  3.24 us
  transfers between devices with their start and end apart: 1, of which 1 were waited for; matrix products, arithmetic and copies ran while one was open for 1% of the time, Pallas kernels for 0%

commit v1 on v0

v1 whole, which is shorter than its diff:
```python
import jax
import jax.numpy as jnp
from jax import lax
from jax.experimental import pallas as pl
from jax.experimental.pallas import tpu as pltpu
from jax.sharding import PartitionSpec as P

TOP = 2
EXTRA = 16

SQRT_TWO_PI = 0.7978845608028654
CUBIC = 0.044715

PARAMS = pltpu.CompilerParams(vmem_limit_bytes=24 * 1024 * 1024)


def iota(shape, dim):
    return lax.broadcasted_iota(jnp.int32, shape, dim)


def slot_positions(ids, experts, capacity):
    rows = ids.shape[1]
    of_expert = iota((experts, rows), 0)
    named = [of_expert == ids[k : k + 1, :] for k in range(TOP)]
    both = sum(jnp.where(m, 1.0, 0.0) for m in named)
    earlier = jnp.where(iota((rows, rows), 0) < iota((rows, rows), 1), 1.0, 0.0)
    before = jnp.dot(
        both.astype(jnp.bfloat16), earlier.astype(jnp.bfloat16), preferred_element_type=jnp.float32
    )
    ranks = [jnp.sum(jnp.where(m, before, 0.0), axis=0, keepdims=True) for m in named]
    return [ids[k : k + 1, :] * capacity + ranks[k].astype(jnp.int32) for k in range(TOP)]


def column_of(row):
    n = row.shape[1]
    eye = iota((n, n), 0) == iota((n, n), 1)
    return jnp.sum(jnp.where(eye, row, jnp.zeros_like(row)), axis=1, keepdims=True)


def row_of(column):
    n = column.shape[0]
    eye = iota((n, n), 0) == iota((n, n), 1)
    return jnp.sum(jnp.where(eye, column, jnp.zeros_like(column)), axis=0, keepdims=True)


def pack_kernel(
    experts, capacity, ids_in, token_in, cot_in, out_ref, ids_ref, token_ref, cot_ref, sems
):
    copies = [
        pltpu.make_async_copy(src, dst, sems.at[i])
        for i, (src, dst) in enumerate(
            ((ids_in, ids_ref), (token_in, token_ref), (cot_in, cot_ref))
        )
    ]
    for copy in copies:
        copy.start()
    copies[0].wait()
    quarter = token_ref.shape[1]
    positions = slot_positions(ids_ref[...], experts, capacity)
    slot = iota((experts * capacity, token_ref.shape[0]), 0)
    hit = slot == positions[0]
    for k in range(1, TOP):
        hit = hit | (slot == positions[k])
    table = jnp.where(hit, 1.0, 0.0).astype(jnp.bfloat16)
    for part, ref in enumerate((token_ref, cot_ref)):
        copies[1 + part].wait()
        out_ref[:, part * quarter : (part + 1) * quarter] = jnp.dot(
            table, ref[...], preferred_element_type=jnp.float32
        ).astype(jnp.bfloat16)


def fetch(source, target, sem):
    copy = pltpu.make_async_copy(source, target, sem)
    copy.start()
    return copy


def forward_kernel(
    rows_ref,
    inner_in,
    outer_in,
    outs_out,
    hidden_out,
    slope_out,
    inner_ref,
    outer_ref,
    outs_ref,
    hidden_ref,
    slope_ref,
    pre_ref,
    sems,
):
    parts, slots, quarter = rows_ref.shape
    piece = [slice(q * quarter, (q + 1) * quarter) for q in range(parts)]
    inner_copies = [
        fetch(inner_in.at[piece[q], :], inner_ref.at[piece[q], :], sems.at[q]) for q in range(parts)
    ]
    outer_copy = fetch(outer_in, outer_ref, sems.at[parts])
    acc = None
    for q in range(parts):
        inner_copies[q].wait()
        term = jnp.dot(rows_ref[q], inner_ref[piece[q], :], preferred_element_type=jnp.float32)
        acc = term if acc is None else acc + term
    pre_ref[...] = acc
    step = 16

    def activate(i, carry):
        at = pl.ds(pl.multiple_of(i * step, step), step)
        u = pre_ref[at, :]
        tangent = jnp.tanh(SQRT_TWO_PI * (u + CUBIC * u * u * u))
        hidden_ref[at, :] = (0.5 * u * (1.0 + tangent)).astype(jnp.bfloat16)
        slope_ref[at, :] = (
            0.5 * (1.0 + tangent)
            + 0.5
            * u
            * (1.0 - tangent * tangent)
            * SQRT_TWO_PI
            * (1.0 + 3.0 * CUBIC * u * u)
        )
        return carry

    lax.fori_loop(0, slots // step, activate, 0)
    saves = [
        fetch(hidden_ref, hidden_out, sems.at[parts + 1]),
        fetch(slope_ref, slope_out, sems.at[parts + 2]),
    ]
    outer_copy.wait()
    for q in range(parts):
        outs_ref[q] = jnp.dot(
            hidden_ref[...], outer_ref[:, piece[q]], preferred_element_type=jnp.float32
        ).astype(jnp.bfloat16)
        saves.append(fetch(outs_ref.at[q], outs_out.at[q], sems.at[parts + 3 + q]))
    for copy in saves:
        copy.wait()


def backward_kernel(parts, me_ref, *refs):
    cot_ins = refs[:parts]
    hidden_in, slope_in, inner_in, outer_in, in_ref = refs[parts : parts + 5]
    (cot_ref, hidden_ref, slope_ref, inner_ref, outer_ref) = refs[parts + 5 : parts + 10]
    back_ref, grad_ref, pre_ref, sems = refs[parts + 10 :]
    slots, quarter = cot_ref.shape[1:]
    width = back_ref.shape[1]
    across = (((1,), (1,)), ((), ()))
    outer_copy = fetch(outer_in, outer_ref, sems.at[parts])
    cot_copies = [fetch(cot_ins[q], cot_ref.at[q], sems.at[q]) for q in range(parts)]
    later = [
        fetch(source, target, sems.at[parts + 1 + i])
        for i, (source, target) in enumerate(
            ((slope_in, slope_ref), (hidden_in, hidden_ref), (inner_in, inner_ref))
        )
    ]
    outer_copy.wait()
    acc = None
    for shift in range(parts):
        source = lax.rem(me_ref[0] + parts - shift, parts)
        columns = pl.ds(pl.multiple_of(source * quarter, quarter), quarter)
        cot_copies[shift].wait()
        term = lax.dot_general(
            cot_ref[shift], outer_ref[:, columns], across, preferred_element_type=jnp.float32
        )
        acc = term if acc is None else acc + term
    back_ref[...] = acc
    for copy in later:
        copy.wait()
    step = 16

    def activate(i, carry):
        at = pl.ds(pl.multiple_of(i * step, step), step)
        back = back_ref[at, :]
        pre_ref[at, :] = (back * slope_ref[at, :]).astype(jnp.bfloat16)
        product = back * hidden_ref[at, :].astype(jnp.float32)
        folded = product[:, :128]
        for j in range(1, width // 128):
            folded = folded + product[:, j * 128 : (j + 1) * 128]
        grad_ref[at, :] = folded
        return carry

    lax.fori_loop(0, slots // step, activate, 0)
    gate = lax.dot_general(
        jnp.ones((8, 128), jnp.float32),
        grad_ref[...],
        across,
        precision=lax.Precision.HIGHEST,
        preferred_element_type=jnp.float32,
    )[:1, :]
    high = gate.astype(jnp.bfloat16).astype(jnp.float32)
    low = gate - high
    place = iota((EXTRA, quarter), 0)
    extra = jnp.zeros((EXTRA, quarter), jnp.float32)
    for j in range(slots // quarter):
        piece = slice(j * quarter, (j + 1) * quarter)
        extra = jnp.where(place == 2 * j, high[:, piece], extra)
        extra = jnp.where(place == 2 * j + 1, low[:, piece], extra)
    for q in range(parts):
        in_ref[q, :slots, :] = lax.dot_general(
            pre_ref[...],
            inner_ref[q * quarter : (q + 1) * quarter, :],
            across,
            preferred_element_type=jnp.float32,
        ).astype(jnp.bfloat16)
        in_ref[q, slots:, :] = extra.astype(jnp.bfloat16)


def add_kernel(outs_ref, ins_ref, sum_ref):
    parts, slots, quarter = outs_ref.shape
    step = 16

    def add(i, carry):
        at = pl.ds(pl.multiple_of(i * step, step), step)
        total = outs_ref[0, at, :].astype(jnp.float32)
        other = ins_ref[0, at, :].astype(jnp.float32)
        for q in range(1, parts):
            total = total + outs_ref[q, at, :].astype(jnp.float32)
            other = other + ins_ref[q, at, :].astype(jnp.float32)
        sum_ref[at, :quarter] = total.astype(jnp.bfloat16)
        sum_ref[at, quarter : 2 * quarter] = other.astype(jnp.bfloat16)
        return carry

    lax.fori_loop(0, slots // step, add, 0)
    extra = ins_ref[0, slots:, :].astype(jnp.float32)
    for q in range(1, parts):
        extra = extra + ins_ref[q, slots:, :].astype(jnp.float32)
    lane = iota((128, 128), 1)
    for j in range(slots // 128):
        at, lanes = divmod(j * 128, quarter)
        gate = column_of(
            extra[2 * at : 2 * at + 1, lanes : lanes + 128]
            + extra[2 * at + 1 : 2 * at + 2, lanes : lanes + 128]
        )
        high = gate.astype(jnp.bfloat16).astype(jnp.float32)
        low = gate - high
        sum_ref[j * 128 : (j + 1) * 128, 2 * quarter :] = jnp.where(
            lane == 0, high, jnp.where(lane == 1, low, 0.0)
        ).astype(jnp.bfloat16)


def table_kernel(experts, capacity, ids_ref, table_ref):
    rows = ids_ref.shape[1]
    positions = slot_positions(ids_ref[...], experts, capacity)
    slot = iota((rows, experts * capacity), 1)
    for k in range(TOP):
        hit = slot == column_of(positions[k])
        table_ref[k * rows : (k + 1) * rows, :] = jnp.where(hit, 1.0, 0.0).astype(jnp.bfloat16)


def combine_kernel(table_ref, gates_ref, back_ref, out_ref, in_ref, gate_ref):
    rows, quarter = out_ref.shape
    total = None
    for k in range(TOP):
        picked = jnp.dot(
            table_ref[k * rows : (k + 1) * rows, :],
            back_ref[...],
            preferred_element_type=jnp.float32,
        )
        term = column_of(gates_ref[k : k + 1, :]) * picked[:, : 2 * quarter]
        total = term if total is None else total + term
        gate = picked[:, 2 * quarter : 2 * quarter + 1] + picked[:, 2 * quarter + 1 : 2 * quarter + 2]
        gate_ref[k : k + 1, :] = row_of(gate)
    out_ref[...] = total[:, :quarter].astype(jnp.bfloat16)
    in_ref[...] = total[:, quarter:].astype(jnp.bfloat16)


def to_everyone(x, axis):
    peers = lax.axis_size(axis)
    return lax.all_to_all(jnp.broadcast_to(x[None], (peers, *x.shape)), axis, 0, 0, tiled=True)


def shape_of(shape, dtype):
    return jax.ShapeDtypeStruct(shape, dtype)


def in_hbm(x):
    return pltpu.with_memory_space_constraint(x, pltpu.HBM)


def exchange(tokens, cotangent, expert_ids, gate_values, inner_weight, outer_weight):
    rows, quarter = tokens.shape
    peers = lax.axis_size("expert")
    experts = peers * inner_weight.shape[0]
    capacity = 2 * rows * TOP // experts
    slots = experts * capacity
    parts = lax.axis_size("rep")
    inner, outer = in_hbm(inner_weight[0]), in_hbm(outer_weight[0])
    depth, width = inner.shape
    ids, gates = expert_ids.T, gate_values.T
    any_spec = pl.BlockSpec(memory_space=pltpu.HBM)
    vmem_spec = pl.BlockSpec(memory_space=pltpu.VMEM)
    half, full = jnp.bfloat16, jnp.float32

    packed = pl.pallas_call(
        lambda *refs: pack_kernel(experts, capacity, *refs),
        out_shape=shape_of((slots, 2 * quarter), half),
        in_specs=[any_spec] * 3,
        scratch_shapes=[
            pltpu.VMEM(ids.shape, ids.dtype),
            pltpu.VMEM(tokens.shape, tokens.dtype),
            pltpu.VMEM(cotangent.shape, cotangent.dtype),
            pltpu.SemaphoreType.DMA((3,)),
        ],
        compiler_params=PARAMS,
        name="pack",
    )(in_hbm(ids), in_hbm(tokens), in_hbm(cotangent))
    arrived = lax.all_to_all(
        packed.reshape(peers, -1, 2 * quarter), "expert", 0, 0, tiled=True
    ).reshape(slots, 2 * quarter)
    cots = arrived[:, quarter:]
    all_rows = to_everyone(arrived[:, :quarter], "rep")
    all_cots = [cots] + [
        lax.ppermute(cots, "rep", [(i, (i + shift) % parts) for i in range(parts)])
        for shift in range(1, parts)
    ]
    table = pl.pallas_call(
        lambda *refs: table_kernel(experts, capacity, *refs),
        out_shape=shape_of((TOP * rows, slots), half),
        compiler_params=PARAMS,
        name="table",
    )(ids)
    me = lax.axis_index("rep").astype(jnp.int32).reshape(1)

    outs, hidden, slope = pl.pallas_call(
        forward_kernel,
        out_shape=(
            pltpu.HBM((parts, slots, quarter), half),
            pltpu.HBM((slots, width), half),
            pltpu.HBM((slots, width), full),
        ),
        in_specs=[vmem_spec, any_spec, any_spec],
        out_specs=(any_spec, any_spec, any_spec),
        scratch_shapes=[
            pltpu.VMEM((depth, width), half),
            pltpu.VMEM((width, depth), half),
            pltpu.VMEM((parts, slots, quarter), half),
            pltpu.VMEM((slots, width), half),
            pltpu.VMEM((slots, width), full),
            pltpu.VMEM((slots, width), full),
            pltpu.SemaphoreType.DMA((2 * parts + 3,)),
        ],
        compiler_params=PARAMS,
        name="forward",
    )(all_rows, inner, outer)
    outs = lax.all_to_all(outs, "rep", 0, 0, tiled=True)
    ins = pl.pallas_call(
        lambda *refs: backward_kernel(parts, *refs),
        out_shape=shape_of((parts, slots + EXTRA, quarter), half),
        in_specs=[pl.BlockSpec(memory_space=pltpu.SMEM)] + [any_spec] * (parts + 4),
        scratch_shapes=[
            pltpu.VMEM((parts, slots, quarter), half),
            pltpu.VMEM((slots, width), half),
            pltpu.VMEM((slots, width), full),
            pltpu.VMEM((depth, width), half),
            pltpu.VMEM((width, depth), half),
            pltpu.VMEM((slots, width), full),
            pltpu.VMEM((slots, 128), full),
            pltpu.VMEM((slots, width), half),
            pltpu.SemaphoreType.DMA((parts + 4,)),
        ],
        compiler_params=PARAMS,
        name="backward",
    )(me, *[in_hbm(x) for x in all_cots], in_hbm(hidden), in_hbm(slope), inner, outer)
    ins = lax.all_to_all(ins, "rep", 0, 0, tiled=True)
    summed = pl.pallas_call(
        add_kernel,
        out_shape=shape_of((slots, 2 * quarter + 128), half),
        compiler_params=PARAMS,
        name="add",
    )(outs, ins)
    back = lax.all_to_all(
        summed.reshape(peers, -1, 2 * quarter + 128), "expert", 0, 0, tiled=True
    ).reshape(slots, 2 * quarter + 128)
    output, input_grads, gate_grads = pl.pallas_call(
        combine_kernel,
        out_shape=(
            shape_of((rows, quarter), half),
            shape_of((rows, quarter), half),
            shape_of((TOP, rows), full),
        ),
        compiler_params=PARAMS,
        name="combine",
    )(table, gates, back)
    return output, input_grads, gate_grads.T


def solution(mesh):
    placed = (
        P("expert", "rep"),
        P("expert", "rep"),
        P("expert", None),
        P("expert", None),
        P("expert", None, "rep"),
        P("expert", "rep", None),
    )
    return jax.shard_map(
        exchange,
        mesh=mesh,
        in_specs=placed,
        out_specs=(P("expert", "rep"), P("expert", "rep"), P("expert", None)),
        check_vma=False,
    )
```

time: 161 us -> 151 us (0.938)
  the two profiles are of different devices: /device:TPU:8 before, /device:TPU:1 now
where the time goes in v1:
time: 151 us
  blocking collectives  73 us (48%)
  waiting for transfers between devices  35 us (23%)
  starting transfers between devices  24.3 us (16%)
  Pallas kernels  15.4 us (10%)
  local copies, waits for them, and re-layouts  2.22 us (1%)
    all_to_all x1, blocking collectives, exchange(): lax.all_to_all(packed.reshape(peers, -1, 2 * quarter), 'expert', 0, 0, ti...  37.6 us
    all_to_all x1, waiting for transfers between devices, exchange(): lax.all_to_all(summed.reshape(peers, -1, 2 * quarter + 128), 'expert', 0,...  21.8 us
    all_to_all x1, blocking collectives, exchange(): ins = lax.all_to_all(ins, 'rep', 0, 0, tiled=True)  18.7 us
    all_to_all x1, blocking collectives, to_everyone(): lax.all_to_all(jnp.broadcast_to(x[None], (peers, *x.shape)), axis, 0, 0,...  16.6 us
    ppermute x3, waiting for transfers between devices, exchange(): lax.ppermute(cots, 'rep', [(i, (i + shift) % parts) for i in range(parts)])  13.2 us
    ppermute x3, starting transfers between devices, exchange(): lax.ppermute(cots, 'rep', [(i, (i + shift) % parts) for i in range(parts)])  10.7 us
    all_to_all x1, starting transfers between devices, exchange(): lax.all_to_all(summed.reshape(peers, -1, 2 * quarter + 128), 'expert', 0,...  10 us
    pallas_call x1, Pallas kernels, exchange(): pl.pallas_call(forward_kernel, out_shape=(pltpu.HBM((parts, slots, quarte...  6.32 us
  transfers between devices with their start and end apart: 5, of which 4 were waited for; matrix products, arithmetic and copies ran while one was open for 0% of the time, Pallas kernels for 4%

profile of v1, /device:TPU:1, one launch (start us, length us, event | category | flops | bytes accessed | tf_op | source)
XLA Modules:
  0.0 150.7 jit_solution(7079212165993686220)
XLA Ops:
  0.6 1.4 pack.1
  2.1 0.1 reshape.22
  2.2 37.6 %all_to_all.25 = bf16[128,4,512]{2,1,0:T(4,128)(2,1)S(1)} all-to-all(bf16[128,4,512]{2,1,0:T(4,128)(2,1)S(1)} %reshape.22), channel_id=1, replica_groups=mesh['expert'=128,'rep'=4] {'expert'}, dimensions={0} | all-to-all | bytes 1048576 | tf_op jit(solution)/shard_map/all_to_all | solution.py:304
  39.9 0.1 reshape.23
  40.0 0.0 copy-start.2
  40.0 0.1 broadcast_in_dim.2
  40.1 16.6 %all_to_all.26.rows_ref = bf16[4,512,256]{2,1,0:T(8,128)(2,1)S(1)} all-to-all(bf16[4,512,256]{2,1,0:T(8,128)(2,1)S(1)} %broadcast_in_dim.2), channel_id=1, replica_groups=mesh['expert'=128,'rep'=4] {'rep'}, dimensions={0} | all-to-all | bytes 2097152 | tf_op jit(solution)/shard_map/all_to_all | solution.py:266
  56.8 6.3 %forward.1 = (bf16[4,512,256]{2,1,0:T(8,128)(2,1)}, bf16[512,1024]{1,0:T(8,128)(2,1)}, f32[512,1024]{1,0:T(8,128)}) custom-call(bf16[4,512,256]{2,1,0:T(8,128)(2,1)S(1)} %all_to_all.26.rows_ref, bf16[1024,1024]{1,0:T(8,128)(2,1)} %bitcast.9, bf16[1024,1024]{1,0:T(8,128)(2,1)} %bitcast.11), custom_call_target="tpu_custom_call" | custom-call | tf_op jit(solution)/shard_map/forward/pallas_call | solution.py:321
  63.1 3.5 %all-to-all-start.2 = ((bf16[4,512,256]{2,1,0:T(8,128)(2,1)}), bf16[4,512,256]{2,1,0:T(8,128)(2,1)S(1)}, u32[]{:S(2)}, u32[]{:S(2)}) async-start(bf16[4,512,256]{2,1,0:T(8,128)(2,1)} %get-tuple-element.9), calls=%async_computation.2 | async-start | bytes 2097152 | tf_op jit(solution)/shard_map/all_to_all | solution.py:342
  66.6 3.3 %collective-permute-start = (bf16[512,256]{1,0:T(8,128)(2,1)S(1)}, bf16[512,256]{1,0:T(8,128)(2,1)S(1)}, u32[]{:S(2)}, u32[]{:S(2)}) collective-permute-start(bf16[512,256]{1,0:T(8,128)(2,1)S(1)} %get-tuple-element.15.refs_1_), channel_id=1, source_target_pairs={{0,1},{1,2},{2,3},{3,0},{4,5},{5,6},{6,7},{7,4},{8,9},{9,10},{10,1... | collective-permute-start | bytes 786440 | tf_op jit(solution)/shard_map/ppermute | solution.py:310
  69.9 4.3 %collective-permute-start.1 = (bf16[512,256]{1,0:T(8,128)(2,1)S(1)}, bf16[512,256]{1,0:T(8,128)(2,1)S(1)}, u32[]{:S(2)}, u32[]{:S(2)}) collective-permute-start(bf16[512,256]{1,0:T(8,128)(2,1)S(1)} %get-tuple-element.15.refs_1_), channel_id=1, source_target_pairs={{0,2},{1,3},{2,0},{3,1},{4,6},{5,7},{6,4},{7,5},{8,10},{9,11},{10,... | collective-permute-start | bytes 786440 | tf_op jit(solution)/shard_map/ppermute | solution.py:310
  74.3 0.0 copy-done.2
  74.3 3.1 %collective-permute-start.2 = (bf16[512,256]{1,0:T(8,128)(2,1)S(1)}, bf16[512,256]{1,0:T(8,128)(2,1)S(1)}, u32[]{:S(2)}, u32[]{:S(2)}) collective-permute-start(bf16[512,256]{1,0:T(8,128)(2,1)S(1)} %get-tuple-element.15.refs_1_), channel_id=1, source_target_pairs={{0,3},{1,0},{2,1},{3,2},{4,7},{5,4},{6,5},{7,6},{8,11},{9,8},{10,9... | collective-permute-start | bytes 786440 | tf_op jit(solution)/shard_map/ppermute | solution.py:310
  77.4 5.4 %collective-permute-done.refs_2_ = bf16[512,256]{1,0:T(8,128)(2,1)S(1)} collective-permute-done((bf16[512,256]{1,0:T(8,128)(2,1)S(1)}, bf16[512,256]{1,0:T(8,128)(2,1)S(1)}, u32[]{:S(2)}, u32[]{:S(2)}) %collective-permute-start) | collective-permute-done | bytes 262176 | tf_op jit(solution)/shard_map/ppermute | solution.py:310
  82.8 0.0 copy-start.3
  82.8 6.7 %collective-permute-done.1.refs_3_ = bf16[512,256]{1,0:T(8,128)(2,1)S(1)} collective-permute-done((bf16[512,256]{1,0:T(8,128)(2,1)S(1)}, bf16[512,256]{1,0:T(8,128)(2,1)S(1)}, u32[]{:S(2)}, u32[]{:S(2)}) %collective-permute-start.1) | collective-permute-done | bytes 262176 | tf_op jit(solution)/shard_map/ppermute | solution.py:310
  89.6 0.0 copy-start.4
  89.6 1.0 collective-permute-done.2.refs_4_
  90.6 0.0 copy-start.5
  90.6 0.0 copy-done.3
  90.6 0.0 copy-done.4
  90.6 0.7 copy-done.5
  91.3 5.5 %backward.1 = bf16[4,528,256]{2,1,0:T(8,128)(2,1)S(1)} custom-call(s32[1]{0:T(128)} %bitcast.4.refs_0_, bf16[512,256]{1,0:T(8,128)(2,1)} %copy-done.2, bf16[512,256]{1,0:T(8,128)(2,1)} %copy-done.3, bf16[512,256]{1,0:T(8,128)(2,1)} %copy-done.4, bf16[512,256]{1,0:T(8,128)(2,1)} %copy-done.5, bf16[512,1024]{1,0:T(8,128)(2,1)} %get-tuple-element.10.refs_5_, ...), custom_call_target="tpu_custom_call" | custom-call | tf_op jit(solution)/shard_map/backward/pallas_call | solution.py:343
  96.9 0.0 all-to-all-done.2.outs_ref
  96.9 18.7 %all_to_all.27.ins_ref = bf16[4,528,256]{2,1,0:T(8,128)(2,1)S(1)} all-to-all(bf16[4,528,256]{2,1,0:T(8,128)(2,1)S(1)} %backward.1), channel_id=1, replica_groups=mesh['expert'=128,'rep'=4] {'rep'}, dimensions={0} | all-to-all | bytes 2162688 | tf_op jit(solution)/shard_map/all_to_all | solution.py:361
  115.6 0.0 copy-start
  115.6 0.6 add.1
  116.1 0.0 copy-start.1
  116.1 1.0 reshape.25
  117.1 10.0 %all-to-all-start.4 = ((bf16[128,4,640]{2,1,0:T(4,128)(2,1)}), bf16[128,4,640]{2,1,0:T(4,128)(2,1)S(1)}, u32[]{:S(2)}, u32[]{:S(2)}) async-start(bf16[128,4,640]{2,1,0:T(4,128)(2,1)} %reshape.25), calls=%async_computation.4 | async-start | bytes 1310720 | tf_op jit(solution)/shard_map/all_to_all | solution.py:368
  127.2 0.0 copy-done
  127.2 0.3 table.1.table_ref
  127.5 21.8 %all-to-all-done.4 = bf16[128,4,640]{2,1,0:T(4,128)(2,1)S(1)} async-done(((bf16[128,4,640]{2,1,0:T(4,128)(2,1)}), bf16[128,4,640]{2,1,0:T(4,128)(2,1)S(1)}, u32[]{:S(2)}, u32[]{:S(2)}) %all-to-all-start.4) | async-done | bytes 655392 | tf_op jit(solution)/shard_map/all_to_all | solution.py:368
  149.3 0.1 reshape.26.back_ref
  149.5 0.0 copy-done.1
  149.5 1.2 combine.1
  (1 shorter events, 0.0 us)
Async XLA Ops:
  40.0 34.2 %copy-start.2 = (bf16[512,256]{1,0:T(8,128)(2,1)}, bf16[512,256]{1,0:T(8,128)(2,1)S(1)}, u32[]{:S(2)}) copy-start(bf16[512,256]{1,0:T(8,128)(2,1)S(1)} %get-tuple-element.15.refs_1_) | copy-start | bytes 786436
  63.1 33.8 %all-to-all-start.2 = ((bf16[4,512,256]{2,1,0:T(8,128)(2,1)}), bf16[4,512,256]{2,1,0:T(8,128)(2,1)S(1)}, u32[]{:S(2)}, u32[]{:S(2)}) async-start(bf16[4,512,256]{2,1,0:T(8,128)(2,1)} %get-tuple-element.9), calls=%async_computation.2 | async-start | bytes 2097152 | tf_op jit(solution)/shard_map/all_to_all | solution.py:342
  66.6 16.2 %collective-permute-start = (bf16[512,256]{1,0:T(8,128)(2,1)S(1)}, bf16[512,256]{1,0:T(8,128)(2,1)S(1)}, u32[]{:S(2)}, u32[]{:S(2)}) collective-permute-start(bf16[512,256]{1,0:T(8,128)(2,1)S(1)} %get-tuple-element.15.refs_1_), channel_id=1, source_target_pairs={{0,1},{1,2},{2,3},{3,0},{4,5},{5,6},{6,7},{7,4},{8,9},{9,10},{10,1... | collective-permute-start | bytes 786440 | tf_op jit(solution)/shard_map/ppermute | solution.py:310
  69.9 19.6 %collective-permute-start.1 = (bf16[512,256]{1,0:T(8,128)(2,1)S(1)}, bf16[512,256]{1,0:T(8,128)(2,1)S(1)}, u32[]{:S(2)}, u32[]{:S(2)}) collective-permute-start(bf16[512,256]{1,0:T(8,128)(2,1)S(1)} %get-tuple-element.15.refs_1_), channel_id=1, source_target_pairs={{0,2},{1,3},{2,0},{3,1},{4,6},{5,7},{6,4},{7,5},{8,10},{9,11},{10,... | collective-permute-start | bytes 786440 | tf_op jit(solution)/shard_map/ppermute | solution.py:310
  74.3 16.3 %collective-permute-start.2 = (bf16[512,256]{1,0:T(8,128)(2,1)S(1)}, bf16[512,256]{1,0:T(8,128)(2,1)S(1)}, u32[]{:S(2)}, u32[]{:S(2)}) collective-permute-start(bf16[512,256]{1,0:T(8,128)(2,1)S(1)} %get-tuple-element.15.refs_1_), channel_id=1, source_target_pairs={{0,3},{1,0},{2,1},{3,2},{4,7},{5,4},{6,5},{7,6},{8,11},{9,8},{10,9... | collective-permute-start | bytes 786440 | tf_op jit(solution)/shard_map/ppermute | solution.py:310
  82.8 7.8 %copy-start.3 = (bf16[512,256]{1,0:T(8,128)(2,1)}, bf16[512,256]{1,0:T(8,128)(2,1)S(1)}, u32[]{:S(2)}) copy-start(bf16[512,256]{1,0:T(8,128)(2,1)S(1)} %collective-permute-done.refs_2_) | copy-start | bytes 786436
  89.6 1.0 copy-start.4
  90.6 0.7 copy-start.5
  115.6 11.6 %copy-start = (s32[128,2]{0,1:T(2,128)S(1)}, s32[128,2]{0,1:T(2,128)}, u32[]{:S(2)}) copy-start(s32[128,2]{0,1:T(2,128)} %param.8) | copy-start | bytes 3076
  116.1 33.4 %copy-start.1 = (f32[128,2]{0,1:T(2,128)S(1)}, f32[128,2]{0,1:T(2,128)}, u32[]{:S(2)}) copy-start(f32[128,2]{0,1:T(2,128)} %param.9) | copy-start | bytes 3076
  117.1 32.2 %all-to-all-start.4 = ((bf16[128,4,640]{2,1,0:T(4,128)(2,1)}), bf16[128,4,640]{2,1,0:T(4,128)(2,1)S(1)}, u32[]{:S(2)}, u32[]{:S(2)}) async-start(bf16[128,4,640]{2,1,0:T(4,128)(2,1)} %reshape.25), calls=%async_computation.4 | async-start | bytes 1310720 | tf_op jit(solution)/shard_map/all_to_all | solution.py:368

commit v2 on v1

--- a/solution.py
+++ b/solution.py
@@ -75,31 +75,29 @@
     return copy
 
 
-def forward_kernel(
-    rows_ref,
-    inner_in,
-    outer_in,
-    outs_out,
-    hidden_out,
-    slope_out,
-    inner_ref,
-    outer_ref,
-    outs_ref,
-    hidden_ref,
-    slope_ref,
-    pre_ref,
-    sems,
-):
-    parts, slots, quarter = rows_ref.shape
+def quarter_of(index, size):
+    return pl.ds(pl.multiple_of(index * size, size), size)
+
+
+def forward_kernel(parts, me_ref, *refs):
+    row_refs = refs[:parts]
+    own_in, row_refs = row_refs[0], row_refs[1:]
+    inner_in, outer_in, outs_out, hidden_out, slope_out = refs[parts : parts + 5]
+    (own_ref, inner_ref, outer_ref, outs_ref, hidden_ref, slope_ref, pre_ref, sems) = refs[parts + 5 :]
+    slots, quarter = own_ref.shape
     piece = [slice(q * quarter, (q + 1) * quarter) for q in range(parts)]
+    of = [quarter_of(lax.rem(me_ref[0] + parts - shift, parts), quarter) for shift in range(parts)]
+    own_copy = fetch(own_in, own_ref, sems.at[2 * parts + 3])
     inner_copies = [
-        fetch(inner_in.at[piece[q], :], inner_ref.at[piece[q], :], sems.at[q]) for q in range(parts)
+        fetch(inner_in.at[of[i], :], inner_ref.at[piece[i], :], sems.at[i]) for i in range(parts)
     ]
     outer_copy = fetch(outer_in, outer_ref, sems.at[parts])
+    own_copy.wait()
     acc = None
-    for q in range(parts):
-        inner_copies[q].wait()
-        term = jnp.dot(rows_ref[q], inner_ref[piece[q], :], preferred_element_type=jnp.float32)
+    for i in range(parts):
+        inner_copies[i].wait()
+        rows = own_ref[...] if i == 0 else row_refs[i - 1][...]
+        term = jnp.dot(rows, inner_ref[piece[i], :], preferred_element_type=jnp.float32)
         acc = term if acc is None else acc + term
     pre_ref[...] = acc
     step = 16
@@ -134,30 +132,27 @@
         copy.wait()
 
 
-def backward_kernel(parts, me_ref, *refs):
-    cot_ins = refs[:parts]
-    hidden_in, slope_in, inner_in, outer_in, in_ref = refs[parts : parts + 5]
-    (cot_ref, hidden_ref, slope_ref, inner_ref, outer_ref) = refs[parts + 5 : parts + 10]
-    back_ref, grad_ref, pre_ref, sems = refs[parts + 10 :]
+def backward_kernel(parts, me_ref, cot_ref, hidden_in, slope_in, inner_in, outer_in, *refs):
+    in_refs = refs[:parts]
+    hidden_ref, slope_ref, inner_ref, outer_ref, back_ref, grad_ref, pre_ref, sems = refs[parts:]
     slots, quarter = cot_ref.shape[1:]
     width = back_ref.shape[1]
     across = (((1,), (1,)), ((), ()))
-    outer_copy = fetch(outer_in, outer_ref, sems.at[parts])
-    cot_copies = [fetch(cot_ins[q], cot_ref.at[q], sems.at[q]) for q in range(parts)]
+    outer_copy = fetch(outer_in, outer_ref, sems.at[0])
     later = [
-        fetch(source, target, sems.at[parts + 1 + i])
+        fetch(source, target, sems.at[1 + i])
         for i, (source, target) in enumerate(
             ((slope_in, slope_ref), (hidden_in, hidden_ref), (inner_in, inner_ref))
         )
     ]
     outer_copy.wait()
     acc = None
-    for shift in range(parts):
-        source = lax.rem(me_ref[0] + parts - shift, parts)
-        columns = pl.ds(pl.multiple_of(source * quarter, quarter), quarter)
-        cot_copies[shift].wait()
+    for q in range(parts):
         term = lax.dot_general(
-            cot_ref[shift], outer_ref[:, columns], across, preferred_element_type=jnp.float32
+            cot_ref[q],
+            outer_ref[:, q * quarter : (q + 1) * quarter],
+            across,
+            preferred_element_type=jnp.float32,
         )
         acc = term if acc is None else acc + term
     back_ref[...] = acc
@@ -192,42 +187,46 @@
         piece = slice(j * quarter, (j + 1) * quarter)
         extra = jnp.where(place == 2 * j, high[:, piece], extra)
         extra = jnp.where(place == 2 * j + 1, low[:, piece], extra)
-    for q in range(parts):
-        in_ref[q, :slots, :] = lax.dot_general(
-            pre_ref[...],
-            inner_ref[q * quarter : (q + 1) * quarter, :],
-            across,
-            preferred_element_type=jnp.float32,
+    for shift in range(parts):
+        of = quarter_of(lax.rem(me_ref[0] + shift, parts), quarter)
+        in_refs[shift][:slots, :] = lax.dot_general(
+            pre_ref[...], inner_ref[of, :], across, preferred_element_type=jnp.float32
         ).astype(jnp.bfloat16)
-        in_ref[q, slots:, :] = extra.astype(jnp.bfloat16)
-
-
-def add_kernel(outs_ref, ins_ref, sum_ref):
+        in_refs[shift][slots:, :] = extra.astype(jnp.bfloat16)
+
+
+def in_pairs(terms):
+    wide = [t.astype(jnp.float32) for t in terms]
+    half = len(wide) // 2
+    if half == 0:
+        return wide[0]
+    return in_pairs([wide[i] + wide[i + half] for i in range(half)])
+
+
+def add_kernel(outs_ref, *refs):
+    in_refs, sum_ref = refs[:-1], refs[-1]
     parts, slots, quarter = outs_ref.shape
     step = 16
 
     def add(i, carry):
         at = pl.ds(pl.multiple_of(i * step, step), step)
-        total = outs_ref[0, at, :].astype(jnp.float32)
-        other = ins_ref[0, at, :].astype(jnp.float32)
-        for q in range(1, parts):
-            total = total + outs_ref[q, at, :].astype(jnp.float32)
-            other = other + ins_ref[q, at, :].astype(jnp.float32)
+        total = in_pairs([outs_ref[q, at, :] for q in range(parts)])
+        other = in_pairs([ref[at, :] for ref in in_refs])
         sum_ref[at, :quarter] = total.astype(jnp.bfloat16)
         sum_ref[at, quarter : 2 * quarter] = other.astype(jnp.bfloat16)
         return carry
 
     lax.fori_loop(0, slots // step, add, 0)
-    extra = ins_ref[0, slots:, :].astype(jnp.float32)
-    for q in range(1, parts):
-        extra = extra + ins_ref[q, slots:, :].astype(jnp.float32)
+    chunks = slots // quarter
+    split = [ref[slots:, :].astype(jnp.float32) for ref in in_refs]
+    extra = [
+        in_pairs([part[2 * j : 2 * j + 1, :] + part[2 * j + 1 : 2 * j + 2, :] for part in split])
+        for j in range(chunks)
+    ]
     lane = iota((128, 128), 1)
     for j in range(slots // 128):
         at, lanes = divmod(j * 128, quarter)
-        gate = column_of(
-            extra[2 * at : 2 * at + 1, lanes : lanes + 128]
-            + extra[2 * at + 1 : 2 * at + 2, lanes : lanes + 128]
-        )
+        gate = column_of(extra[at][:, lanes : lanes + 128])
         high = gate.astype(jnp.bfloat16).astype(jnp.float32)
         low = gate - high
         sum_ref[j * 128 : (j + 1) * 128, 2 * quarter :] = jnp.where(
@@ -266,6 +265,15 @@
     return lax.all_to_all(jnp.broadcast_to(x[None], (peers, *x.shape)), axis, 0, 0, tiled=True)
 
 
+def shift_by(x, axis, shift):
+    peers = lax.axis_size(axis)
+    return lax.ppermute(x, axis, [(i, (i + shift) % peers) for i in range(peers)])
+
+
+def shifted(x, axis):
+    return [shift_by(x, axis, shift) for shift in range(1, lax.axis_size(axis))]
+
+
 def shape_of(shape, dtype):
     return jax.ShapeDtypeStruct(shape, dtype)
 
@@ -304,12 +312,9 @@
     arrived = lax.all_to_all(
         packed.reshape(peers, -1, 2 * quarter), "expert", 0, 0, tiled=True
     ).reshape(slots, 2 * quarter)
-    cots = arrived[:, quarter:]
-    all_rows = to_everyone(arrived[:, :quarter], "rep")
-    all_cots = [cots] + [
-        lax.ppermute(cots, "rep", [(i, (i + shift) % parts) for i in range(parts)])
-        for shift in range(1, parts)
-    ]
+    mine = arrived[:, :quarter]
+    near = shifted(mine, "rep")
+    all_cots = to_everyone(arrived[:, quarter:], "rep")
     table = pl.pallas_call(
         lambda *refs: table_kernel(experts, capacity, *refs),
         out_shape=shape_of((TOP * rows, slots), half),
@@ -317,35 +322,36 @@
         name="table",
     )(ids)
     me = lax.axis_index("rep").astype(jnp.int32).reshape(1)
+    smem_spec = pl.BlockSpec(memory_space=pltpu.SMEM)
 
     outs, hidden, slope = pl.pallas_call(
-        forward_kernel,
+        lambda *refs: forward_kernel(parts, *refs),
         out_shape=(
             pltpu.HBM((parts, slots, quarter), half),
             pltpu.HBM((slots, width), half),
             pltpu.HBM((slots, width), full),
         ),
-        in_specs=[vmem_spec, any_spec, any_spec],
+        in_specs=[smem_spec, any_spec] + [vmem_spec] * (parts - 1) + [any_spec] * 2,
         out_specs=(any_spec, any_spec, any_spec),
         scratch_shapes=[
+            pltpu.VMEM((slots, quarter), half),
             pltpu.VMEM((depth, width), half),
             pltpu.VMEM((width, depth), half),
             pltpu.VMEM((parts, slots, quarter), half),
             pltpu.VMEM((slots, width), half),
             pltpu.VMEM((slots, width), full),
             pltpu.VMEM((slots, width), full),
-            pltpu.SemaphoreType.DMA((2 * parts + 3,)),
+            pltpu.SemaphoreType.DMA((2 * parts + 4,)),
         ],
         compiler_params=PARAMS,
         name="forward",
-    )(all_rows, inner, outer)
+    )(me, in_hbm(mine), *near, inner, outer)
     outs = lax.all_to_all(outs, "rep", 0, 0, tiled=True)
-    ins = pl.pallas_call(
+    own, *others = pl.pallas_call(
         lambda *refs: backward_kernel(parts, *refs),
-        out_shape=shape_of((parts, slots + EXTRA, quarter), half),
-        in_specs=[pl.BlockSpec(memory_space=pltpu.SMEM)] + [any_spec] * (parts + 4),
+        out_shape=(shape_of((slots + EXTRA, quarter), half),) * parts,
+        in_specs=[smem_spec, vmem_spec] + [any_spec] * 4,
         scratch_shapes=[
-            pltpu.VMEM((parts, slots, quarter), half),
             pltpu.VMEM((slots, width), half),
             pltpu.VMEM((slots, width), full),
             pltpu.VMEM((depth, width), half),
@@ -353,18 +359,18 @@
             pltpu.VMEM((slots, width), full),
             pltpu.VMEM((slots, 128), full),
             pltpu.VMEM((slots, width), half),
-            pltpu.SemaphoreType.DMA((parts + 4,)),
+            pltpu.SemaphoreType.DMA((4,)),
         ],
         compiler_params=PARAMS,
         name="backward",
-    )(me, *[in_hbm(x) for x in all_cots], in_hbm(hidden), in_hbm(slope), inner, outer)
-    ins = lax.all_to_all(ins, "rep", 0, 0, tiled=True)
+    )(me, all_cots, in_hbm(hidden), in_hbm(slope), inner, outer)
+    arrivals = [own] + [shift_by(x, "rep", 1 + i) for i, x in enumerate(others)]
     summed = pl.pallas_call(
         add_kernel,
         out_shape=shape_of((slots, 2 * quarter + 128), half),
         compiler_params=PARAMS,
         name="add",
-    )(outs, ins)
+    )(outs, *arrivals)
     back = lax.all_to_all(
         summed.reshape(peers, -1, 2 * quarter + 128), "expert", 0, 0, tiled=True
     ).reshape(slots, 2 * quarter + 128)

time: 151 us -> 140 us (0.927)
  the two profiles are of different devices: /device:TPU:1 before, /device:TPU:2 now
where the time goes in v2:
time: 140 us
  waiting for transfers between devices  44.1 us (32%)
  starting transfers between devices  38.3 us (27%)
  blocking collectives  38.2 us (27%)
  Pallas kernels  15.8 us (11%)
  local copies, waits for them, and re-layouts  2.49 us (2%)
    all_to_all x1, blocking collectives, exchange(): lax.all_to_all(packed.reshape(peers, -1, 2 * quarter), 'expert', 0, 0, ti...  38.2 us
    all_to_all x1, waiting for transfers between devices, exchange(): lax.all_to_all(summed.reshape(peers, -1, 2 * quarter + 128), 'expert', 0,...  23 us
    ppermute x6, waiting for transfers between devices, shift_by(): lax.ppermute(x, axis, [(i, (i + shift) % peers) for i in range(peers)])  21.1 us
    ppermute x6, starting transfers between devices, shift_by(): lax.ppermute(x, axis, [(i, (i + shift) % peers) for i in range(peers)])  20.8 us
    all_to_all x1, starting transfers between devices, exchange(): lax.all_to_all(summed.reshape(peers, -1, 2 * quarter + 128), 'expert', 0,...  7.11 us
    pallas_call x1, Pallas kernels, exchange(): pl.pallas_call(lambda *refs: forward_kernel(parts, *refs), out_shape=(plt...  6.39 us
    pallas_call x1, Pallas kernels, exchange(): pl.pallas_call(lambda *refs: backward_kernel(parts, *refs), out_shape=(sh...  5.86 us
    all_to_all x1, starting transfers between devices, exchange(): outs = lax.all_to_all(outs, 'rep', 0, 0, tiled=True)  5.56 us
  transfers between devices with their start and end apart: 9, of which 6 were waited for; matrix products, arithmetic and copies ran while one was open for 0% of the time, Pallas kernels for 9%

profile of v2, /device:TPU:2, one launch (start us, length us, event | category | flops | bytes accessed | tf_op | source)
XLA Modules:
  0.0 139.7 jit_solution(11131305524404353224)
XLA Ops:
  0.6 1.5 %pack.1 = bf16[512,512]{1,0:T(8,128)(2,1)S(1)} custom-call(s32[2,128]{1,0:T(2,128)} %bitcast.6, bf16[128,256]{1,0:T(8,128)(2,1)} %refs_1_.1, bf16[128,256]{1,0:T(8,128)(2,1)} %refs_2_.1), custom_call_target="tpu_custom_call" | custom-call | tf_op jit(solution)/shard_map/pack/pallas_call | solution.py:299
  2.1 0.1 reshape.23
  2.2 38.2 %all_to_all.20 = bf16[128,4,512]{2,1,0:T(4,128)(2,1)S(1)} all-to-all(bf16[128,4,512]{2,1,0:T(4,128)(2,1)S(1)} %reshape.23), channel_id=1, replica_groups=mesh['expert'=128,'rep'=4] {'expert'}, dimensions={0} | all-to-all | bytes 1048576 | tf_op jit(solution)/shard_map/all_to_all | solution.py:312
  40.4 0.1 reshape.24
  40.6 0.0 copy-start.2
  40.6 1.1 broadcast_in_dim.2
  41.7 4.8 %all-to-all-start.2 = ((bf16[4,512,256]{2,1,0:T(8,128)(2,1)}), bf16[4,512,256]{2,1,0:T(8,128)(2,1)S(1)}, u32[]{:S(2)}, u32[]{:S(2)}) async-start(bf16[4,512,256]{2,1,0:T(8,128)(2,1)} %broadcast_in_dim.2), calls=%async_computation.2 | async-start | bytes 2097152 | tf_op jit(solution)/shard_map/all_to_all | solution.py:265
  46.5 3.4 %collective-permute-start = (bf16[512,256]{1,0:T(8,128)(2,1)S(1)}, bf16[512,256]{1,0:T(8,128)(2,1)S(1)}, u32[]{:S(2)}, u32[]{:S(2)}) collective-permute-start(bf16[512,256]{1,0:T(8,128)(2,1)S(1)} %get-tuple-element.24.refs_1_), channel_id=1, source_target_pairs={{0,1},{1,2},{2,3},{3,0},{4,5},{5,6},{6,7},{7,4},{8,9},{9,10},{10,1... | collective-permute-start | bytes 786440 | tf_op jit(solution)/shard_map/ppermute | solution.py:270
  49.9 2.5 %collective-permute-start.1 = (bf16[512,256]{1,0:T(8,128)(2,1)S(1)}, bf16[512,256]{1,0:T(8,128)(2,1)S(1)}, u32[]{:S(2)}, u32[]{:S(2)}) collective-permute-start(bf16[512,256]{1,0:T(8,128)(2,1)S(1)} %get-tuple-element.24.refs_1_), channel_id=1, source_target_pairs={{0,2},{1,3},{2,0},{3,1},{4,6},{5,7},{6,4},{7,5},{8,10},{9,11},{10,... | collective-permute-start | bytes 786440 | tf_op jit(solution)/shard_map/ppermute | solution.py:270
  52.4 4.5 %collective-permute-start.2 = (bf16[512,256]{1,0:T(8,128)(2,1)S(1)}, bf16[512,256]{1,0:T(8,128)(2,1)S(1)}, u32[]{:S(2)}, u32[]{:S(2)}) collective-permute-start(bf16[512,256]{1,0:T(8,128)(2,1)S(1)} %get-tuple-element.24.refs_1_), channel_id=1, source_target_pairs={{0,3},{1,0},{2,1},{3,2},{4,7},{5,4},{6,5},{7,6},{8,11},{9,8},{10,9... | collective-permute-start | bytes 786440 | tf_op jit(solution)/shard_map/ppermute | solution.py:270
  56.9 10.5 %collective-permute-done.refs_2_ = bf16[512,256]{1,0:T(8,128)(2,1)S(1)} collective-permute-done((bf16[512,256]{1,0:T(8,128)(2,1)S(1)}, bf16[512,256]{1,0:T(8,128)(2,1)S(1)}, u32[]{:S(2)}, u32[]{:S(2)}) %collective-permute-start) | collective-permute-done | bytes 262176 | tf_op jit(solution)/shard_map/ppermute | solution.py:270
  67.5 0.0 collective-permute-done.1.refs_3_
  67.5 1.9 %collective-permute-done.2.refs_4_ = bf16[512,256]{1,0:T(8,128)(2,1)S(1)} collective-permute-done((bf16[512,256]{1,0:T(8,128)(2,1)S(1)}, bf16[512,256]{1,0:T(8,128)(2,1)S(1)}, u32[]{:S(2)}, u32[]{:S(2)}) %collective-permute-start.2) | collective-permute-done | bytes 262176 | tf_op jit(solution)/shard_map/ppermute | solution.py:270
  69.4 0.0 copy-done.2
  69.4 6.4 %forward.1 = (bf16[4,512,256]{2,1,0:T(8,128)(2,1)}, bf16[512,1024]{1,0:T(8,128)(2,1)}, f32[512,1024]{1,0:T(8,128)}) custom-call(s32[1]{0:T(128)} %bitcast.2.refs_0_, bf16[512,256]{1,0:T(8,128)(2,1)} %copy-done.2, bf16[512,256]{1,0:T(8,128)(2,1)S(1)} %collective-permute-done.refs_2_, bf16[512,256]{1,0:T(8,128)(2,1)S(1)} %collective-permute-done.1.refs_3_, ...), custom_call_target="tpu_custom_call" | custom-call | tf_op jit(solution)/shard_map/forward/pallas_call | solution.py:327
  75.8 0.0 all-to-all-done.2.refs_1_
  75.8 5.6 %all-to-all-start.1 = ((bf16[4,512,256]{2,1,0:T(8,128)(2,1)}), bf16[4,512,256]{2,1,0:T(8,128)(2,1)S(1)}, u32[]{:S(2)}, u32[]{:S(2)}) async-start(bf16[4,512,256]{2,1,0:T(8,128)(2,1)} %get-tuple-element.13), calls=%async_computation.1 | async-start | bytes 2097152 | tf_op jit(solution)/shard_map/all_to_all | solution.py:349
  81.3 5.9 %backward.1 = (bf16[528,256]{1,0:T(8,128)(2,1)S(1)}, bf16[528,256]{1,0:T(8,128)(2,1)}, bf16[528,256]{1,0:T(8,128)(2,1)S(1)}, bf16[528,256]{1,0:T(8,128)(2,1)S(1)}) custom-call(s32[1]{0:T(128)} %bitcast.2.refs_0_, bf16[4,512,256]{2,1,0:T(8,128)(2,1)S(1)} %all-to-all-done.2.refs_1_, bf16[512,1024]{1,0:T(8,128)(2,1)} %get-tuple-element.14.refs_2_, ...), custom_call_target="tpu_custom_call" | custom-call | tf_op jit(solution)/shard_map/backward/pallas_call | solution.py:350
  87.2 3.4 %collective-permute-start.3 = (bf16[528,256]{1,0:T(8,128)(2,1)}, bf16[528,256]{1,0:T(8,128)(2,1)S(1)}, u32[]{:S(2)}, u32[]{:S(2)}) collective-permute-start(bf16[528,256]{1,0:T(8,128)(2,1)} %get-tuple-element.17), channel_id=1, source_target_pairs={{0,1},{1,2},{2,3},{3,0},{4,5},{5,6},{6,7},{7,4},{8,9},{9,10},{10,1... | collective-permute-start | bytes 811016 | tf_op jit(solution)/shard_map/ppermute | solution.py:270
  90.6 2.6 %collective-permute-start.4 = (bf16[528,256]{1,0:T(8,128)(2,1)S(1)}, bf16[528,256]{1,0:T(8,128)(2,1)S(1)}, u32[]{:S(2)}, u32[]{:S(2)}) collective-permute-start(bf16[528,256]{1,0:T(8,128)(2,1)S(1)} %get-tuple-element.18), channel_id=1, source_target_pairs={{0,2},{1,3},{2,0},{3,1},{4,6},{5,7},{6,4},{7,5},{8,10},{9,11},{10,... | collective-permute-start | bytes 811016 | tf_op jit(solution)/shard_map/ppermute | solution.py:270
  93.2 4.5 %collective-permute-start.5 = (bf16[528,256]{1,0:T(8,128)(2,1)S(1)}, bf16[528,256]{1,0:T(8,128)(2,1)S(1)}, u32[]{:S(2)}, u32[]{:S(2)}) collective-permute-start(bf16[528,256]{1,0:T(8,128)(2,1)S(1)} %get-tuple-element.19), channel_id=1, source_target_pairs={{0,3},{1,0},{2,1},{3,2},{4,7},{5,4},{6,5},{7,6},{8,11},{9,8},{10,9... | collective-permute-start | bytes 811016 | tf_op jit(solution)/shard_map/ppermute | solution.py:270
  97.7 0.0 all-to-all-done.1.outs_ref
  97.7 2.5 %collective-permute-done.3.refs_1_ = bf16[528,256]{1,0:T(8,128)(2,1)S(1)} collective-permute-done((bf16[528,256]{1,0:T(8,128)(2,1)}, bf16[528,256]{1,0:T(8,128)(2,1)S(1)}, u32[]{:S(2)}, u32[]{:S(2)}) %collective-permute-start.3) | collective-permute-done | bytes 270368 | tf_op jit(solution)/shard_map/ppermute | solution.py:270
  100.2 3.2 %collective-permute-done.4.refs_2_ = bf16[528,256]{1,0:T(8,128)(2,1)S(1)} collective-permute-done((bf16[528,256]{1,0:T(8,128)(2,1)S(1)}, bf16[528,256]{1,0:T(8,128)(2,1)S(1)}, u32[]{:S(2)}, u32[]{:S(2)}) %collective-permute-start.4) | collective-permute-done | bytes 270368 | tf_op jit(solution)/shard_map/ppermute | solution.py:270
  103.4 3.0 %collective-permute-done.5.refs_3_ = bf16[528,256]{1,0:T(8,128)(2,1)S(1)} collective-permute-done((bf16[528,256]{1,0:T(8,128)(2,1)S(1)}, bf16[528,256]{1,0:T(8,128)(2,1)S(1)}, u32[]{:S(2)}, u32[]{:S(2)}) %collective-permute-start.5) | collective-permute-done | bytes 270368 | tf_op jit(solution)/shard_map/ppermute | solution.py:270
  106.4 0.0 copy-start
  106.4 0.5 add.1
  106.9 0.0 copy-start.1
  107.0 1.0 reshape.25
  107.9 7.1 %all-to-all-start.3 = ((bf16[128,4,640]{2,1,0:T(4,128)(2,1)}), bf16[128,4,640]{2,1,0:T(4,128)(2,1)S(1)}, u32[]{:S(2)}, u32[]{:S(2)}) async-start(bf16[128,4,640]{2,1,0:T(4,128)(2,1)} %reshape.25), calls=%async_computation.3 | async-start | bytes 1310720 | tf_op jit(solution)/shard_map/all_to_all | solution.py:374
  115.1 0.0 copy-done
  115.1 0.3 table.1.table_ref
  115.4 23.0 %all-to-all-done.3 = bf16[128,4,640]{2,1,0:T(4,128)(2,1)S(1)} async-done(((bf16[128,4,640]{2,1,0:T(4,128)(2,1)}), bf16[128,4,640]{2,1,0:T(4,128)(2,1)S(1)}, u32[]{:S(2)}, u32[]{:S(2)}) %all-to-all-start.3) | async-done | bytes 655392 | tf_op jit(solution)/shard_map/all_to_all | solution.py:374
  138.4 0.1 reshape.26.back_ref
  138.5 0.0 copy-done.1
  138.5 1.2 combine.1
  (1 shorter events, 0.0 us)
Async XLA Ops:
  40.6 28.8 %copy-start.2 = (bf16[512,256]{1,0:T(8,128)(2,1)}, bf16[512,256]{1,0:T(8,128)(2,1)S(1)}, u32[]{:S(2)}) copy-start(bf16[512,256]{1,0:T(8,128)(2,1)S(1)} %get-tuple-element.24.refs_1_) | copy-start | bytes 786436
  41.7 34.1 %all-to-all-start.2 = ((bf16[4,512,256]{2,1,0:T(8,128)(2,1)}), bf16[4,512,256]{2,1,0:T(8,128)(2,1)S(1)}, u32[]{:S(2)}, u32[]{:S(2)}) async-start(bf16[4,512,256]{2,1,0:T(8,128)(2,1)} %broadcast_in_dim.2), calls=%async_computation.2 | async-start | bytes 2097152 | tf_op jit(solution)/shard_map/all_to_all | solution.py:265
  46.5 21.0 %collective-permute-start = (bf16[512,256]{1,0:T(8,128)(2,1)S(1)}, bf16[512,256]{1,0:T(8,128)(2,1)S(1)}, u32[]{:S(2)}, u32[]{:S(2)}) collective-permute-start(bf16[512,256]{1,0:T(8,128)(2,1)S(1)} %get-tuple-element.24.refs_1_), channel_id=1, source_target_pairs={{0,1},{1,2},{2,3},{3,0},{4,5},{5,6},{6,7},{7,4},{8,9},{9,10},{10,1... | collective-permute-start | bytes 786440 | tf_op jit(solution)/shard_map/ppermute | solution.py:270
  49.9 17.6 %collective-permute-start.1 = (bf16[512,256]{1,0:T(8,128)(2,1)S(1)}, bf16[512,256]{1,0:T(8,128)(2,1)S(1)}, u32[]{:S(2)}, u32[]{:S(2)}) collective-permute-start(bf16[512,256]{1,0:T(8,128)(2,1)S(1)} %get-tuple-element.24.refs_1_), channel_id=1, source_target_pairs={{0,2},{1,3},{2,0},{3,1},{4,6},{5,7},{6,4},{7,5},{8,10},{9,11},{10,... | collective-permute-start | bytes 786440 | tf_op jit(solution)/shard_map/ppermute | solution.py:270
  52.4 17.0 %collective-permute-start.2 = (bf16[512,256]{1,0:T(8,128)(2,1)S(1)}, bf16[512,256]{1,0:T(8,128)(2,1)S(1)}, u32[]{:S(2)}, u32[]{:S(2)}) collective-permute-start(bf16[512,256]{1,0:T(8,128)(2,1)S(1)} %get-tuple-element.24.refs_1_), channel_id=1, source_target_pairs={{0,3},{1,0},{2,1},{3,2},{4,7},{5,4},{6,5},{7,6},{8,11},{9,8},{10,9... | collective-permute-start | bytes 786440 | tf_op jit(solution)/shard_map/ppermute | solution.py:270
  75.8 21.9 %all-to-all-start.1 = ((bf16[4,512,256]{2,1,0:T(8,128)(2,1)}), bf16[4,512,256]{2,1,0:T(8,128)(2,1)S(1)}, u32[]{:S(2)}, u32[]{:S(2)}) async-start(bf16[4,512,256]{2,1,0:T(8,128)(2,1)} %get-tuple-element.13), calls=%async_computation.1 | async-start | bytes 2097152 | tf_op jit(solution)/shard_map/all_to_all | solution.py:349
  87.2 13.0 %collective-permute-start.3 = (bf16[528,256]{1,0:T(8,128)(2,1)}, bf16[528,256]{1,0:T(8,128)(2,1)S(1)}, u32[]{:S(2)}, u32[]{:S(2)}) collective-permute-start(bf16[528,256]{1,0:T(8,128)(2,1)} %get-tuple-element.17), channel_id=1, source_target_pairs={{0,1},{1,2},{2,3},{3,0},{4,5},{5,6},{6,7},{7,4},{8,9},{9,10},{10,1... | collective-permute-start | bytes 811016 | tf_op jit(solution)/shard_map/ppermute | solution.py:270
  90.6 12.8 %collective-permute-start.4 = (bf16[528,256]{1,0:T(8,128)(2,1)S(1)}, bf16[528,256]{1,0:T(8,128)(2,1)S(1)}, u32[]{:S(2)}, u32[]{:S(2)}) collective-permute-start(bf16[528,256]{1,0:T(8,128)(2,1)S(1)} %get-tuple-element.18), channel_id=1, source_target_pairs={{0,2},{1,3},{2,0},{3,1},{4,6},{5,7},{6,4},{7,5},{8,10},{9,11},{10,... | collective-permute-start | bytes 811016 | tf_op jit(solution)/shard_map/ppermute | solution.py:270
  93.2 13.2 %collective-permute-start.5 = (bf16[528,256]{1,0:T(8,128)(2,1)S(1)}, bf16[528,256]{1,0:T(8,128)(2,1)S(1)}, u32[]{:S(2)}, u32[]{:S(2)}) collective-permute-start(bf16[528,256]{1,0:T(8,128)(2,1)S(1)} %get-tuple-element.19), channel_id=1, source_target_pairs={{0,3},{1,0},{2,1},{3,2},{4,7},{5,4},{6,5},{7,6},{8,11},{9,8},{10,9... | collective-permute-start | bytes 811016 | tf_op jit(solution)/shard_map/ppermute | solution.py:270
  106.4 8.7 %copy-start = (s32[128,2]{0,1:T(2,128)S(1)}, s32[128,2]{0,1:T(2,128)}, u32[]{:S(2)}) copy-start(s32[128,2]{0,1:T(2,128)} %param.8) | copy-start | bytes 3076
  106.9 31.6 %copy-start.1 = (f32[128,2]{0,1:T(2,128)S(1)}, f32[128,2]{0,1:T(2,128)}, u32[]{:S(2)}) copy-start(f32[128,2]{0,1:T(2,128)} %param.9) | copy-start | bytes 3076
  107.9 30.4 %all-to-all-start.3 = ((bf16[128,4,640]{2,1,0:T(4,128)(2,1)}), bf16[128,4,640]{2,1,0:T(4,128)(2,1)S(1)}, u32[]{:S(2)}, u32[]{:S(2)}) async-start(bf16[128,4,640]{2,1,0:T(4,128)(2,1)} %reshape.25), calls=%async_computation.3 | async-start | bytes 1310720 | tf_op jit(solution)/shard_map/all_to_all | solution.py:374

commit v3 on v1

--- a/solution.py
+++ b/solution.py
@@ -69,10 +69,24 @@
         ).astype(jnp.bfloat16)
 
 
+def spread_kernel(arrived_ref, rows_out, cots_out, sems):
+    parts, _, quarter = rows_out.shape
+    copies = [
+        fetch(arrived_ref.at[:, :quarter], rows_out.at[q], sems.at[q]) for q in range(parts)
+    ]
+    copies.append(fetch(arrived_ref.at[:, quarter:], cots_out, sems.at[parts]))
+    for copy in copies:
+        copy.wait()
+
+
 def fetch(source, target, sem):
     copy = pltpu.make_async_copy(source, target, sem)
     copy.start()
     return copy
+
+
+def quarter_of(index, size):
+    return pl.ds(pl.multiple_of(index * size, size), size)
 
 
 def forward_kernel(
@@ -107,16 +121,17 @@
     def activate(i, carry):
         at = pl.ds(pl.multiple_of(i * step, step), step)
         u = pre_ref[at, :]
-        tangent = jnp.tanh(SQRT_TWO_PI * (u + CUBIC * u * u * u))
-        hidden_ref[at, :] = (0.5 * u * (1.0 + tangent)).astype(jnp.bfloat16)
+        square = u * u
+        tangent = jnp.tanh(u * (SQRT_TWO_PI + (SQRT_TWO_PI * CUBIC) * square))
+        share = 0.5 + 0.5 * tangent
+        result = u * share
+        hidden_ref[at, :] = result.astype(jnp.bfloat16)
         slope_ref[at, :] = (
-            0.5 * (1.0 + tangent)
-            + 0.5
-            * u
-            * (1.0 - tangent * tangent)
-            * SQRT_TWO_PI
-            * (1.0 + 3.0 * CUBIC * u * u)
-        )
+            share
+            + result
+            * (1.0 - share)
+            * (2.0 * SQRT_TWO_PI + (6.0 * SQRT_TWO_PI * CUBIC) * square)
+        ).astype(jnp.bfloat16)
         return carry
 
     lax.fori_loop(0, slots // step, activate, 0)
@@ -135,40 +150,61 @@
 
 
 def backward_kernel(parts, me_ref, *refs):
-    cot_ins = refs[:parts]
-    hidden_in, slope_in, inner_in, outer_in, in_ref = refs[parts : parts + 5]
-    (cot_ref, hidden_ref, slope_ref, inner_ref, outer_ref) = refs[parts + 5 : parts + 10]
-    back_ref, grad_ref, pre_ref, sems = refs[parts + 10 :]
+    cot_ins, (hidden_in, slope_in, inner_in, outer_in) = refs[:parts], refs[parts : parts + 4]
+    in_outs = refs[parts + 4 : 2 * parts + 4]
+    (
+        cot_ref,
+        hidden_ref,
+        slope_ref,
+        inner_ref,
+        outer_ref,
+        in_ref,
+        back_ref,
+        grad_ref,
+        pre_ref,
+        sems,
+    ) = refs[2 * parts + 4 :]
     slots, quarter = cot_ref.shape[1:]
     width = back_ref.shape[1]
     across = (((1,), (1,)), ((), ()))
-    outer_copy = fetch(outer_in, outer_ref, sems.at[parts])
-    cot_copies = [fetch(cot_ins[q], cot_ref.at[q], sems.at[q]) for q in range(parts)]
-    later = [
-        fetch(source, target, sems.at[parts + 1 + i])
+    piece = [slice(q * quarter, (q + 1) * quarter) for q in range(parts)]
+    first = [
+        (
+            fetch(cot_ins[shift], cot_ref.at[shift], sems.at[2 * shift]),
+            fetch(
+                outer_in.at[:, quarter_of(lax.rem(me_ref[0] + parts - shift, parts), quarter)],
+                outer_ref.at[:, piece[shift]],
+                sems.at[2 * shift + 1],
+            ),
+        )
+        for shift in range(parts)
+    ]
+    copies = [
+        fetch(source, target, sems.at[2 * parts + i])
         for i, (source, target) in enumerate(
             ((slope_in, slope_ref), (hidden_in, hidden_ref), (inner_in, inner_ref))
         )
     ]
-    outer_copy.wait()
     acc = None
     for shift in range(parts):
-        source = lax.rem(me_ref[0] + parts - shift, parts)
-        columns = pl.ds(pl.multiple_of(source * quarter, quarter), quarter)
-        cot_copies[shift].wait()
+        for copy in first[shift]:
+            copy.wait()
         term = lax.dot_general(
-            cot_ref[shift], outer_ref[:, columns], across, preferred_element_type=jnp.float32
+            cot_ref[shift],
+            outer_ref[:, piece[shift]],
+            across,
+            preferred_element_type=jnp.float32,
         )
         acc = term if acc is None else acc + term
     back_ref[...] = acc
-    for copy in later:
-        copy.wait()
+    copies[0].wait()
+    copies[1].wait()
     step = 16
 
     def activate(i, carry):
         at = pl.ds(pl.multiple_of(i * step, step), step)
         back = back_ref[at, :]
-        pre_ref[at, :] = (back * slope_ref[at, :]).astype(jnp.bfloat16)
+        pre_ref[at, :] = (back * slope_ref[at, :].astype(jnp.float32)).astype(jnp.bfloat16)
         product = back * hidden_ref[at, :].astype(jnp.float32)
         folded = product[:, :128]
         for j in range(1, width // 128):
@@ -189,45 +225,59 @@
     place = iota((EXTRA, quarter), 0)
     extra = jnp.zeros((EXTRA, quarter), jnp.float32)
     for j in range(slots // quarter):
-        piece = slice(j * quarter, (j + 1) * quarter)
-        extra = jnp.where(place == 2 * j, high[:, piece], extra)
-        extra = jnp.where(place == 2 * j + 1, low[:, piece], extra)
-    for q in range(parts):
-        in_ref[q, :slots, :] = lax.dot_general(
-            pre_ref[...],
-            inner_ref[q * quarter : (q + 1) * quarter, :],
-            across,
-            preferred_element_type=jnp.float32,
+        extra = jnp.where(place == 2 * j, high[:, piece[j]], extra)
+        extra = jnp.where(place == 2 * j + 1, low[:, piece[j]], extra)
+    copies[2].wait()
+    saves = []
+    for shift in range(parts):
+        of = quarter_of(lax.rem(me_ref[0] + shift, parts), quarter)
+        in_ref[shift, :slots, :] = lax.dot_general(
+            pre_ref[...], inner_ref[of, :], across, preferred_element_type=jnp.float32
         ).astype(jnp.bfloat16)
-        in_ref[q, slots:, :] = extra.astype(jnp.bfloat16)
-
-
-def add_kernel(outs_ref, ins_ref, sum_ref):
-    parts, slots, quarter = outs_ref.shape
+        in_ref[shift, slots:, :] = extra.astype(jnp.bfloat16)
+        saves.append(fetch(in_ref.at[shift], in_outs[shift], sems.at[2 * parts + 3 + shift]))
+    for copy in saves:
+        copy.wait()
+
+
+def in_pairs(terms):
+    wide = [t.astype(jnp.float32) for t in terms]
+    half = len(wide) // 2
+    if half == 0:
+        return wide[0]
+    return in_pairs([wide[i] + wide[i + half] for i in range(half)])
+
+
+def add_outs_kernel(outs_ref, own_in, sum_ref, own_ref, sem):
+    copy = fetch(own_in, own_ref, sem)
+    sum_ref[...] = in_pairs([outs_ref[q] for q in range(outs_ref.shape[0])]).astype(jnp.bfloat16)
+    copy.wait()
+
+
+def add_kernel(out_ref, *refs):
+    in_refs, sum_ref = refs[:-1], refs[-1]
+    slots, quarter = out_ref.shape
     step = 16
 
     def add(i, carry):
         at = pl.ds(pl.multiple_of(i * step, step), step)
-        total = outs_ref[0, at, :].astype(jnp.float32)
-        other = ins_ref[0, at, :].astype(jnp.float32)
-        for q in range(1, parts):
-            total = total + outs_ref[q, at, :].astype(jnp.float32)
-            other = other + ins_ref[q, at, :].astype(jnp.float32)
-        sum_ref[at, :quarter] = total.astype(jnp.bfloat16)
-        sum_ref[at, quarter : 2 * quarter] = other.astype(jnp.bfloat16)
+        sum_ref[at, :quarter] = out_ref[at, :]
+        sum_ref[at, quarter : 2 * quarter] = in_pairs([ref[at, :] for ref in in_refs]).astype(
+            jnp.bfloat16
+        )
         return carry
 
     lax.fori_loop(0, slots // step, add, 0)
-    extra = ins_ref[0, slots:, :].astype(jnp.float32)
-    for q in range(1, parts):
-        extra = extra + ins_ref[q, slots:, :].astype(jnp.float32)
+    chunks = slots // quarter
+    split = [ref[slots:, :].astype(jnp.float32) for ref in in_refs]
+    extra = [
+        in_pairs([part[2 * j : 2 * j + 1, :] + part[2 * j + 1 : 2 * j + 2, :] for part in split])
+        for j in range(chunks)
+    ]
     lane = iota((128, 128), 1)
     for j in range(slots // 128):
         at, lanes = divmod(j * 128, quarter)
-        gate = column_of(
-            extra[2 * at : 2 * at + 1, lanes : lanes + 128]
-            + extra[2 * at + 1 : 2 * at + 2, lanes : lanes + 128]
-        )
+        gate = column_of(extra[at][:, lanes : lanes + 128])
         high = gate.astype(jnp.bfloat16).astype(jnp.float32)
         low = gate - high
         sum_ref[j * 128 : (j + 1) * 128, 2 * quarter :] = jnp.where(
@@ -235,24 +285,20 @@
         ).astype(jnp.bfloat16)
 
 
-def table_kernel(experts, capacity, ids_ref, table_ref):
+def table_kernel(experts, capacity, k, ids_ref, table_ref):
     rows = ids_ref.shape[1]
-    positions = slot_positions(ids_ref[...], experts, capacity)
-    slot = iota((rows, experts * capacity), 1)
-    for k in range(TOP):
-        hit = slot == column_of(positions[k])
-        table_ref[k * rows : (k + 1) * rows, :] = jnp.where(hit, 1.0, 0.0).astype(jnp.bfloat16)
-
-
-def combine_kernel(table_ref, gates_ref, back_ref, out_ref, in_ref, gate_ref):
-    rows, quarter = out_ref.shape
+    position = slot_positions(ids_ref[...], experts, capacity)[k]
+    hit = iota((rows, experts * capacity), 1) == column_of(position)
+    table_ref[...] = jnp.where(hit, 1.0, 0.0).astype(jnp.bfloat16)
+
+
+def combine_kernel(*refs):
+    table_refs, gates_ref, back_ref = refs[:TOP], refs[TOP], refs[TOP + 1]
+    out_ref, in_ref, gate_ref = refs[TOP + 2 :]
+    quarter = out_ref.shape[1]
     total = None
     for k in range(TOP):
-        picked = jnp.dot(
-            table_ref[k * rows : (k + 1) * rows, :],
-            back_ref[...],
-            preferred_element_type=jnp.float32,
-        )
+        picked = jnp.dot(table_refs[k][...], back_ref[...], preferred_element_type=jnp.float32)
         term = column_of(gates_ref[k : k + 1, :]) * picked[:, : 2 * quarter]
         total = term if total is None else total + term
         gate = picked[:, 2 * quarter : 2 * quarter + 1] + picked[:, 2 * quarter + 1 : 2 * quarter + 2]
@@ -261,9 +307,15 @@
     in_ref[...] = total[:, quarter:].astype(jnp.bfloat16)
 
 
-def to_everyone(x, axis):
+def shift_by(x, axis, shift):
     peers = lax.axis_size(axis)
-    return lax.all_to_all(jnp.broadcast_to(x[None], (peers, *x.shape)), axis, 0, 0, tiled=True)
+    return lax.ppermute(x, axis, [(i, (i + shift) % peers) for i in range(peers)])
+
+
+def sent_on(pieces, axis):
+    order = sorted(range(1, len(pieces)), key=lambda s: -min(s, len(pieces) - s))
+    moved = {0: pieces[0]} | {s: shift_by(pieces[s], axis, s) for s in order}
+    return [moved[s] for s in range(len(pieces))]
 
 
 def shape_of(shape, dtype):
@@ -281,7 +333,7 @@
     capacity = 2 * rows * TOP // experts
     slots = experts * capacity
     parts = lax.axis_size("rep")
-    inner, outer = in_hbm(inner_weight[0]), in_hbm(outer_weight[0])
+    inner, outer = inner_weight[0], outer_weight[0]
     depth, width = inner.shape
     ids, gates = expert_ids.T, gate_values.T
     any_spec = pl.BlockSpec(memory_space=pltpu.HBM)
@@ -304,67 +356,86 @@
     arrived = lax.all_to_all(
         packed.reshape(peers, -1, 2 * quarter), "expert", 0, 0, tiled=True
     ).reshape(slots, 2 * quarter)
-    cots = arrived[:, quarter:]
-    all_rows = to_everyone(arrived[:, :quarter], "rep")
-    all_cots = [cots] + [
-        lax.ppermute(cots, "rep", [(i, (i + shift) % parts) for i in range(parts)])
-        for shift in range(1, parts)
-    ]
-    table = pl.pallas_call(
-        lambda *refs: table_kernel(experts, capacity, *refs),
-        out_shape=shape_of((TOP * rows, slots), half),
-        compiler_params=PARAMS,
-        name="table",
-    )(ids)
+    copied, cots = pl.pallas_call(
+        spread_kernel,
+        out_shape=(pltpu.HBM((parts, slots, quarter), half), pltpu.HBM((slots, quarter), half)),
+        in_specs=[vmem_spec],
+        out_specs=(any_spec, any_spec),
+        scratch_shapes=[pltpu.SemaphoreType.DMA((parts + 1,))],
+        compiler_params=PARAMS,
+        name="spread",
+    )(arrived)
+    all_rows = lax.all_to_all(copied, "rep", 0, 0, tiled=True)
+    all_cots = sent_on([cots] * parts, "rep")
+    tables = []
+    for k in range(TOP):
+        tables.append(
+            pl.pallas_call(
+                lambda *refs: table_kernel(experts, capacity, k, *refs),
+                out_shape=shape_of((rows, slots), half),
+                compiler_params=PARAMS,
+            )(ids)
+        )
     me = lax.axis_index("rep").astype(jnp.int32).reshape(1)
+    smem_spec = pl.BlockSpec(memory_space=pltpu.SMEM)
 
     outs, hidden, slope = pl.pallas_call(
         forward_kernel,
         out_shape=(
             pltpu.HBM((parts, slots, quarter), half),
             pltpu.HBM((slots, width), half),
-            pltpu.HBM((slots, width), full),
+            pltpu.HBM((slots, width), half),
         ),
         in_specs=[vmem_spec, any_spec, any_spec],
-        out_specs=(any_spec, any_spec, any_spec),
+        out_specs=(any_spec,) * 3,
         scratch_shapes=[
             pltpu.VMEM((depth, width), half),
             pltpu.VMEM((width, depth), half),
             pltpu.VMEM((parts, slots, quarter), half),
             pltpu.VMEM((slots, width), half),
-            pltpu.VMEM((slots, width), full),
+            pltpu.VMEM((slots, width), half),
             pltpu.VMEM((slots, width), full),
             pltpu.SemaphoreType.DMA((2 * parts + 3,)),
         ],
         compiler_params=PARAMS,
         name="forward",
-    )(all_rows, inner, outer)
+    )(all_rows, in_hbm(inner), in_hbm(outer))
     outs = lax.all_to_all(outs, "rep", 0, 0, tiled=True)
     ins = pl.pallas_call(
         lambda *refs: backward_kernel(parts, *refs),
-        out_shape=shape_of((parts, slots + EXTRA, quarter), half),
-        in_specs=[pl.BlockSpec(memory_space=pltpu.SMEM)] + [any_spec] * (parts + 4),
+        out_shape=(pltpu.HBM((slots + EXTRA, quarter), half),) * parts,
+        in_specs=[smem_spec] + [any_spec] * (parts + 4),
+        out_specs=(any_spec,) * parts,
         scratch_shapes=[
             pltpu.VMEM((parts, slots, quarter), half),
             pltpu.VMEM((slots, width), half),
-            pltpu.VMEM((slots, width), full),
+            pltpu.VMEM((slots, width), half),
             pltpu.VMEM((depth, width), half),
             pltpu.VMEM((width, depth), half),
+            pltpu.VMEM((parts, slots + EXTRA, quarter), half),
             pltpu.VMEM((slots, width), full),
             pltpu.VMEM((slots, 128), full),
             pltpu.VMEM((slots, width), half),
-            pltpu.SemaphoreType.DMA((parts + 4,)),
+            pltpu.SemaphoreType.DMA((3 * parts + 3,)),
         ],
         compiler_params=PARAMS,
         name="backward",
-    )(me, *[in_hbm(x) for x in all_cots], in_hbm(hidden), in_hbm(slope), inner, outer)
-    ins = lax.all_to_all(ins, "rep", 0, 0, tiled=True)
+    )(me, *all_cots, *[in_hbm(x) for x in (hidden, slope, inner, outer)])
+    arrivals = sent_on(ins, "rep")
+    out, own = pl.pallas_call(
+        add_outs_kernel,
+        out_shape=(shape_of((slots, quarter), half), shape_of((slots + EXTRA, quarter), half)),
+        in_specs=[vmem_spec, any_spec],
+        scratch_shapes=[pltpu.SemaphoreType.DMA(())],
+        compiler_params=PARAMS,
+        name="add_outs",
+    )(outs, in_hbm(arrivals[0]))
     summed = pl.pallas_call(
         add_kernel,
         out_shape=shape_of((slots, 2 * quarter + 128), half),
         compiler_params=PARAMS,
         name="add",
-    )(outs, ins)
+    )(out, own, *arrivals[1:])
     back = lax.all_to_all(
         summed.reshape(peers, -1, 2 * quarter + 128), "expert", 0, 0, tiled=True
     ).reshape(slots, 2 * quarter + 128)
@@ -377,7 +448,7 @@
         ),
         compiler_params=PARAMS,
         name="combine",
-    )(table, gates, back)
+    )(*tables, gates, back)
     return output, input_grads, gate_grads.T
 
 

time: 151 us -> 153 us (1.013)
  the two profiles are of different devices: /device:TPU:1 before, /device:TPU:2 now
where the time goes in v3:
time: 153 us; the launch traced here: 152 us
  blocking collectives  55.3 us (36%)
  waiting for transfers between devices  42.7 us (28%)
  starting transfers between devices  34.5 us (23%)
  Pallas kernels  17.5 us (11%)
    all_to_all x1, blocking collectives, exchange(): lax.all_to_all(packed.reshape(peers, -1, 2 * quarter), 'expert', 0, 0, ti...  38.2 us
    all_to_all x1, waiting for transfers between devices, exchange(): lax.all_to_all(summed.reshape(peers, -1, 2 * quarter + 128), 'expert', 0,...  22.7 us
    ppermute x6, starting transfers between devices, shift_by(): lax.ppermute(x, axis, [(i, (i + shift) % peers) for i in range(peers)])  20.2 us
    ppermute x6, waiting for transfers between devices, shift_by(): lax.ppermute(x, axis, [(i, (i + shift) % peers) for i in range(peers)])  20 us
    all_to_all x1, blocking collectives, exchange(): all_rows = lax.all_to_all(copied, 'rep', 0, 0, tiled=True)  17.1 us
    all_to_all x1, starting transfers between devices, exchange(): lax.all_to_all(summed.reshape(peers, -1, 2 * quarter + 128), 'expert', 0,...  9.13 us
    pallas_call x1, Pallas kernels, exchange(): pl.pallas_call(forward_kernel, out_shape=(pltpu.HBM((parts, slots, quarte...  5.97 us
    pallas_call x1, Pallas kernels, exchange(): pl.pallas_call(lambda *refs: backward_kernel(parts, *refs), out_shape=(pl...  5.82 us
  transfers between devices with their start and end apart: 8, of which 6 were waited for; matrix products, arithmetic and copies ran while one was open for 0% of the time, Pallas kernels for 5%

profile of v3, /device:TPU:2, one launch (start us, length us, event | category | flops | bytes accessed | tf_op | source)
XLA Modules:
  0.0 152.2 jit_solution(9856918872799348214)
XLA Ops:
  0.6 1.5 pack.1
  2.1 0.1 reshape.21
  2.2 38.2 %all_to_all.20 = bf16[128,4,512]{2,1,0:T(4,128)(2,1)S(1)} all-to-all(bf16[128,4,512]{2,1,0:T(4,128)(2,1)S(1)} %reshape.21), channel_id=1, replica_groups=mesh['expert'=128,'rep'=4] {'expert'}, dimensions={0} | all-to-all | bytes 1048576 | tf_op jit(solution)/shard_map/all_to_all | solution.py:356
  40.4 0.1 reshape.22.arrived_ref
  40.6 1.1 spread.1
  41.7 17.1 %all_to_all.21.rows_ref = bf16[4,512,256]{2,1,0:T(8,128)(2,1)S(1)} all-to-all(bf16[4,512,256]{2,1,0:T(8,128)(2,1)} %get-tuple-element.17), channel_id=1, replica_groups=mesh['expert'=128,'rep'=4] {'rep'}, dimensions={0} | all-to-all | bytes 2097152 | tf_op jit(solution)/shard_map/all_to_all | solution.py:368
  58.8 6.0 %forward.1 = (bf16[4,512,256]{2,1,0:T(8,128)(2,1)}, bf16[512,1024]{1,0:T(8,128)(2,1)}, bf16[512,1024]{1,0:T(8,128)(2,1)}) custom-call(bf16[4,512,256]{2,1,0:T(8,128)(2,1)S(1)} %all_to_all.21.rows_ref, bf16[1024,1024]{1,0:T(8,128)(2,1)} %bitcast.10, bf16[1024,1024]{1,0:T(8,128)(2,1)} %bitcast.12), custom_call_target="tpu_custom_call" | custom-call | tf_op jit(solution)/shard_map/forward/pallas_call | solution.py:382
  64.7 0.0 copy-start
  64.7 5.1 %all-to-all-start.2 = ((bf16[4,512,256]{2,1,0:T(8,128)(2,1)}), bf16[4,512,256]{2,1,0:T(8,128)(2,1)S(1)}, u32[]{:S(2)}, u32[]{:S(2)}) async-start(bf16[4,512,256]{2,1,0:T(8,128)(2,1)} %get-tuple-element.18), calls=%async_computation.2 | async-start | bytes 2097152 | tf_op jit(solution)/shard_map/all_to_all | solution.py:403
  69.8 0.0 copy-done
  69.8 3.4 %collective-permute-start = (bf16[512,256]{1,0:T(8,128)(2,1)S(1)}, bf16[512,256]{1,0:T(8,128)(2,1)S(1)}, u32[]{:S(2)}, u32[]{:S(2)}) collective-permute-start(bf16[512,256]{1,0:T(8,128)(2,1)S(1)} %copy-done), channel_id=1, source_target_pairs={{0,1},{1,2},{2,3},{3,0},{4,5},{5,6},{6,7},{7,4},{8,9},{9,10},{10,1... | collective-permute-start | bytes 786440 | tf_op jit(solution)/shard_map/ppermute | solution.py:312
  73.2 2.6 %collective-permute-start.1 = (bf16[512,256]{1,0:T(8,128)(2,1)S(1)}, bf16[512,256]{1,0:T(8,128)(2,1)S(1)}, u32[]{:S(2)}, u32[]{:S(2)}) collective-permute-start(bf16[512,256]{1,0:T(8,128)(2,1)S(1)} %copy-done), channel_id=1, source_target_pairs={{0,2},{1,3},{2,0},{3,1},{4,6},{5,7},{6,4},{7,5},{8,10},{9,11},{10,... | collective-permute-start | bytes 786440 | tf_op jit(solution)/shard_map/ppermute | solution.py:312
  75.8 4.5 %collective-permute-start.2 = (bf16[512,256]{1,0:T(8,128)(2,1)S(1)}, bf16[512,256]{1,0:T(8,128)(2,1)S(1)}, u32[]{:S(2)}, u32[]{:S(2)}) collective-permute-start(bf16[512,256]{1,0:T(8,128)(2,1)S(1)} %copy-done), channel_id=1, source_target_pairs={{0,3},{1,0},{2,1},{3,2},{4,7},{5,4},{6,5},{7,6},{8,11},{9,8},{10,9... | collective-permute-start | bytes 786440 | tf_op jit(solution)/shard_map/ppermute | solution.py:312
  80.3 7.6 %collective-permute-done.refs_2_ = bf16[512,256]{1,0:T(8,128)(2,1)S(1)} collective-permute-done((bf16[512,256]{1,0:T(8,128)(2,1)S(1)}, bf16[512,256]{1,0:T(8,128)(2,1)S(1)}, u32[]{:S(2)}, u32[]{:S(2)}) %collective-permute-start) | collective-permute-done | bytes 262176 | tf_op jit(solution)/shard_map/ppermute | solution.py:312
  87.9 1.7 %collective-permute-done.1.refs_3_ = bf16[512,256]{1,0:T(8,128)(2,1)S(1)} collective-permute-done((bf16[512,256]{1,0:T(8,128)(2,1)S(1)}, bf16[512,256]{1,0:T(8,128)(2,1)S(1)}, u32[]{:S(2)}, u32[]{:S(2)}) %collective-permute-start.1) | collective-permute-done | bytes 262176 | tf_op jit(solution)/shard_map/ppermute | solution.py:312
  89.6 2.8 %collective-permute-done.2.refs_4_ = bf16[512,256]{1,0:T(8,128)(2,1)S(1)} collective-permute-done((bf16[512,256]{1,0:T(8,128)(2,1)S(1)}, bf16[512,256]{1,0:T(8,128)(2,1)S(1)}, u32[]{:S(2)}, u32[]{:S(2)}) %collective-permute-start.2) | collective-permute-done | bytes 262176 | tf_op jit(solution)/shard_map/ppermute | solution.py:312
  92.4 5.8 %backward.1 = (bf16[528,256]{1,0:T(8,128)(2,1)}, bf16[528,256]{1,0:T(8,128)(2,1)}, bf16[528,256]{1,0:T(8,128)(2,1)}, bf16[528,256]{1,0:T(8,128)(2,1)}) custom-call(s32[1]{0:T(128)} %bitcast.4.refs_0_, bf16[512,256]{1,0:T(8,128)(2,1)S(1)} %copy-done, bf16[512,256]{1,0:T(8,128)(2,1)S(1)} %collective-permute-done.refs_2_, ...), custom_call_target="tpu_custom_call" | custom-call | tf_op jit(solution)/shard_map/backward/pallas_call | solution.py:404
  98.3 2.5 %collective-permute-start.3 = (bf16[528,256]{1,0:T(8,128)(2,1)}, bf16[528,256]{1,0:T(8,128)(2,1)S(1)}, u32[]{:S(2)}, u32[]{:S(2)}) collective-permute-start(bf16[528,256]{1,0:T(8,128)(2,1)} %get-tuple-element.25), channel_id=1, source_target_pairs={{0,1},{1,2},{2,3},{3,0},{4,5},{5,6},{6,7},{7,4},{8,9},{9,10},{10,1... | collective-permute-start | bytes 811016 | tf_op jit(solution)/shard_map/ppermute | solution.py:312
  100.8 4.9 %collective-permute-start.4 = (bf16[528,256]{1,0:T(8,128)(2,1)}, bf16[528,256]{1,0:T(8,128)(2,1)S(1)}, u32[]{:S(2)}, u32[]{:S(2)}) collective-permute-start(bf16[528,256]{1,0:T(8,128)(2,1)} %get-tuple-element.26), channel_id=1, source_target_pairs={{0,2},{1,3},{2,0},{3,1},{4,6},{5,7},{6,4},{7,5},{8,10},{9,11},{10,... | collective-permute-start | bytes 811016 | tf_op jit(solution)/shard_map/ppermute | solution.py:312
  105.7 2.4 %collective-permute-start.5 = (bf16[528,256]{1,0:T(8,128)(2,1)}, bf16[528,256]{1,0:T(8,128)(2,1)S(1)}, u32[]{:S(2)}, u32[]{:S(2)}) collective-permute-start(bf16[528,256]{1,0:T(8,128)(2,1)} %get-tuple-element.27), channel_id=1, source_target_pairs={{0,3},{1,0},{2,1},{3,2},{4,7},{5,4},{6,5},{7,6},{8,11},{9,8},{10,9... | collective-permute-start | bytes 811016 | tf_op jit(solution)/shard_map/ppermute | solution.py:312
  108.1 0.0 all-to-all-done.2.outs_ref
  108.1 1.0 add_outs.1
  109.1 0.0 collective-permute-done.3.refs_1_
  109.1 4.6 %collective-permute-done.4.refs_2_ = bf16[528,256]{1,0:T(8,128)(2,1)S(1)} collective-permute-done((bf16[528,256]{1,0:T(8,128)(2,1)}, bf16[528,256]{1,0:T(8,128)(2,1)S(1)}, u32[]{:S(2)}, u32[]{:S(2)}) %collective-permute-start.4) | collective-permute-done | bytes 270368 | tf_op jit(solution)/shard_map/ppermute | solution.py:312
  113.7 3.3 %collective-permute-done.5.refs_3_ = bf16[528,256]{1,0:T(8,128)(2,1)S(1)} collective-permute-done((bf16[528,256]{1,0:T(8,128)(2,1)}, bf16[528,256]{1,0:T(8,128)(2,1)S(1)}, u32[]{:S(2)}, u32[]{:S(2)}) %collective-permute-start.5) | collective-permute-done | bytes 270368 | tf_op jit(solution)/shard_map/ppermute | solution.py:312
  117.0 0.0 copy-start.1
  117.0 0.4 add.1
  117.4 0.0 copy-start.2
  117.4 1.0 reshape.24
  118.4 9.1 %all-to-all-start.3 = ((bf16[128,4,640]{2,1,0:T(4,128)(2,1)}), bf16[128,4,640]{2,1,0:T(4,128)(2,1)S(1)}, u32[]{:S(2)}, u32[]{:S(2)}) async-start(bf16[128,4,640]{2,1,0:T(4,128)(2,1)} %reshape.24), calls=%async_computation.3 | async-start | bytes 1310720 | tf_op jit(solution)/shard_map/all_to_all | solution.py:439
  127.5 0.0 copy-done.1
  127.6 0.3 shard_map.85.refs_0_
  127.8 0.3 shard_map.86.refs_1_
  128.1 22.7 %all-to-all-done.3 = bf16[128,4,640]{2,1,0:T(4,128)(2,1)S(1)} async-done(((bf16[128,4,640]{2,1,0:T(4,128)(2,1)}), bf16[128,4,640]{2,1,0:T(4,128)(2,1)S(1)}, u32[]{:S(2)}, u32[]{:S(2)}) %all-to-all-start.3) | async-done | bytes 655392 | tf_op jit(solution)/shard_map/all_to_all | solution.py:439
  150.8 0.1 reshape.25.refs_3_
  151.0 0.0 copy-done.2
  151.0 1.2 combine.1
Async XLA Ops:
  64.7 5.1 %copy-start = (bf16[512,256]{1,0:T(8,128)(2,1)S(1)}, bf16[512,256]{1,0:T(8,128)(2,1)}, u32[]{:S(2)}) copy-start(bf16[512,256]{1,0:T(8,128)(2,1)} %get-tuple-element.19.refs_1_) | copy-start | bytes 786436
  64.7 43.4 %all-to-all-start.2 = ((bf16[4,512,256]{2,1,0:T(8,128)(2,1)}), bf16[4,512,256]{2,1,0:T(8,128)(2,1)S(1)}, u32[]{:S(2)}, u32[]{:S(2)}) async-start(bf16[4,512,256]{2,1,0:T(8,128)(2,1)} %get-tuple-element.18), calls=%async_computation.2 | async-start | bytes 2097152 | tf_op jit(solution)/shard_map/all_to_all | solution.py:403
  69.8 18.1 %collective-permute-start = (bf16[512,256]{1,0:T(8,128)(2,1)S(1)}, bf16[512,256]{1,0:T(8,128)(2,1)S(1)}, u32[]{:S(2)}, u32[]{:S(2)}) collective-permute-start(bf16[512,256]{1,0:T(8,128)(2,1)S(1)} %copy-done), channel_id=1, source_target_pairs={{0,1},{1,2},{2,3},{3,0},{4,5},{5,6},{6,7},{7,4},{8,9},{9,10},{10,1... | collective-permute-start | bytes 786440 | tf_op jit(solution)/shard_map/ppermute | solution.py:312
  73.2 16.4 %collective-permute-start.1 = (bf16[512,256]{1,0:T(8,128)(2,1)S(1)}, bf16[512,256]{1,0:T(8,128)(2,1)S(1)}, u32[]{:S(2)}, u32[]{:S(2)}) collective-permute-start(bf16[512,256]{1,0:T(8,128)(2,1)S(1)} %copy-done), channel_id=1, source_target_pairs={{0,2},{1,3},{2,0},{3,1},{4,6},{5,7},{6,4},{7,5},{8,10},{9,11},{10,... | collective-permute-start | bytes 786440 | tf_op jit(solution)/shard_map/ppermute | solution.py:312
  75.8 16.7 %collective-permute-start.2 = (bf16[512,256]{1,0:T(8,128)(2,1)S(1)}, bf16[512,256]{1,0:T(8,128)(2,1)S(1)}, u32[]{:S(2)}, u32[]{:S(2)}) collective-permute-start(bf16[512,256]{1,0:T(8,128)(2,1)S(1)} %copy-done), channel_id=1, source_target_pairs={{0,3},{1,0},{2,1},{3,2},{4,7},{5,4},{6,5},{7,6},{8,11},{9,8},{10,9... | collective-permute-start | bytes 786440 | tf_op jit(solution)/shard_map/ppermute | solution.py:312
  98.3 10.8 %collective-permute-start.3 = (bf16[528,256]{1,0:T(8,128)(2,1)}, bf16[528,256]{1,0:T(8,128)(2,1)S(1)}, u32[]{:S(2)}, u32[]{:S(2)}) collective-permute-start(bf16[528,256]{1,0:T(8,128)(2,1)} %get-tuple-element.25), channel_id=1, source_target_pairs={{0,1},{1,2},{2,3},{3,0},{4,5},{5,6},{6,7},{7,4},{8,9},{9,10},{10,1... | collective-permute-start | bytes 811016 | tf_op jit(solution)/shard_map/ppermute | solution.py:312
  100.8 13.0 %collective-permute-start.4 = (bf16[528,256]{1,0:T(8,128)(2,1)}, bf16[528,256]{1,0:T(8,128)(2,1)S(1)}, u32[]{:S(2)}, u32[]{:S(2)}) collective-permute-start(bf16[528,256]{1,0:T(8,128)(2,1)} %get-tuple-element.26), channel_id=1, source_target_pairs={{0,2},{1,3},{2,0},{3,1},{4,6},{5,7},{6,4},{7,5},{8,10},{9,11},{10,... | collective-permute-start | bytes 811016 | tf_op jit(solution)/shard_map/ppermute | solution.py:312
  105.7 11.3 %collective-permute-start.5 = (bf16[528,256]{1,0:T(8,128)(2,1)}, bf16[528,256]{1,0:T(8,128)(2,1)S(1)}, u32[]{:S(2)}, u32[]{:S(2)}) collective-permute-start(bf16[528,256]{1,0:T(8,128)(2,1)} %get-tuple-element.27), channel_id=1, source_target_pairs={{0,3},{1,0},{2,1},{3,2},{4,7},{5,4},{6,5},{7,6},{8,11},{9,8},{10,9... | collective-permute-start | bytes 811016 | tf_op jit(solution)/shard_map/ppermute | solution.py:312
  117.0 10.6 %copy-start.1 = (s32[128,2]{0,1:T(2,128)S(1)}, s32[128,2]{0,1:T(2,128)}, u32[]{:S(2)}) copy-start(s32[128,2]{0,1:T(2,128)} %param.8) | copy-start | bytes 3076
  117.4 33.6 %copy-start.2 = (f32[128,2]{0,1:T(2,128)S(1)}, f32[128,2]{0,1:T(2,128)}, u32[]{:S(2)}) copy-start(f32[128,2]{0,1:T(2,128)} %param.9) | copy-start | bytes 3076
  118.4 32.4 %all-to-all-start.3 = ((bf16[128,4,640]{2,1,0:T(4,128)(2,1)}), bf16[128,4,640]{2,1,0:T(4,128)(2,1)S(1)}, u32[]{:S(2)}, u32[]{:S(2)}) async-start(bf16[128,4,640]{2,1,0:T(4,128)(2,1)} %reshape.24), calls=%async_computation.3 | async-start | bytes 1310720 | tf_op jit(solution)/shard_map/all_to_all | solution.py:439

commit v4 on v3

--- a/solution.py
+++ b/solution.py
@@ -91,12 +91,11 @@
 
 def forward_kernel(
     rows_ref,
-    inner_in,
+    inner_ref,
     outer_in,
     outs_out,
     hidden_out,
     slope_out,
-    inner_ref,
     outer_ref,
     outs_ref,
     hidden_ref,
@@ -106,17 +105,13 @@
 ):
     parts, slots, quarter = rows_ref.shape
     piece = [slice(q * quarter, (q + 1) * quarter) for q in range(parts)]
-    inner_copies = [
-        fetch(inner_in.at[piece[q], :], inner_ref.at[piece[q], :], sems.at[q]) for q in range(parts)
-    ]
     outer_copy = fetch(outer_in, outer_ref, sems.at[parts])
     acc = None
     for q in range(parts):
-        inner_copies[q].wait()
         term = jnp.dot(rows_ref[q], inner_ref[piece[q], :], preferred_element_type=jnp.float32)
         acc = term if acc is None else acc + term
     pre_ref[...] = acc
-    step = 16
+    step = 32
 
     def activate(i, carry):
         at = pl.ds(pl.multiple_of(i * step, step), step)
@@ -150,14 +145,13 @@
 
 
 def backward_kernel(parts, me_ref, *refs):
-    cot_ins, (hidden_in, slope_in, inner_in, outer_in) = refs[:parts], refs[parts : parts + 4]
+    cot_ins, (hidden_in, slope_in, inner_in, outer_ref) = refs[:parts], refs[parts : parts + 4]
     in_outs = refs[parts + 4 : 2 * parts + 4]
     (
         cot_ref,
         hidden_ref,
         slope_ref,
         inner_ref,
-        outer_ref,
         in_ref,
         back_ref,
         grad_ref,
@@ -168,17 +162,7 @@
     width = back_ref.shape[1]
     across = (((1,), (1,)), ((), ()))
     piece = [slice(q * quarter, (q + 1) * quarter) for q in range(parts)]
-    first = [
-        (
-            fetch(cot_ins[shift], cot_ref.at[shift], sems.at[2 * shift]),
-            fetch(
-                outer_in.at[:, quarter_of(lax.rem(me_ref[0] + parts - shift, parts), quarter)],
-                outer_ref.at[:, piece[shift]],
-                sems.at[2 * shift + 1],
-            ),
-        )
-        for shift in range(parts)
-    ]
+    first = [fetch(cot_ins[i], cot_ref.at[i], sems.at[i]) for i in range(parts)]
     copies = [
         fetch(source, target, sems.at[2 * parts + i])
         for i, (source, target) in enumerate(
@@ -187,11 +171,11 @@
     ]
     acc = None
     for shift in range(parts):
-        for copy in first[shift]:
-            copy.wait()
+        first[shift].wait()
+        of = quarter_of(lax.rem(me_ref[0] + parts - shift, parts), quarter)
         term = lax.dot_general(
             cot_ref[shift],
-            outer_ref[:, piece[shift]],
+            outer_ref[:, of],
             across,
             preferred_element_type=jnp.float32,
         )
@@ -313,9 +297,10 @@
 
 
 def sent_on(pieces, axis):
-    order = sorted(range(1, len(pieces)), key=lambda s: -min(s, len(pieces) - s))
-    moved = {0: pieces[0]} | {s: shift_by(pieces[s], axis, s) for s in order}
-    return [moved[s] for s in range(len(pieces))]
+    moved = [pieces[0]]
+    for shift in range(1, len(pieces)):
+        moved.append(shift_by(pieces[shift], axis, shift))
+    return moved
 
 
 def shape_of(shape, dtype):
@@ -386,10 +371,9 @@
             pltpu.HBM((slots, width), half),
             pltpu.HBM((slots, width), half),
         ),
-        in_specs=[vmem_spec, any_spec, any_spec],
+        in_specs=[vmem_spec, vmem_spec, any_spec],
         out_specs=(any_spec,) * 3,
         scratch_shapes=[
-            pltpu.VMEM((depth, width), half),
             pltpu.VMEM((width, depth), half),
             pltpu.VMEM((parts, slots, quarter), half),
             pltpu.VMEM((slots, width), half),
@@ -399,19 +383,18 @@
         ],
         compiler_params=PARAMS,
         name="forward",
-    )(all_rows, in_hbm(inner), in_hbm(outer))
+    )(all_rows, inner, in_hbm(outer))
     outs = lax.all_to_all(outs, "rep", 0, 0, tiled=True)
     ins = pl.pallas_call(
         lambda *refs: backward_kernel(parts, *refs),
         out_shape=(pltpu.HBM((slots + EXTRA, quarter), half),) * parts,
-        in_specs=[smem_spec] + [any_spec] * (parts + 4),
+        in_specs=[smem_spec] + [any_spec] * (parts + 3) + [vmem_spec],
         out_specs=(any_spec,) * parts,
         scratch_shapes=[
             pltpu.VMEM((parts, slots, quarter), half),
             pltpu.VMEM((slots, width), half),
             pltpu.VMEM((slots, width), half),
             pltpu.VMEM((depth, width), half),
-            pltpu.VMEM((width, depth), half),
             pltpu.VMEM((parts, slots + EXTRA, quarter), half),
             pltpu.VMEM((slots, width), full),
             pltpu.VMEM((slots, 128), full),
@@ -420,7 +403,7 @@
         ],
         compiler_params=PARAMS,
         name="backward",
-    )(me, *all_cots, *[in_hbm(x) for x in (hidden, slope, inner, outer)])
+    )(me, *all_cots, *[in_hbm(x) for x in (hidden, slope, inner)], outer)
     arrivals = sent_on(ins, "rep")
     out, own = pl.pallas_call(
         add_outs_kernel,

time: 153 us -> 152 us (level)
  no operation moved by 1% of the time
where the time goes in v4:
time: 152 us; the launch traced here: 151 us
  blocking collectives  55.3 us (36%)
  waiting for transfers between devices  42.8 us (28%)
  starting transfers between devices  34.5 us (23%)
  Pallas kernels  16.1 us (11%)
    all_to_all x1, blocking collectives, exchange(): lax.all_to_all(packed.reshape(peers, -1, 2 * quarter), 'expert', 0, 0, ti...  38.2 us
    all_to_all x1, waiting for transfers between devices, exchange(): lax.all_to_all(summed.reshape(peers, -1, 2 * quarter + 128), 'expert', 0,...  22.7 us
    ppermute x6, starting transfers between devices, shift_by(): lax.ppermute(x, axis, [(i, (i + shift) % peers) for i in range(peers)])  20.2 us
    ppermute x6, waiting for transfers between devices, shift_by(): lax.ppermute(x, axis, [(i, (i + shift) % peers) for i in range(peers)])  20.1 us
    all_to_all x1, blocking collectives, exchange(): all_rows = lax.all_to_all(copied, 'rep', 0, 0, tiled=True)  17.1 us
    all_to_all x1, starting transfers between devices, exchange(): lax.all_to_all(summed.reshape(peers, -1, 2 * quarter + 128), 'expert', 0,...  9.14 us
    pallas_call x1, Pallas kernels, exchange(): pl.pallas_call(lambda *refs: backward_kernel(parts, *refs), out_shape=(pl...  5.58 us
    all_to_all x1, starting transfers between devices, exchange(): outs = lax.all_to_all(outs, 'rep', 0, 0, tiled=True)  5.09 us
  transfers between devices with their start and end apart: 8, of which 6 were waited for; matrix products, arithmetic and copies ran while one was open for 0% of the time, Pallas kernels for 5%

profile of v4, /device:TPU:2, one launch (start us, length us, event | category | flops | bytes accessed | tf_op | source)
XLA Modules:
  0.0 151.0 jit_solution(1770623242774054851)
XLA Ops:
  0.6 1.5 pack.1
  2.1 0.1 reshape.21
  2.2 38.2 %all_to_all.20 = bf16[128,4,512]{2,1,0:T(4,128)(2,1)S(1)} all-to-all(bf16[128,4,512]{2,1,0:T(4,128)(2,1)S(1)} %reshape.21), channel_id=1, replica_groups=mesh['expert'=128,'rep'=4] {'expert'}, dimensions={0} | all-to-all | bytes 1048576 | tf_op jit(solution)/shard_map/all_to_all | solution.py:341
  40.4 0.0 copy-start
  40.4 0.1 reshape.22.arrived_ref
  40.6 1.1 spread.1
  41.7 17.1 %all_to_all.21.rows_ref = bf16[4,512,256]{2,1,0:T(8,128)(2,1)S(1)} all-to-all(bf16[4,512,256]{2,1,0:T(8,128)(2,1)} %get-tuple-element.17), channel_id=1, replica_groups=mesh['expert'=128,'rep'=4] {'rep'}, dimensions={0} | all-to-all | bytes 2097152 | tf_op jit(solution)/shard_map/all_to_all | solution.py:353
  58.8 0.0 copy-done
  58.8 0.0 copy-start.2
  58.8 4.9 %forward.1 = (bf16[4,512,256]{2,1,0:T(8,128)(2,1)}, bf16[512,1024]{1,0:T(8,128)(2,1)}, bf16[512,1024]{1,0:T(8,128)(2,1)}) custom-call(bf16[4,512,256]{2,1,0:T(8,128)(2,1)S(1)} %all_to_all.21.rows_ref, bf16[1024,1024]{1,0:T(8,128)(2,1)S(1)} %bitcast.7, bf16[1024,1024]{1,0:T(8,128)(2,1)} %bitcast.8), custom_call_target="tpu_custom_call" | custom-call | tf_op jit(solution)/shard_map/forward/pallas_call | solution.py:367
  63.6 0.0 copy-start.1
  63.6 5.1 %all-to-all-start.2 = ((bf16[4,512,256]{2,1,0:T(8,128)(2,1)}), bf16[4,512,256]{2,1,0:T(8,128)(2,1)S(1)}, u32[]{:S(2)}, u32[]{:S(2)}) async-start(bf16[4,512,256]{2,1,0:T(8,128)(2,1)} %get-tuple-element.18), calls=%async_computation.2 | async-start | bytes 2097152 | tf_op jit(solution)/shard_map/all_to_all | solution.py:387
  68.7 0.0 copy-done.2
  68.7 3.4 %collective-permute-start = (bf16[512,256]{1,0:T(8,128)(2,1)S(1)}, bf16[512,256]{1,0:T(8,128)(2,1)}, u32[]{:S(2)}, u32[]{:S(2)}) collective-permute-start(bf16[512,256]{1,0:T(8,128)(2,1)S(1)} %copy-done.2), channel_id=1, source_target_pairs={{0,1},{1,2},{2,3},{3,0},{4,5},{5,6},{6,7},{7,4},{8,9},{9,10},{10,1... | collective-permute-start | bytes 786440 | tf_op jit(solution)/shard_map/ppermute | solution.py:296
  72.1 2.6 %collective-permute-start.1 = (bf16[512,256]{1,0:T(8,128)(2,1)S(1)}, bf16[512,256]{1,0:T(8,128)(2,1)}, u32[]{:S(2)}, u32[]{:S(2)}) collective-permute-start(bf16[512,256]{1,0:T(8,128)(2,1)S(1)} %copy-done.2), channel_id=1, source_target_pairs={{0,2},{1,3},{2,0},{3,1},{4,6},{5,7},{6,4},{7,5},{8,10},{9,11},{10,... | collective-permute-start | bytes 786440 | tf_op jit(solution)/shard_map/ppermute | solution.py:296
  74.7 4.5 %collective-permute-start.2 = (bf16[512,256]{1,0:T(8,128)(2,1)S(1)}, bf16[512,256]{1,0:T(8,128)(2,1)}, u32[]{:S(2)}, u32[]{:S(2)}) collective-permute-start(bf16[512,256]{1,0:T(8,128)(2,1)S(1)} %copy-done.2), channel_id=1, source_target_pairs={{0,3},{1,0},{2,1},{3,2},{4,7},{5,4},{6,5},{7,6},{8,11},{9,8},{10,9... | collective-permute-start | bytes 786440 | tf_op jit(solution)/shard_map/ppermute | solution.py:296
  79.2 7.7 %collective-permute-done.refs_2_ = bf16[512,256]{1,0:T(8,128)(2,1)} collective-permute-done((bf16[512,256]{1,0:T(8,128)(2,1)S(1)}, bf16[512,256]{1,0:T(8,128)(2,1)}, u32[]{:S(2)}, u32[]{:S(2)}) %collective-permute-start) | collective-permute-done | bytes 262176 | tf_op jit(solution)/shard_map/ppermute | solution.py:296
  86.9 1.7 %collective-permute-done.1.refs_3_ = bf16[512,256]{1,0:T(8,128)(2,1)} collective-permute-done((bf16[512,256]{1,0:T(8,128)(2,1)S(1)}, bf16[512,256]{1,0:T(8,128)(2,1)}, u32[]{:S(2)}, u32[]{:S(2)}) %collective-permute-start.1) | collective-permute-done | bytes 262176 | tf_op jit(solution)/shard_map/ppermute | solution.py:296
  88.6 2.8 %collective-permute-done.2.refs_4_ = bf16[512,256]{1,0:T(8,128)(2,1)} collective-permute-done((bf16[512,256]{1,0:T(8,128)(2,1)S(1)}, bf16[512,256]{1,0:T(8,128)(2,1)}, u32[]{:S(2)}, u32[]{:S(2)}) %collective-permute-start.2) | collective-permute-done | bytes 262176 | tf_op jit(solution)/shard_map/ppermute | solution.py:296
  91.5 0.0 copy-done.1
  91.5 5.6 %backward.1 = (bf16[528,256]{1,0:T(8,128)(2,1)}, bf16[528,256]{1,0:T(8,128)(2,1)}, bf16[528,256]{1,0:T(8,128)(2,1)}, bf16[528,256]{1,0:T(8,128)(2,1)}) custom-call(s32[1]{0:T(128)} %bitcast.4.refs_0_, bf16[512,256]{1,0:T(8,128)(2,1)S(1)} %copy-done.2, bf16[512,256]{1,0:T(8,128)(2,1)} %collective-permute-done.refs_2_, ...), custom_call_target="tpu_custom_call" | custom-call | tf_op jit(solution)/shard_map/backward/pallas_call | solution.py:388
  97.0 2.5 %collective-permute-start.3 = (bf16[528,256]{1,0:T(8,128)(2,1)}, bf16[528,256]{1,0:T(8,128)(2,1)S(1)}, u32[]{:S(2)}, u32[]{:S(2)}) collective-permute-start(bf16[528,256]{1,0:T(8,128)(2,1)} %get-tuple-element.25), channel_id=1, source_target_pairs={{0,1},{1,2},{2,3},{3,0},{4,5},{5,6},{6,7},{7,4},{8,9},{9,10},{10,1... | collective-permute-start | bytes 811016 | tf_op jit(solution)/shard_map/ppermute | solution.py:296
  99.5 4.9 %collective-permute-start.4 = (bf16[528,256]{1,0:T(8,128)(2,1)}, bf16[528,256]{1,0:T(8,128)(2,1)S(1)}, u32[]{:S(2)}, u32[]{:S(2)}) collective-permute-start(bf16[528,256]{1,0:T(8,128)(2,1)} %get-tuple-element.26), channel_id=1, source_target_pairs={{0,2},{1,3},{2,0},{3,1},{4,6},{5,7},{6,4},{7,5},{8,10},{9,11},{10,... | collective-permute-start | bytes 811016 | tf_op jit(solution)/shard_map/ppermute | solution.py:296
  104.5 2.4 %collective-permute-start.5 = (bf16[528,256]{1,0:T(8,128)(2,1)}, bf16[528,256]{1,0:T(8,128)(2,1)S(1)}, u32[]{:S(2)}, u32[]{:S(2)}) collective-permute-start(bf16[528,256]{1,0:T(8,128)(2,1)} %get-tuple-element.27), channel_id=1, source_target_pairs={{0,3},{1,0},{2,1},{3,2},{4,7},{5,4},{6,5},{7,6},{8,11},{9,8},{10,9... | collective-permute-start | bytes 811016 | tf_op jit(solution)/shard_map/ppermute | solution.py:296
  106.9 0.0 all-to-all-done.2.outs_ref
  106.9 1.0 add_outs.1
  107.9 0.0 collective-permute-done.3.refs_1_
  107.9 4.6 %collective-permute-done.4.refs_2_ = bf16[528,256]{1,0:T(8,128)(2,1)S(1)} collective-permute-done((bf16[528,256]{1,0:T(8,128)(2,1)}, bf16[528,256]{1,0:T(8,128)(2,1)S(1)}, u32[]{:S(2)}, u32[]{:S(2)}) %collective-permute-start.4) | collective-permute-done | bytes 270368 | tf_op jit(solution)/shard_map/ppermute | solution.py:296
  112.5 3.3 %collective-permute-done.5.refs_3_ = bf16[528,256]{1,0:T(8,128)(2,1)S(1)} collective-permute-done((bf16[528,256]{1,0:T(8,128)(2,1)}, bf16[528,256]{1,0:T(8,128)(2,1)S(1)}, u32[]{:S(2)}, u32[]{:S(2)}) %collective-permute-start.5) | collective-permute-done | bytes 270368 | tf_op jit(solution)/shard_map/ppermute | solution.py:296
  115.7 0.0 copy-start.3
  115.7 0.4 add.1
  116.2 0.0 copy-start.4
  116.2 1.0 reshape.24
  117.2 9.1 %all-to-all-start.3 = ((bf16[128,4,640]{2,1,0:T(4,128)(2,1)}), bf16[128,4,640]{2,1,0:T(4,128)(2,1)S(1)}, u32[]{:S(2)}, u32[]{:S(2)}) async-start(bf16[128,4,640]{2,1,0:T(4,128)(2,1)} %reshape.24), calls=%async_computation.3 | async-start | bytes 1310720 | tf_op jit(solution)/shard_map/all_to_all | solution.py:422
  126.3 0.0 copy-done.3
  126.3 0.3 shard_map.85.refs_0_
  126.6 0.3 shard_map.86.refs_1_
  126.9 22.7 %all-to-all-done.3 = bf16[128,4,640]{2,1,0:T(4,128)(2,1)S(1)} async-done(((bf16[128,4,640]{2,1,0:T(4,128)(2,1)}), bf16[128,4,640]{2,1,0:T(4,128)(2,1)S(1)}, u32[]{:S(2)}, u32[]{:S(2)}) %all-to-all-start.3) | async-done | bytes 655392 | tf_op jit(solution)/shard_map/all_to_all | solution.py:422
  149.6 0.1 reshape.25.refs_3_
  149.8 0.0 copy-done.4
  149.8 1.2 combine.1
Async XLA Ops:
  40.4 18.3 %copy-start = (bf16[1,1024,1024]{2,1,0:T(8,128)(2,1)S(1)}, bf16[1,1024,1024]{2,1,0:T(8,128)(2,1)}, u32[]{:S(2)}) copy-start(bf16[1,1024,1024]{2,1,0:T(8,128)(2,1)} %param.10) | copy-start | bytes 6291460
  58.8 10.0 %copy-start.2 = (bf16[512,256]{1,0:T(8,128)(2,1)S(1)}, bf16[512,256]{1,0:T(8,128)(2,1)}, u32[]{:S(2)}) copy-start(bf16[512,256]{1,0:T(8,128)(2,1)} %get-tuple-element.19.refs_1_) | copy-start | bytes 786436
  63.6 27.8 %copy-start.1 = (bf16[1,1024,1024]{2,1,0:T(8,128)(2,1)S(1)}, bf16[1,1024,1024]{2,1,0:T(8,128)(2,1)}, u32[]{:S(2)}) copy-start(bf16[1,1024,1024]{2,1,0:T(8,128)(2,1)} %param.11) | copy-start | bytes 6291460
  63.6 43.2 %all-to-all-start.2 = ((bf16[4,512,256]{2,1,0:T(8,128)(2,1)}), bf16[4,512,256]{2,1,0:T(8,128)(2,1)S(1)}, u32[]{:S(2)}, u32[]{:S(2)}) async-start(bf16[4,512,256]{2,1,0:T(8,128)(2,1)} %get-tuple-element.18), calls=%async_computation.2 | async-start | bytes 2097152 | tf_op jit(solution)/shard_map/all_to_all | solution.py:387
  68.7 18.2 %collective-permute-start = (bf16[512,256]{1,0:T(8,128)(2,1)S(1)}, bf16[512,256]{1,0:T(8,128)(2,1)}, u32[]{:S(2)}, u32[]{:S(2)}) collective-permute-start(bf16[512,256]{1,0:T(8,128)(2,1)S(1)} %copy-done.2), channel_id=1, source_target_pairs={{0,1},{1,2},{2,3},{3,0},{4,5},{5,6},{6,7},{7,4},{8,9},{9,10},{10,1... | collective-permute-start | bytes 786440 | tf_op jit(solution)/shard_map/ppermute | solution.py:296
  72.1 16.5 %collective-permute-start.1 = (bf16[512,256]{1,0:T(8,128)(2,1)S(1)}, bf16[512,256]{1,0:T(8,128)(2,1)}, u32[]{:S(2)}, u32[]{:S(2)}) collective-permute-start(bf16[512,256]{1,0:T(8,128)(2,1)S(1)} %copy-done.2), channel_id=1, source_target_pairs={{0,2},{1,3},{2,0},{3,1},{4,6},{5,7},{6,4},{7,5},{8,10},{9,11},{10,... | collective-permute-start | bytes 786440 | tf_op jit(solution)/shard_map/ppermute | solution.py:296
  74.7 16.8 %collective-permute-start.2 = (bf16[512,256]{1,0:T(8,128)(2,1)S(1)}, bf16[512,256]{1,0:T(8,128)(2,1)}, u32[]{:S(2)}, u32[]{:S(2)}) collective-permute-start(bf16[512,256]{1,0:T(8,128)(2,1)S(1)} %copy-done.2), channel_id=1, source_target_pairs={{0,3},{1,0},{2,1},{3,2},{4,7},{5,4},{6,5},{7,6},{8,11},{9,8},{10,9... | collective-permute-start | bytes 786440 | tf_op jit(solution)/shard_map/ppermute | solution.py:296
  97.0 10.8 %collective-permute-start.3 = (bf16[528,256]{1,0:T(8,128)(2,1)}, bf16[528,256]{1,0:T(8,128)(2,1)S(1)}, u32[]{:S(2)}, u32[]{:S(2)}) collective-permute-start(bf16[528,256]{1,0:T(8,128)(2,1)} %get-tuple-element.25), channel_id=1, source_target_pairs={{0,1},{1,2},{2,3},{3,0},{4,5},{5,6},{6,7},{7,4},{8,9},{9,10},{10,1... | collective-permute-start | bytes 811016 | tf_op jit(solution)/shard_map/ppermute | solution.py:296
  99.5 13.0 %collective-permute-start.4 = (bf16[528,256]{1,0:T(8,128)(2,1)}, bf16[528,256]{1,0:T(8,128)(2,1)S(1)}, u32[]{:S(2)}, u32[]{:S(2)}) collective-permute-start(bf16[528,256]{1,0:T(8,128)(2,1)} %get-tuple-element.26), channel_id=1, source_target_pairs={{0,2},{1,3},{2,0},{3,1},{4,6},{5,7},{6,4},{7,5},{8,10},{9,11},{10,... | collective-permute-start | bytes 811016 | tf_op jit(solution)/shard_map/ppermute | solution.py:296
  104.5 11.3 %collective-permute-start.5 = (bf16[528,256]{1,0:T(8,128)(2,1)}, bf16[528,256]{1,0:T(8,128)(2,1)S(1)}, u32[]{:S(2)}, u32[]{:S(2)}) collective-permute-start(bf16[528,256]{1,0:T(8,128)(2,1)} %get-tuple-element.27), channel_id=1, source_target_pairs={{0,3},{1,0},{2,1},{3,2},{4,7},{5,4},{6,5},{7,6},{8,11},{9,8},{10,9... | collective-permute-start | bytes 811016 | tf_op jit(solution)/shard_map/ppermute | solution.py:296
  115.7 10.6 %copy-start.3 = (s32[128,2]{0,1:T(2,128)S(1)}, s32[128,2]{0,1:T(2,128)}, u32[]{:S(2)}) copy-start(s32[128,2]{0,1:T(2,128)} %param.8) | copy-start | bytes 3076
  116.2 33.6 %copy-start.4 = (f32[128,2]{0,1:T(2,128)S(1)}, f32[128,2]{0,1:T(2,128)}, u32[]{:S(2)}) copy-start(f32[128,2]{0,1:T(2,128)} %param.9) | copy-start | bytes 3076
  117.2 32.4 %all-to-all-start.3 = ((bf16[128,4,640]{2,1,0:T(4,128)(2,1)}), bf16[128,4,640]{2,1,0:T(4,128)(2,1)S(1)}, u32[]{:S(2)}, u32[]{:S(2)}) async-start(bf16[128,4,640]{2,1,0:T(4,128)(2,1)} %reshape.24), calls=%async_computation.3 | async-start | bytes 1310720 | tf_op jit(solution)/shard_map/all_to_all | solution.py:422

commit v5 on v4

--- a/solution.py
+++ b/solution.py
@@ -105,7 +105,7 @@
 ):
     parts, slots, quarter = rows_ref.shape
     piece = [slice(q * quarter, (q + 1) * quarter) for q in range(parts)]
-    outer_copy = fetch(outer_in, outer_ref, sems.at[parts])
+    outer_copy = fetch(outer_in, outer_ref, sems.at[0])
     acc = None
     for q in range(parts):
         term = jnp.dot(rows_ref[q], inner_ref[piece[q], :], preferred_element_type=jnp.float32)
@@ -131,28 +131,28 @@
 
     lax.fori_loop(0, slots // step, activate, 0)
     saves = [
-        fetch(hidden_ref, hidden_out, sems.at[parts + 1]),
-        fetch(slope_ref, slope_out, sems.at[parts + 2]),
+        fetch(hidden_ref, hidden_out, sems.at[1]),
+        fetch(slope_ref, slope_out, sems.at[2]),
     ]
     outer_copy.wait()
     for q in range(parts):
         outs_ref[q] = jnp.dot(
             hidden_ref[...], outer_ref[:, piece[q]], preferred_element_type=jnp.float32
         ).astype(jnp.bfloat16)
-        saves.append(fetch(outs_ref.at[q], outs_out.at[q], sems.at[parts + 3 + q]))
+        saves.append(fetch(outs_ref.at[q], outs_out.at[q], sems.at[3 + q]))
     for copy in saves:
         copy.wait()
 
 
 def backward_kernel(parts, me_ref, *refs):
-    cot_ins, (hidden_in, slope_in, inner_in, outer_ref) = refs[:parts], refs[parts : parts + 4]
-    in_outs = refs[parts + 4 : 2 * parts + 4]
+    cot_ins, (hidden_in, slope_in, inner_in, outer_in) = refs[:parts], refs[parts : parts + 4]
+    in_refs = refs[parts + 4 : 2 * parts + 4]
     (
         cot_ref,
         hidden_ref,
         slope_ref,
         inner_ref,
-        in_ref,
+        outer_ref,
         back_ref,
         grad_ref,
         pre_ref,
@@ -162,20 +162,26 @@
     width = back_ref.shape[1]
     across = (((1,), (1,)), ((), ()))
     piece = [slice(q * quarter, (q + 1) * quarter) for q in range(parts)]
-    first = [fetch(cot_ins[i], cot_ref.at[i], sems.at[i]) for i in range(parts)]
-    copies = [
-        fetch(source, target, sems.at[2 * parts + i])
-        for i, (source, target) in enumerate(
-            ((slope_in, slope_ref), (hidden_in, hidden_ref), (inner_in, inner_ref))
+
+    def operands(shift):
+        of = quarter_of(lax.rem(me_ref[0] + parts - shift, parts), quarter)
+        return (
+            fetch(cot_ins[shift], cot_ref.at[shift], sems.at[2 * shift]),
+            fetch(outer_in.at[:, of], outer_ref.at[:, piece[shift]], sems.at[2 * shift + 1]),
         )
-    ]
+
+    later = ((slope_in, slope_ref), (hidden_in, hidden_ref), (inner_in, inner_ref))
+    first = [operands(shift) for shift in range(parts)]
+    copies = []
     acc = None
     for shift in range(parts):
-        first[shift].wait()
-        of = quarter_of(lax.rem(me_ref[0] + parts - shift, parts), quarter)
+        for copy in first[shift]:
+            copy.wait()
+        if shift < len(later):
+            copies.append(fetch(*later[shift], sems.at[2 * parts + shift]))
         term = lax.dot_general(
             cot_ref[shift],
-            outer_ref[:, of],
+            outer_ref[:, piece[shift]],
             across,
             preferred_element_type=jnp.float32,
         )
@@ -197,6 +203,12 @@
         return carry
 
     lax.fori_loop(0, slots // step, activate, 0)
+    copies[2].wait()
+    for shift in range(parts):
+        of = quarter_of(lax.rem(me_ref[0] + shift, parts), quarter)
+        in_refs[shift][:slots, :] = lax.dot_general(
+            pre_ref[...], inner_ref[of, :], across, preferred_element_type=jnp.float32
+        ).astype(jnp.bfloat16)
     gate = lax.dot_general(
         jnp.ones((8, 128), jnp.float32),
         grad_ref[...],
@@ -211,17 +223,8 @@
     for j in range(slots // quarter):
         extra = jnp.where(place == 2 * j, high[:, piece[j]], extra)
         extra = jnp.where(place == 2 * j + 1, low[:, piece[j]], extra)
-    copies[2].wait()
-    saves = []
     for shift in range(parts):
-        of = quarter_of(lax.rem(me_ref[0] + shift, parts), quarter)
-        in_ref[shift, :slots, :] = lax.dot_general(
-            pre_ref[...], inner_ref[of, :], across, preferred_element_type=jnp.float32
-        ).astype(jnp.bfloat16)
-        in_ref[shift, slots:, :] = extra.astype(jnp.bfloat16)
-        saves.append(fetch(in_ref.at[shift], in_outs[shift], sems.at[2 * parts + 3 + shift]))
-    for copy in saves:
-        copy.wait()
+        in_refs[shift][slots:, :] = extra.astype(jnp.bfloat16)
 
 
 def in_pairs(terms):
@@ -232,10 +235,8 @@
     return in_pairs([wide[i] + wide[i + half] for i in range(half)])
 
 
-def add_outs_kernel(outs_ref, own_in, sum_ref, own_ref, sem):
-    copy = fetch(own_in, own_ref, sem)
+def add_outs_kernel(outs_ref, sum_ref):
     sum_ref[...] = in_pairs([outs_ref[q] for q in range(outs_ref.shape[0])]).astype(jnp.bfloat16)
-    copy.wait()
 
 
 def add_kernel(out_ref, *refs):
@@ -379,7 +380,7 @@
             pltpu.VMEM((slots, width), half),
             pltpu.VMEM((slots, width), half),
             pltpu.VMEM((slots, width), full),
-            pltpu.SemaphoreType.DMA((2 * parts + 3,)),
+            pltpu.SemaphoreType.DMA((parts + 3,)),
         ],
         compiler_params=PARAMS,
         name="forward",
@@ -387,38 +388,36 @@
     outs = lax.all_to_all(outs, "rep", 0, 0, tiled=True)
     ins = pl.pallas_call(
         lambda *refs: backward_kernel(parts, *refs),
-        out_shape=(pltpu.HBM((slots + EXTRA, quarter), half),) * parts,
-        in_specs=[smem_spec] + [any_spec] * (parts + 3) + [vmem_spec],
-        out_specs=(any_spec,) * parts,
+        out_shape=(shape_of((slots + EXTRA, quarter), half),) * parts,
+        in_specs=[smem_spec] + [any_spec] * (parts + 4),
+        out_specs=(vmem_spec,) * parts,
         scratch_shapes=[
             pltpu.VMEM((parts, slots, quarter), half),
             pltpu.VMEM((slots, width), half),
             pltpu.VMEM((slots, width), half),
             pltpu.VMEM((depth, width), half),
-            pltpu.VMEM((parts, slots + EXTRA, quarter), half),
+            pltpu.VMEM((width, depth), half),
             pltpu.VMEM((slots, width), full),
             pltpu.VMEM((slots, 128), full),
             pltpu.VMEM((slots, width), half),
-            pltpu.SemaphoreType.DMA((3 * parts + 3,)),
+            pltpu.SemaphoreType.DMA((2 * parts + 3,)),
         ],
         compiler_params=PARAMS,
         name="backward",
-    )(me, *all_cots, *[in_hbm(x) for x in (hidden, slope, inner)], outer)
+    )(me, *all_cots, *[in_hbm(x) for x in (hidden, slope, inner, outer)])
     arrivals = sent_on(ins, "rep")
-    out, own = pl.pallas_call(
+    out = pl.pallas_call(
         add_outs_kernel,
-        out_shape=(shape_of((slots, quarter), half), shape_of((slots + EXTRA, quarter), half)),
-        in_specs=[vmem_spec, any_spec],
-        scratch_shapes=[pltpu.SemaphoreType.DMA(())],
+        out_shape=shape_of((slots, quarter), half),
         compiler_params=PARAMS,
         name="add_outs",
-    )(outs, in_hbm(arrivals[0]))
+    )(outs)
     summed = pl.pallas_call(
         add_kernel,
         out_shape=shape_of((slots, 2 * quarter + 128), half),
         compiler_params=PARAMS,
         name="add",
-    )(out, own, *arrivals[1:])
+    )(out, *arrivals)
     back = lax.all_to_all(
         summed.reshape(peers, -1, 2 * quarter + 128), "expert", 0, 0, tiled=True
     ).reshape(slots, 2 * quarter + 128)

time: 152 us -> 151 us (level)
  transfers between devices with their start and end apart: 8 -> 8, of which waited for: 6 -> 7; matrix products, arithmetic and copies ran while one was open for 0% -> 0% of each run, Pallas kernels for 5% -> 4%
where the time goes in v5:
time: 151 us; the launch traced here: 150 us
  blocking collectives  55.3 us (37%)
  waiting for transfers between devices  43.4 us (29%)
  starting transfers between devices  34.5 us (23%)
  Pallas kernels  14.9 us (10%)
    all_to_all x1, blocking collectives, exchange(): lax.all_to_all(packed.reshape(peers, -1, 2 * quarter), 'expert', 0, 0, ti...  38.2 us
    all_to_all x1, waiting for transfers between devices, exchange(): lax.all_to_all(summed.reshape(peers, -1, 2 * quarter + 128), 'expert', 0,...  22.7 us
    ppermute x6, waiting for transfers between devices, shift_by(): lax.ppermute(x, axis, [(i, (i + shift) % peers) for i in range(peers)])  20.6 us
    ppermute x6, starting transfers between devices, shift_by(): lax.ppermute(x, axis, [(i, (i + shift) % peers) for i in range(peers)])  20.2 us
    all_to_all x1, blocking collectives, exchange(): all_rows = lax.all_to_all(copied, 'rep', 0, 0, tiled=True)  17.1 us
    all_to_all x1, starting transfers between devices, exchange(): lax.all_to_all(summed.reshape(peers, -1, 2 * quarter + 128), 'expert', 0,...  9.16 us
    pallas_call x1, Pallas kernels, exchange(): pl.pallas_call(lambda *refs: backward_kernel(parts, *refs), out_shape=(sh...  5.17 us
    all_to_all x1, starting transfers between devices, exchange(): outs = lax.all_to_all(outs, 'rep', 0, 0, tiled=True)  5.1 us
  transfers between devices with their start and end apart: 8, of which 7 were waited for; matrix products, arithmetic and copies ran while one was open for 0% of the time, Pallas kernels for 4%

profile of v5, /device:TPU:2, one launch (start us, length us, event | category | flops | bytes accessed | tf_op | source)
XLA Modules:
  0.0 150.2 jit_solution(13378338502756020770)
XLA Ops:
  0.6 1.5 pack.1
  2.1 0.1 reshape.21
  2.2 38.2 %all_to_all.20 = bf16[128,4,512]{2,1,0:T(4,128)(2,1)S(1)} all-to-all(bf16[128,4,512]{2,1,0:T(4,128)(2,1)S(1)} %reshape.21), channel_id=1, replica_groups=mesh['expert'=128,'rep'=4] {'expert'}, dimensions={0} | all-to-all | bytes 1048576 | tf_op jit(solution)/shard_map/all_to_all | solution.py:342
  40.4 0.0 copy-start
  40.4 0.1 reshape.22.arrived_ref
  40.6 1.1 spread.1
  41.7 17.1 %all_to_all.21.rows_ref = bf16[4,512,256]{2,1,0:T(8,128)(2,1)S(1)} all-to-all(bf16[4,512,256]{2,1,0:T(8,128)(2,1)} %get-tuple-element.15), channel_id=1, replica_groups=mesh['expert'=128,'rep'=4] {'rep'}, dimensions={0} | all-to-all | bytes 2097152 | tf_op jit(solution)/shard_map/all_to_all | solution.py:354
  58.8 0.0 copy-done
  58.8 4.8 %forward.1 = (bf16[4,512,256]{2,1,0:T(8,128)(2,1)}, bf16[512,1024]{1,0:T(8,128)(2,1)}, bf16[512,1024]{1,0:T(8,128)(2,1)}) custom-call(bf16[4,512,256]{2,1,0:T(8,128)(2,1)S(1)} %all_to_all.21.rows_ref, bf16[1024,1024]{1,0:T(8,128)(2,1)S(1)} %bitcast.7, bf16[1024,1024]{1,0:T(8,128)(2,1)} %bitcast.12), custom_call_target="tpu_custom_call" | custom-call | tf_op jit(solution)/shard_map/forward/pallas_call | solution.py:368
  63.6 0.0 copy-start.1
  63.6 5.1 %all-to-all-start.2 = ((bf16[4,512,256]{2,1,0:T(8,128)(2,1)}), bf16[4,512,256]{2,1,0:T(8,128)(2,1)S(1)}, u32[]{:S(2)}, u32[]{:S(2)}) async-start(bf16[4,512,256]{2,1,0:T(8,128)(2,1)} %get-tuple-element.16), calls=%async_computation.2 | async-start | bytes 2097152 | tf_op jit(solution)/shard_map/all_to_all | solution.py:388
  68.7 0.0 copy-done.1
  68.7 3.4 %collective-permute-start = (bf16[512,256]{1,0:T(8,128)(2,1)S(1)}, bf16[512,256]{1,0:T(8,128)(2,1)S(1)}, u32[]{:S(2)}, u32[]{:S(2)}) collective-permute-start(bf16[512,256]{1,0:T(8,128)(2,1)S(1)} %copy-done.1), channel_id=1, source_target_pairs={{0,1},{1,2},{2,3},{3,0},{4,5},{5,6},{6,7},{7,4},{8,9},{9,10},{10,1... | collective-permute-start | bytes 786440 | tf_op jit(solution)/shard_map/ppermute | solution.py:297
  72.1 2.6 %collective-permute-start.1 = (bf16[512,256]{1,0:T(8,128)(2,1)S(1)}, bf16[512,256]{1,0:T(8,128)(2,1)S(1)}, u32[]{:S(2)}, u32[]{:S(2)}) collective-permute-start(bf16[512,256]{1,0:T(8,128)(2,1)S(1)} %copy-done.1), channel_id=1, source_target_pairs={{0,2},{1,3},{2,0},{3,1},{4,6},{5,7},{6,4},{7,5},{8,10},{9,11},{10,... | collective-permute-start | bytes 786440 | tf_op jit(solution)/shard_map/ppermute | solution.py:297
  74.7 4.5 %collective-permute-start.2 = (bf16[512,256]{1,0:T(8,128)(2,1)S(1)}, bf16[512,256]{1,0:T(8,128)(2,1)S(1)}, u32[]{:S(2)}, u32[]{:S(2)}) collective-permute-start(bf16[512,256]{1,0:T(8,128)(2,1)S(1)} %copy-done.1), channel_id=1, source_target_pairs={{0,3},{1,0},{2,1},{3,2},{4,7},{5,4},{6,5},{7,6},{8,11},{9,8},{10,9... | collective-permute-start | bytes 786440 | tf_op jit(solution)/shard_map/ppermute | solution.py:297
  79.2 7.6 %collective-permute-done.refs_2_ = bf16[512,256]{1,0:T(8,128)(2,1)S(1)} collective-permute-done((bf16[512,256]{1,0:T(8,128)(2,1)S(1)}, bf16[512,256]{1,0:T(8,128)(2,1)S(1)}, u32[]{:S(2)}, u32[]{:S(2)}) %collective-permute-start) | collective-permute-done | bytes 262176 | tf_op jit(solution)/shard_map/ppermute | solution.py:297
  86.8 1.7 %collective-permute-done.1.refs_3_ = bf16[512,256]{1,0:T(8,128)(2,1)S(1)} collective-permute-done((bf16[512,256]{1,0:T(8,128)(2,1)S(1)}, bf16[512,256]{1,0:T(8,128)(2,1)S(1)}, u32[]{:S(2)}, u32[]{:S(2)}) %collective-permute-start.1) | collective-permute-done | bytes 262176 | tf_op jit(solution)/shard_map/ppermute | solution.py:297
  88.5 2.8 %collective-permute-done.2.refs_4_ = bf16[512,256]{1,0:T(8,128)(2,1)S(1)} collective-permute-done((bf16[512,256]{1,0:T(8,128)(2,1)S(1)}, bf16[512,256]{1,0:T(8,128)(2,1)S(1)}, u32[]{:S(2)}, u32[]{:S(2)}) %collective-permute-start.2) | collective-permute-done | bytes 262176 | tf_op jit(solution)/shard_map/ppermute | solution.py:297
  91.3 5.2 %backward.1 = (bf16[528,256]{1,0:T(8,128)(2,1)S(1)}, bf16[528,256]{1,0:T(8,128)(2,1)S(1)}, bf16[528,256]{1,0:T(8,128)(2,1)S(1)}, bf16[528,256]{1,0:T(8,128)(2,1)S(1)}) custom-call(s32[1]{0:T(128)} %bitcast.4.refs_0_, bf16[512,256]{1,0:T(8,128)(2,1)S(1)} %copy-done.1, bf16[512,256]{1,0:T(8,128)(2,1)S(1)} %collective-permute-done.refs_2_, ...), custom_call_target="tpu_custom_call" | custom-call | tf_op jit(solution)/shard_map/backward/pallas_call | solution.py:389
  96.5 2.5 %collective-permute-start.3 = (bf16[528,256]{1,0:T(8,128)(2,1)S(1)}, bf16[528,256]{1,0:T(8,128)(2,1)S(1)}, u32[]{:S(2)}, u32[]{:S(2)}) collective-permute-start(bf16[528,256]{1,0:T(8,128)(2,1)S(1)} %get-tuple-element.21), channel_id=1, source_target_pairs={{0,1},{1,2},{2,3},{3,0},{4,5},{5,6},{6,7},{7,4},{8,9},{9,10},{10,1... | collective-permute-start | bytes 811016 | tf_op jit(solution)/shard_map/ppermute | solution.py:297
  99.0 4.9 %collective-permute-start.4 = (bf16[528,256]{1,0:T(8,128)(2,1)S(1)}, bf16[528,256]{1,0:T(8,128)(2,1)S(1)}, u32[]{:S(2)}, u32[]{:S(2)}) collective-permute-start(bf16[528,256]{1,0:T(8,128)(2,1)S(1)} %get-tuple-element.22), channel_id=1, source_target_pairs={{0,2},{1,3},{2,0},{3,1},{4,6},{5,7},{6,4},{7,5},{8,10},{9,11},{10,... | collective-permute-start | bytes 811016 | tf_op jit(solution)/shard_map/ppermute | solution.py:297
  103.9 2.4 %collective-permute-start.5 = (bf16[528,256]{1,0:T(8,128)(2,1)S(1)}, bf16[528,256]{1,0:T(8,128)(2,1)S(1)}, u32[]{:S(2)}, u32[]{:S(2)}) collective-permute-start(bf16[528,256]{1,0:T(8,128)(2,1)S(1)} %get-tuple-element.23), channel_id=1, source_target_pairs={{0,3},{1,0},{2,1},{3,2},{4,7},{5,4},{6,5},{7,6},{8,11},{9,8},{10,9... | collective-permute-start | bytes 811016 | tf_op jit(solution)/shard_map/ppermute | solution.py:297
  106.3 0.0 all-to-all-done.2.outs_ref
  106.4 0.1 add_outs.1.out_ref
  106.5 0.6 collective-permute-done.3.refs_1_
  107.1 4.7 %collective-permute-done.4.refs_2_ = bf16[528,256]{1,0:T(8,128)(2,1)S(1)} collective-permute-done((bf16[528,256]{1,0:T(8,128)(2,1)S(1)}, bf16[528,256]{1,0:T(8,128)(2,1)S(1)}, u32[]{:S(2)}, u32[]{:S(2)}) %collective-permute-start.4) | collective-permute-done | bytes 270368 | tf_op jit(solution)/shard_map/ppermute | solution.py:297
  111.7 3.2 %collective-permute-done.5.refs_3_ = bf16[528,256]{1,0:T(8,128)(2,1)S(1)} collective-permute-done((bf16[528,256]{1,0:T(8,128)(2,1)S(1)}, bf16[528,256]{1,0:T(8,128)(2,1)S(1)}, u32[]{:S(2)}, u32[]{:S(2)}) %collective-permute-start.5) | collective-permute-done | bytes 270368 | tf_op jit(solution)/shard_map/ppermute | solution.py:297
  115.0 0.0 copy-start.2
  115.0 0.4 add.1
  115.4 0.0 copy-start.3
  115.4 1.0 reshape.24
  116.4 9.2 %all-to-all-start.3 = ((bf16[128,4,640]{2,1,0:T(4,128)(2,1)}), bf16[128,4,640]{2,1,0:T(4,128)(2,1)S(1)}, u32[]{:S(2)}, u32[]{:S(2)}) async-start(bf16[128,4,640]{2,1,0:T(4,128)(2,1)} %reshape.24), calls=%async_computation.3 | async-start | bytes 1310720 | tf_op jit(solution)/shard_map/all_to_all | solution.py:421
  125.6 0.0 copy-done.2
  125.6 0.3 shard_map.85.refs_0_
  125.9 0.3 shard_map.86.refs_1_
  126.2 22.7 %all-to-all-done.3 = bf16[128,4,640]{2,1,0:T(4,128)(2,1)S(1)} async-done(((bf16[128,4,640]{2,1,0:T(4,128)(2,1)}), bf16[128,4,640]{2,1,0:T(4,128)(2,1)S(1)}, u32[]{:S(2)}, u32[]{:S(2)}) %all-to-all-start.3) | async-done | bytes 655392 | tf_op jit(solution)/shard_map/all_to_all | solution.py:421
  148.9 0.1 reshape.25.refs_3_
  149.0 0.0 copy-done.3
  149.0 1.2 combine.1
Async XLA Ops:
  40.4 18.3 %copy-start = (bf16[1,1024,1024]{2,1,0:T(8,128)(2,1)S(1)}, bf16[1,1024,1024]{2,1,0:T(8,128)(2,1)}, u32[]{:S(2)}) copy-start(bf16[1,1024,1024]{2,1,0:T(8,128)(2,1)} %param.10) | copy-start | bytes 6291460
  63.6 5.1 %copy-start.1 = (bf16[512,256]{1,0:T(8,128)(2,1)S(1)}, bf16[512,256]{1,0:T(8,128)(2,1)}, u32[]{:S(2)}) copy-start(bf16[512,256]{1,0:T(8,128)(2,1)} %get-tuple-element.17.refs_1_) | copy-start | bytes 786436
  63.6 42.7 %all-to-all-start.2 = ((bf16[4,512,256]{2,1,0:T(8,128)(2,1)}), bf16[4,512,256]{2,1,0:T(8,128)(2,1)S(1)}, u32[]{:S(2)}, u32[]{:S(2)}) async-start(bf16[4,512,256]{2,1,0:T(8,128)(2,1)} %get-tuple-element.16), calls=%async_computation.2 | async-start | bytes 2097152 | tf_op jit(solution)/shard_map/all_to_all | solution.py:388
  68.7 18.1 %collective-permute-start = (bf16[512,256]{1,0:T(8,128)(2,1)S(1)}, bf16[512,256]{1,0:T(8,128)(2,1)S(1)}, u32[]{:S(2)}, u32[]{:S(2)}) collective-permute-start(bf16[512,256]{1,0:T(8,128)(2,1)S(1)} %copy-done.1), channel_id=1, source_target_pairs={{0,1},{1,2},{2,3},{3,0},{4,5},{5,6},{6,7},{7,4},{8,9},{9,10},{10,1... | collective-permute-start | bytes 786440 | tf_op jit(solution)/shard_map/ppermute | solution.py:297
  72.1 16.4 %collective-permute-start.1 = (bf16[512,256]{1,0:T(8,128)(2,1)S(1)}, bf16[512,256]{1,0:T(8,128)(2,1)S(1)}, u32[]{:S(2)}, u32[]{:S(2)}) collective-permute-start(bf16[512,256]{1,0:T(8,128)(2,1)S(1)} %copy-done.1), channel_id=1, source_target_pairs={{0,2},{1,3},{2,0},{3,1},{4,6},{5,7},{6,4},{7,5},{8,10},{9,11},{10,... | collective-permute-start | bytes 786440 | tf_op jit(solution)/shard_map/ppermute | solution.py:297
  74.7 16.7 %collective-permute-start.2 = (bf16[512,256]{1,0:T(8,128)(2,1)S(1)}, bf16[512,256]{1,0:T(8,128)(2,1)S(1)}, u32[]{:S(2)}, u32[]{:S(2)}) collective-permute-start(bf16[512,256]{1,0:T(8,128)(2,1)S(1)} %copy-done.1), channel_id=1, source_target_pairs={{0,3},{1,0},{2,1},{3,2},{4,7},{5,4},{6,5},{7,6},{8,11},{9,8},{10,9... | collective-permute-start | bytes 786440 | tf_op jit(solution)/shard_map/ppermute | solution.py:297
  96.5 10.6 %collective-permute-start.3 = (bf16[528,256]{1,0:T(8,128)(2,1)S(1)}, bf16[528,256]{1,0:T(8,128)(2,1)S(1)}, u32[]{:S(2)}, u32[]{:S(2)}) collective-permute-start(bf16[528,256]{1,0:T(8,128)(2,1)S(1)} %get-tuple-element.21), channel_id=1, source_target_pairs={{0,1},{1,2},{2,3},{3,0},{4,5},{5,6},{6,7},{7,4},{8,9},{9,10},{10,1... | collective-permute-start | bytes 811016 | tf_op jit(solution)/shard_map/ppermute | solution.py:297
  99.0 12.8 %collective-permute-start.4 = (bf16[528,256]{1,0:T(8,128)(2,1)S(1)}, bf16[528,256]{1,0:T(8,128)(2,1)S(1)}, u32[]{:S(2)}, u32[]{:S(2)}) collective-permute-start(bf16[528,256]{1,0:T(8,128)(2,1)S(1)} %get-tuple-element.22), channel_id=1, source_target_pairs={{0,2},{1,3},{2,0},{3,1},{4,6},{5,7},{6,4},{7,5},{8,10},{9,11},{10,... | collective-permute-start | bytes 811016 | tf_op jit(solution)/shard_map/ppermute | solution.py:297
  103.9 11.1 %collective-permute-start.5 = (bf16[528,256]{1,0:T(8,128)(2,1)S(1)}, bf16[528,256]{1,0:T(8,128)(2,1)S(1)}, u32[]{:S(2)}, u32[]{:S(2)}) collective-permute-start(bf16[528,256]{1,0:T(8,128)(2,1)S(1)} %get-tuple-element.23), channel_id=1, source_target_pairs={{0,3},{1,0},{2,1},{3,2},{4,7},{5,4},{6,5},{7,6},{8,11},{9,8},{10,9... | collective-permute-start | bytes 811016 | tf_op jit(solution)/shard_map/ppermute | solution.py:297
  115.0 10.6 %copy-start.2 = (s32[128,2]{0,1:T(2,128)S(1)}, s32[128,2]{0,1:T(2,128)}, u32[]{:S(2)}) copy-start(s32[128,2]{0,1:T(2,128)} %param.8) | copy-start | bytes 3076
  115.4 33.6 %copy-start.3 = (f32[128,2]{0,1:T(2,128)S(1)}, f32[128,2]{0,1:T(2,128)}, u32[]{:S(2)}) copy-start(f32[128,2]{0,1:T(2,128)} %param.9) | copy-start | bytes 3076
  116.4 32.5 %all-to-all-start.3 = ((bf16[128,4,640]{2,1,0:T(4,128)(2,1)}), bf16[128,4,640]{2,1,0:T(4,128)(2,1)S(1)}, u32[]{:S(2)}, u32[]{:S(2)}) async-start(bf16[128,4,640]{2,1,0:T(4,128)(2,1)} %reshape.24), calls=%async_computation.3 | async-start | bytes 1310720 | tf_op jit(solution)/shard_map/all_to_all | solution.py:421

commit v6 on v5

--- a/solution.py
+++ b/solution.py
@@ -69,12 +69,12 @@
         ).astype(jnp.bfloat16)
 
 
-def spread_kernel(arrived_ref, rows_out, cots_out, sems):
+def spread_kernel(arrived_ref, rows_out, cots_ref, sems):
     parts, _, quarter = rows_out.shape
     copies = [
         fetch(arrived_ref.at[:, :quarter], rows_out.at[q], sems.at[q]) for q in range(parts)
     ]
-    copies.append(fetch(arrived_ref.at[:, quarter:], cots_out, sems.at[parts]))
+    cots_ref[...] = arrived_ref[:, quarter:]
     for copy in copies:
         copy.wait()
 
@@ -270,23 +270,32 @@
         ).astype(jnp.bfloat16)
 
 
-def table_kernel(experts, capacity, k, ids_ref, table_ref):
+def table_kernel(experts, capacity, ids_ref, table_ref):
     rows = ids_ref.shape[1]
-    position = slot_positions(ids_ref[...], experts, capacity)[k]
-    hit = iota((rows, experts * capacity), 1) == column_of(position)
-    table_ref[...] = jnp.where(hit, 1.0, 0.0).astype(jnp.bfloat16)
-
-
-def combine_kernel(*refs):
-    table_refs, gates_ref, back_ref = refs[:TOP], refs[TOP], refs[TOP + 1]
-    out_ref, in_ref, gate_ref = refs[TOP + 2 :]
-    quarter = out_ref.shape[1]
+    positions = slot_positions(ids_ref[...], experts, capacity)
+    slot = iota((rows, experts * capacity), 1)
+    for k in range(TOP):
+        hit = slot == column_of(positions[k])
+        table_ref[k * rows : (k + 1) * rows, :] = jnp.where(hit, 1.0, 0.0).astype(jnp.bfloat16)
+
+
+def gates_kernel(gates_ref, wide_ref):
+    rows, lanes = gates_ref.shape[1], wide_ref.shape[1]
+    for k in range(TOP):
+        wide_ref[k * rows : (k + 1) * rows, :] = jnp.broadcast_to(
+            column_of(gates_ref[k : k + 1, :]), (rows, lanes)
+        )
+
+
+def combine_kernel(table_ref, gates_ref, back_ref, out_ref, in_ref, gate_ref):
+    rows, quarter = out_ref.shape
+    picked = jnp.dot(table_ref[...], back_ref[...], preferred_element_type=jnp.float32)
     total = None
     for k in range(TOP):
-        picked = jnp.dot(table_refs[k][...], back_ref[...], preferred_element_type=jnp.float32)
-        term = column_of(gates_ref[k : k + 1, :]) * picked[:, : 2 * quarter]
+        mine = picked[k * rows : (k + 1) * rows, :]
+        term = gates_ref[k * rows : (k + 1) * rows, :] * mine[:, : 2 * quarter]
         total = term if total is None else total + term
-        gate = picked[:, 2 * quarter : 2 * quarter + 1] + picked[:, 2 * quarter + 1 : 2 * quarter + 2]
+        gate = mine[:, 2 * quarter : 2 * quarter + 1] + mine[:, 2 * quarter + 1 : 2 * quarter + 2]
         gate_ref[k : k + 1, :] = row_of(gate)
     out_ref[...] = total[:, :quarter].astype(jnp.bfloat16)
     in_ref[...] = total[:, quarter:].astype(jnp.bfloat16)
@@ -344,24 +353,27 @@
     ).reshape(slots, 2 * quarter)
     copied, cots = pl.pallas_call(
         spread_kernel,
-        out_shape=(pltpu.HBM((parts, slots, quarter), half), pltpu.HBM((slots, quarter), half)),
+        out_shape=(pltpu.HBM((parts, slots, quarter), half), shape_of((slots, quarter), half)),
         in_specs=[vmem_spec],
-        out_specs=(any_spec, any_spec),
-        scratch_shapes=[pltpu.SemaphoreType.DMA((parts + 1,))],
+        out_specs=(any_spec, vmem_spec),
+        scratch_shapes=[pltpu.SemaphoreType.DMA((parts,))],
         compiler_params=PARAMS,
         name="spread",
     )(arrived)
     all_rows = lax.all_to_all(copied, "rep", 0, 0, tiled=True)
     all_cots = sent_on([cots] * parts, "rep")
-    tables = []
-    for k in range(TOP):
-        tables.append(
-            pl.pallas_call(
-                lambda *refs: table_kernel(experts, capacity, k, *refs),
-                out_shape=shape_of((rows, slots), half),
-                compiler_params=PARAMS,
-            )(ids)
-        )
+    table = pl.pallas_call(
+        lambda *refs: table_kernel(experts, capacity, *refs),
+        out_shape=shape_of((TOP * rows, slots), half),
+        compiler_params=PARAMS,
+        name="table",
+    )(ids)
+    wide_gates = pl.pallas_call(
+        gates_kernel,
+        out_shape=shape_of((TOP * rows, 2 * quarter), full),
+        compiler_params=PARAMS,
+        name="gates",
+    )(gates)
     me = lax.axis_index("rep").astype(jnp.int32).reshape(1)
     smem_spec = pl.BlockSpec(memory_space=pltpu.SMEM)
 
@@ -430,7 +442,7 @@
         ),
         compiler_params=PARAMS,
         name="combine",
-    )(*tables, gates, back)
+    )(table, wide_gates, back)
     return output, input_grads, gate_grads.T
 
 

time: 151 us -> 150 us (level)
  no operation moved by 1% of the time
where the time goes in v6:
time: 150 us
  blocking collectives  55.3 us (37%)
  waiting for transfers between devices  43.5 us (29%)
  starting transfers between devices  34.3 us (23%)
  Pallas kernels  14.5 us (10%)
    all_to_all x1, blocking collectives, exchange(): lax.all_to_all(packed.reshape(peers, -1, 2 * quarter), 'expert', 0, 0, ti...  38.2 us
    all_to_all x1, waiting for transfers between devices, exchange(): lax.all_to_all(summed.reshape(peers, -1, 2 * quarter + 128), 'expert', 0,...  22.8 us
    ppermute x6, waiting for transfers between devices, shift_by(): lax.ppermute(x, axis, [(i, (i + shift) % peers) for i in range(peers)])  20.7 us
    ppermute x6, starting transfers between devices, shift_by(): lax.ppermute(x, axis, [(i, (i + shift) % peers) for i in range(peers)])  20.2 us
    all_to_all x1, blocking collectives, exchange(): all_rows = lax.all_to_all(copied, 'rep', 0, 0, tiled=True)  17.1 us
    all_to_all x1, starting transfers between devices, exchange(): lax.all_to_all(summed.reshape(peers, -1, 2 * quarter + 128), 'expert', 0,...  9.14 us
    pallas_call x1, Pallas kernels, exchange(): pl.pallas_call(lambda *refs: backward_kernel(parts, *refs), out_shape=(sh...  5.17 us
    all_to_all x1, starting transfers between devices, exchange(): outs = lax.all_to_all(outs, 'rep', 0, 0, tiled=True)  4.95 us
  transfers between devices with their start and end apart: 8, of which 7 were waited for; matrix products, arithmetic and copies ran while one was open for 0% of the time, Pallas kernels for 4%

profile of v6, /device:TPU:2, one launch (start us, length us, event | category | flops | bytes accessed | tf_op | source)
XLA Modules:
  0.0 149.8 jit_solution(2805210986596039616)
XLA Ops:
  0.6 1.5 pack.1
  2.1 0.1 reshape.21
  2.2 38.2 %all_to_all.20 = bf16[128,4,512]{2,1,0:T(4,128)(2,1)S(1)} all-to-all(bf16[128,4,512]{2,1,0:T(4,128)(2,1)S(1)} %reshape.21), channel_id=1, replica_groups=mesh['expert'=128,'rep'=4] {'expert'}, dimensions={0} | all-to-all | bytes 1048576 | tf_op jit(solution)/shard_map/all_to_all | solution.py:351
  40.4 0.0 copy-start
  40.4 0.1 reshape.22.arrived_ref
  40.6 1.0 spread.1
  41.6 17.1 %all_to_all.21.rows_ref = bf16[4,512,256]{2,1,0:T(8,128)(2,1)S(1)} all-to-all(bf16[4,512,256]{2,1,0:T(8,128)(2,1)} %get-tuple-element.15), channel_id=1, replica_groups=mesh['expert'=128,'rep'=4] {'rep'}, dimensions={0} | all-to-all | bytes 2097152 | tf_op jit(solution)/shard_map/all_to_all | solution.py:363
  58.7 0.0 copy-done
  58.7 4.9 %forward.1 = (bf16[4,512,256]{2,1,0:T(8,128)(2,1)}, bf16[512,1024]{1,0:T(8,128)(2,1)}, bf16[512,1024]{1,0:T(8,128)(2,1)}) custom-call(bf16[4,512,256]{2,1,0:T(8,128)(2,1)S(1)} %all_to_all.21.rows_ref, bf16[1024,1024]{1,0:T(8,128)(2,1)S(1)} %bitcast.7, bf16[1024,1024]{1,0:T(8,128)(2,1)} %bitcast.11), custom_call_target="tpu_custom_call" | custom-call | tf_op jit(solution)/shard_map/forward/pallas_call | solution.py:380
  63.5 4.9 %all-to-all-start.2 = ((bf16[4,512,256]{2,1,0:T(8,128)(2,1)}), bf16[4,512,256]{2,1,0:T(8,128)(2,1)S(1)}, u32[]{:S(2)}, u32[]{:S(2)}) async-start(bf16[4,512,256]{2,1,0:T(8,128)(2,1)} %get-tuple-element.16), calls=%async_computation.2 | async-start | bytes 2097152 | tf_op jit(solution)/shard_map/all_to_all | solution.py:400
  68.5 3.4 %collective-permute-start = (bf16[512,256]{1,0:T(8,128)(2,1)S(1)}, bf16[512,256]{1,0:T(8,128)(2,1)S(1)}, u32[]{:S(2)}, u32[]{:S(2)}) collective-permute-start(bf16[512,256]{1,0:T(8,128)(2,1)S(1)} %get-tuple-element.17.refs_1_), channel_id=1, source_target_pairs={{0,1},{1,2},{2,3},{3,0},{4,5},{5,6},{6,7},{7,4},{8,9},{9,10},{10,1... | collective-permute-start | bytes 786440 | tf_op jit(solution)/shard_map/ppermute | solution.py:306
  71.8 2.6 %collective-permute-start.1 = (bf16[512,256]{1,0:T(8,128)(2,1)S(1)}, bf16[512,256]{1,0:T(8,128)(2,1)S(1)}, u32[]{:S(2)}, u32[]{:S(2)}) collective-permute-start(bf16[512,256]{1,0:T(8,128)(2,1)S(1)} %get-tuple-element.17.refs_1_), channel_id=1, source_target_pairs={{0,2},{1,3},{2,0},{3,1},{4,6},{5,7},{6,4},{7,5},{8,10},{9,11},{10,... | collective-permute-start | bytes 786440 | tf_op jit(solution)/shard_map/ppermute | solution.py:306
  74.4 4.5 %collective-permute-start.2 = (bf16[512,256]{1,0:T(8,128)(2,1)S(1)}, bf16[512,256]{1,0:T(8,128)(2,1)S(1)}, u32[]{:S(2)}, u32[]{:S(2)}) collective-permute-start(bf16[512,256]{1,0:T(8,128)(2,1)S(1)} %get-tuple-element.17.refs_1_), channel_id=1, source_target_pairs={{0,3},{1,0},{2,1},{3,2},{4,7},{5,4},{6,5},{7,6},{8,11},{9,8},{10,9... | collective-permute-start | bytes 786440 | tf_op jit(solution)/shard_map/ppermute | solution.py:306
  78.9 7.6 %collective-permute-done.refs_2_ = bf16[512,256]{1,0:T(8,128)(2,1)S(1)} collective-permute-done((bf16[512,256]{1,0:T(8,128)(2,1)S(1)}, bf16[512,256]{1,0:T(8,128)(2,1)S(1)}, u32[]{:S(2)}, u32[]{:S(2)}) %collective-permute-start) | collective-permute-done | bytes 262176 | tf_op jit(solution)/shard_map/ppermute | solution.py:306
  86.5 1.7 %collective-permute-done.1.refs_3_ = bf16[512,256]{1,0:T(8,128)(2,1)S(1)} collective-permute-done((bf16[512,256]{1,0:T(8,128)(2,1)S(1)}, bf16[512,256]{1,0:T(8,128)(2,1)S(1)}, u32[]{:S(2)}, u32[]{:S(2)}) %collective-permute-start.1) | collective-permute-done | bytes 262176 | tf_op jit(solution)/shard_map/ppermute | solution.py:306
  88.3 2.8 %collective-permute-done.2.refs_4_ = bf16[512,256]{1,0:T(8,128)(2,1)S(1)} collective-permute-done((bf16[512,256]{1,0:T(8,128)(2,1)S(1)}, bf16[512,256]{1,0:T(8,128)(2,1)S(1)}, u32[]{:S(2)}, u32[]{:S(2)}) %collective-permute-start.2) | collective-permute-done | bytes 262176 | tf_op jit(solution)/shard_map/ppermute | solution.py:306
  91.1 5.2 %backward.1 = (bf16[528,256]{1,0:T(8,128)(2,1)S(1)}, bf16[528,256]{1,0:T(8,128)(2,1)S(1)}, bf16[528,256]{1,0:T(8,128)(2,1)S(1)}, bf16[528,256]{1,0:T(8,128)(2,1)S(1)}) custom-call(s32[1]{0:T(128)} %bitcast.4.refs_0_, bf16[512,256]{1,0:T(8,128)(2,1)S(1)} %get-tuple-element.17.refs_1_, bf16[512,256]{1,0:T(8,128)(2,1)S(1)} %collective-permute-done.refs_2_, ...), custom_call_target="tpu_custom_call" | custom-call | tf_op jit(solution)/shard_map/backward/pallas_call | solution.py:401
  96.3 2.5 %collective-permute-start.3 = (bf16[528,256]{1,0:T(8,128)(2,1)S(1)}, bf16[528,256]{1,0:T(8,128)(2,1)S(1)}, u32[]{:S(2)}, u32[]{:S(2)}) collective-permute-start(bf16[528,256]{1,0:T(8,128)(2,1)S(1)} %get-tuple-element.21), channel_id=1, source_target_pairs={{0,1},{1,2},{2,3},{3,0},{4,5},{5,6},{6,7},{7,4},{8,9},{9,10},{10,1... | collective-permute-start | bytes 811016 | tf_op jit(solution)/shard_map/ppermute | solution.py:306
  98.7 4.9 %collective-permute-start.4 = (bf16[528,256]{1,0:T(8,128)(2,1)S(1)}, bf16[528,256]{1,0:T(8,128)(2,1)S(1)}, u32[]{:S(2)}, u32[]{:S(2)}) collective-permute-start(bf16[528,256]{1,0:T(8,128)(2,1)S(1)} %get-tuple-element.22), channel_id=1, source_target_pairs={{0,2},{1,3},{2,0},{3,1},{4,6},{5,7},{6,4},{7,5},{8,10},{9,11},{10,... | collective-permute-start | bytes 811016 | tf_op jit(solution)/shard_map/ppermute | solution.py:306
  103.7 2.4 %collective-permute-start.5 = (bf16[528,256]{1,0:T(8,128)(2,1)S(1)}, bf16[528,256]{1,0:T(8,128)(2,1)S(1)}, u32[]{:S(2)}, u32[]{:S(2)}) collective-permute-start(bf16[528,256]{1,0:T(8,128)(2,1)S(1)} %get-tuple-element.23), channel_id=1, source_target_pairs={{0,3},{1,0},{2,1},{3,2},{4,7},{5,4},{6,5},{7,6},{8,11},{9,8},{10,9... | collective-permute-start | bytes 811016 | tf_op jit(solution)/shard_map/ppermute | solution.py:306
  106.1 0.0 all-to-all-done.2.outs_ref
  106.1 0.1 add_outs.1.out_ref
  106.2 0.6 collective-permute-done.3.refs_1_
  106.8 4.7 %collective-permute-done.4.refs_2_ = bf16[528,256]{1,0:T(8,128)(2,1)S(1)} collective-permute-done((bf16[528,256]{1,0:T(8,128)(2,1)S(1)}, bf16[528,256]{1,0:T(8,128)(2,1)S(1)}, u32[]{:S(2)}, u32[]{:S(2)}) %collective-permute-start.4) | collective-permute-done | bytes 270368 | tf_op jit(solution)/shard_map/ppermute | solution.py:306
  111.5 3.2 %collective-permute-done.5.refs_3_ = bf16[528,256]{1,0:T(8,128)(2,1)S(1)} collective-permute-done((bf16[528,256]{1,0:T(8,128)(2,1)S(1)}, bf16[528,256]{1,0:T(8,128)(2,1)S(1)}, u32[]{:S(2)}, u32[]{:S(2)}) %collective-permute-start.5) | collective-permute-done | bytes 270368 | tf_op jit(solution)/shard_map/ppermute | solution.py:306
  114.7 0.0 copy-start.1
  114.7 0.0 copy-start.2
  114.7 0.4 add.1
  115.2 1.0 reshape.24
  116.2 9.1 %all-to-all-start.3 = ((bf16[128,4,640]{2,1,0:T(4,128)(2,1)}), bf16[128,4,640]{2,1,0:T(4,128)(2,1)S(1)}, u32[]{:S(2)}, u32[]{:S(2)}) async-start(bf16[128,4,640]{2,1,0:T(4,128)(2,1)} %reshape.24), calls=%async_computation.3 | async-start | bytes 1310720 | tf_op jit(solution)/shard_map/all_to_all | solution.py:433
  125.3 0.0 copy-done.1
  125.3 0.3 table.1.table_ref
  125.6 0.0 copy-done.2
  125.6 0.1 gates.1.gates_ref
  125.8 22.8 %all-to-all-done.3 = bf16[128,4,640]{2,1,0:T(4,128)(2,1)S(1)} async-done(((bf16[128,4,640]{2,1,0:T(4,128)(2,1)}), bf16[128,4,640]{2,1,0:T(4,128)(2,1)S(1)}, u32[]{:S(2)}, u32[]{:S(2)}) %all-to-all-start.3) | async-done | bytes 655392 | tf_op jit(solution)/shard_map/all_to_all | solution.py:433
  148.6 0.1 reshape.25.back_ref
  148.7 1.1 combine.1
Async XLA Ops:
  40.4 18.2 %copy-start = (bf16[1,1024,1024]{2,1,0:T(8,128)(2,1)S(1)}, bf16[1,1024,1024]{2,1,0:T(8,128)(2,1)}, u32[]{:S(2)}) copy-start(bf16[1,1024,1024]{2,1,0:T(8,128)(2,1)} %param.10) | copy-start | bytes 6291460
  63.5 42.6 %all-to-all-start.2 = ((bf16[4,512,256]{2,1,0:T(8,128)(2,1)}), bf16[4,512,256]{2,1,0:T(8,128)(2,1)S(1)}, u32[]{:S(2)}, u32[]{:S(2)}) async-start(bf16[4,512,256]{2,1,0:T(8,128)(2,1)} %get-tuple-element.16), calls=%async_computation.2 | async-start | bytes 2097152 | tf_op jit(solution)/shard_map/all_to_all | solution.py:400
  68.5 18.1 %collective-permute-start = (bf16[512,256]{1,0:T(8,128)(2,1)S(1)}, bf16[512,256]{1,0:T(8,128)(2,1)S(1)}, u32[]{:S(2)}, u32[]{:S(2)}) collective-permute-start(bf16[512,256]{1,0:T(8,128)(2,1)S(1)} %get-tuple-element.17.refs_1_), channel_id=1, source_target_pairs={{0,1},{1,2},{2,3},{3,0},{4,5},{5,6},{6,7},{7,4},{8,9},{9,10},{10,1... | collective-permute-start | bytes 786440 | tf_op jit(solution)/shard_map/ppermute | solution.py:306
  71.8 16.4 %collective-permute-start.1 = (bf16[512,256]{1,0:T(8,128)(2,1)S(1)}, bf16[512,256]{1,0:T(8,128)(2,1)S(1)}, u32[]{:S(2)}, u32[]{:S(2)}) collective-permute-start(bf16[512,256]{1,0:T(8,128)(2,1)S(1)} %get-tuple-element.17.refs_1_), channel_id=1, source_target_pairs={{0,2},{1,3},{2,0},{3,1},{4,6},{5,7},{6,4},{7,5},{8,10},{9,11},{10,... | collective-permute-start | bytes 786440 | tf_op jit(solution)/shard_map/ppermute | solution.py:306
  74.4 16.7 %collective-permute-start.2 = (bf16[512,256]{1,0:T(8,128)(2,1)S(1)}, bf16[512,256]{1,0:T(8,128)(2,1)S(1)}, u32[]{:S(2)}, u32[]{:S(2)}) collective-permute-start(bf16[512,256]{1,0:T(8,128)(2,1)S(1)} %get-tuple-element.17.refs_1_), channel_id=1, source_target_pairs={{0,3},{1,0},{2,1},{3,2},{4,7},{5,4},{6,5},{7,6},{8,11},{9,8},{10,9... | collective-permute-start | bytes 786440 | tf_op jit(solution)/shard_map/ppermute | solution.py:306
  96.3 10.6 %collective-permute-start.3 = (bf16[528,256]{1,0:T(8,128)(2,1)S(1)}, bf16[528,256]{1,0:T(8,128)(2,1)S(1)}, u32[]{:S(2)}, u32[]{:S(2)}) collective-permute-start(bf16[528,256]{1,0:T(8,128)(2,1)S(1)} %get-tuple-element.21), channel_id=1, source_target_pairs={{0,1},{1,2},{2,3},{3,0},{4,5},{5,6},{6,7},{7,4},{8,9},{9,10},{10,1... | collective-permute-start | bytes 811016 | tf_op jit(solution)/shard_map/ppermute | solution.py:306
  98.7 12.8 %collective-permute-start.4 = (bf16[528,256]{1,0:T(8,128)(2,1)S(1)}, bf16[528,256]{1,0:T(8,128)(2,1)S(1)}, u32[]{:S(2)}, u32[]{:S(2)}) collective-permute-start(bf16[528,256]{1,0:T(8,128)(2,1)S(1)} %get-tuple-element.22), channel_id=1, source_target_pairs={{0,2},{1,3},{2,0},{3,1},{4,6},{5,7},{6,4},{7,5},{8,10},{9,11},{10,... | collective-permute-start | bytes 811016 | tf_op jit(solution)/shard_map/ppermute | solution.py:306
  103.7 11.1 %collective-permute-start.5 = (bf16[528,256]{1,0:T(8,128)(2,1)S(1)}, bf16[528,256]{1,0:T(8,128)(2,1)S(1)}, u32[]{:S(2)}, u32[]{:S(2)}) collective-permute-start(bf16[528,256]{1,0:T(8,128)(2,1)S(1)} %get-tuple-element.23), channel_id=1, source_target_pairs={{0,3},{1,0},{2,1},{3,2},{4,7},{5,4},{6,5},{7,6},{8,11},{9,8},{10,9... | collective-permute-start | bytes 811016 | tf_op jit(solution)/shard_map/ppermute | solution.py:306
  114.7 10.6 %copy-start.1 = (s32[128,2]{0,1:T(2,128)S(1)}, s32[128,2]{0,1:T(2,128)}, u32[]{:S(2)}) copy-start(s32[128,2]{0,1:T(2,128)} %param.8) | copy-start | bytes 3076
  114.7 10.9 %copy-start.2 = (f32[128,2]{0,1:T(2,128)S(1)}, f32[128,2]{0,1:T(2,128)}, u32[]{:S(2)}) copy-start(f32[128,2]{0,1:T(2,128)} %param.9) | copy-start | bytes 3076
  116.2 32.4 %all-to-all-start.3 = ((bf16[128,4,640]{2,1,0:T(4,128)(2,1)}), bf16[128,4,640]{2,1,0:T(4,128)(2,1)S(1)}, u32[]{:S(2)}, u32[]{:S(2)}) async-start(bf16[128,4,640]{2,1,0:T(4,128)(2,1)} %reshape.24), calls=%async_computation.3 | async-start | bytes 1310720 | tf_op jit(solution)/shard_map/all_to_all | solution.py:433

commit v7 on v5

--- a/solution.py
+++ b/solution.py
@@ -89,17 +89,24 @@
     return pl.ds(pl.multiple_of(index * size, size), size)
 
 
+def gelu_parts(u):
+    square = u * u
+    tangent = jnp.tanh(u * (SQRT_TWO_PI + (SQRT_TWO_PI * CUBIC) * square))
+    share = 0.5 + 0.5 * tangent
+    result = u * share
+    return result, share, 2.0 * SQRT_TWO_PI + (6.0 * SQRT_TWO_PI * CUBIC) * square
+
+
 def forward_kernel(
     rows_ref,
     inner_ref,
     outer_in,
     outs_out,
-    hidden_out,
-    slope_out,
+    save_out,
     outer_ref,
     outs_ref,
     hidden_ref,
-    slope_ref,
+    save_ref,
     pre_ref,
     sems,
 ):
@@ -116,48 +123,28 @@
     def activate(i, carry):
         at = pl.ds(pl.multiple_of(i * step, step), step)
         u = pre_ref[at, :]
-        square = u * u
-        tangent = jnp.tanh(u * (SQRT_TWO_PI + (SQRT_TWO_PI * CUBIC) * square))
-        share = 0.5 + 0.5 * tangent
-        result = u * share
-        hidden_ref[at, :] = result.astype(jnp.bfloat16)
-        slope_ref[at, :] = (
-            share
-            + result
-            * (1.0 - share)
-            * (2.0 * SQRT_TWO_PI + (6.0 * SQRT_TWO_PI * CUBIC) * square)
-        ).astype(jnp.bfloat16)
+        hidden_ref[at, :] = gelu_parts(u)[0].astype(jnp.bfloat16)
+        save_ref[at, :] = u.astype(jnp.bfloat16)
         return carry
 
     lax.fori_loop(0, slots // step, activate, 0)
-    saves = [
-        fetch(hidden_ref, hidden_out, sems.at[1]),
-        fetch(slope_ref, slope_out, sems.at[2]),
-    ]
+    saves = [fetch(save_ref, save_out, sems.at[1])]
     outer_copy.wait()
     for q in range(parts):
         outs_ref[q] = jnp.dot(
             hidden_ref[...], outer_ref[:, piece[q]], preferred_element_type=jnp.float32
         ).astype(jnp.bfloat16)
-        saves.append(fetch(outs_ref.at[q], outs_out.at[q], sems.at[3 + q]))
+        saves.append(fetch(outs_ref.at[q], outs_out.at[q], sems.at[2 + q]))
     for copy in saves:
         copy.wait()
 
 
 def backward_kernel(parts, me_ref, *refs):
-    cot_ins, (hidden_in, slope_in, inner_in, outer_in) = refs[:parts], refs[parts : parts + 4]
-    in_refs = refs[parts + 4 : 2 * parts + 4]
-    (
-        cot_ref,
-        hidden_ref,
-        slope_ref,
-        inner_ref,
-        outer_ref,
-        back_ref,
-        grad_ref,
-        pre_ref,
-        sems,
-    ) = refs[2 * parts + 4 :]
+    cot_ins, (saved_in, inner_in, outer_in) = refs[:parts], refs[parts : parts + 3]
+    in_refs = refs[parts + 3 : 2 * parts + 3]
+    cot_ref, saved_ref, inner_ref, outer_ref, back_ref, grad_ref, pre_ref, sems = refs[
+        2 * parts + 3 :
+    ]
     slots, quarter = cot_ref.shape[1:]
     width = back_ref.shape[1]
     across = (((1,), (1,)), ((), ()))
@@ -170,7 +157,7 @@
             fetch(outer_in.at[:, of], outer_ref.at[:, piece[shift]], sems.at[2 * shift + 1]),
         )
 
-    later = ((slope_in, slope_ref), (hidden_in, hidden_ref), (inner_in, inner_ref))
+    later = ((saved_in, saved_ref), (inner_in, inner_ref))
     first = [operands(shift) for shift in range(parts)]
     copies = []
     acc = None
@@ -188,14 +175,15 @@
         acc = term if acc is None else acc + term
     back_ref[...] = acc
     copies[0].wait()
-    copies[1].wait()
     step = 16
 
     def activate(i, carry):
         at = pl.ds(pl.multiple_of(i * step, step), step)
         back = back_ref[at, :]
-        pre_ref[at, :] = (back * slope_ref[at, :].astype(jnp.float32)).astype(jnp.bfloat16)
-        product = back * hidden_ref[at, :].astype(jnp.float32)
+        result, share, factor = gelu_parts(saved_ref[at, :].astype(jnp.float32))
+        slope = share + result * (1.0 - share) * factor
+        pre_ref[at, :] = (back * slope).astype(jnp.bfloat16)
+        product = back * result
         folded = product[:, :128]
         for j in range(1, width // 128):
             folded = folded + product[:, j * 128 : (j + 1) * 128]
@@ -203,7 +191,7 @@
         return carry
 
     lax.fori_loop(0, slots // step, activate, 0)
-    copies[2].wait()
+    copies[1].wait()
     for shift in range(parts):
         of = quarter_of(lax.rem(me_ref[0] + shift, parts), quarter)
         in_refs[shift][:slots, :] = lax.dot_general(
@@ -365,22 +353,21 @@
     me = lax.axis_index("rep").astype(jnp.int32).reshape(1)
     smem_spec = pl.BlockSpec(memory_space=pltpu.SMEM)
 
-    outs, hidden, slope = pl.pallas_call(
+    outs, saved = pl.pallas_call(
         forward_kernel,
         out_shape=(
             pltpu.HBM((parts, slots, quarter), half),
             pltpu.HBM((slots, width), half),
-            pltpu.HBM((slots, width), half),
         ),
         in_specs=[vmem_spec, vmem_spec, any_spec],
-        out_specs=(any_spec,) * 3,
+        out_specs=(any_spec,) * 2,
         scratch_shapes=[
             pltpu.VMEM((width, depth), half),
             pltpu.VMEM((parts, slots, quarter), half),
             pltpu.VMEM((slots, width), half),
             pltpu.VMEM((slots, width), half),
             pltpu.VMEM((slots, width), full),
-            pltpu.SemaphoreType.DMA((parts + 3,)),
+            pltpu.SemaphoreType.DMA((parts + 2,)),
         ],
         compiler_params=PARAMS,
         name="forward",
@@ -389,22 +376,21 @@
     ins = pl.pallas_call(
         lambda *refs: backward_kernel(parts, *refs),
         out_shape=(shape_of((slots + EXTRA, quarter), half),) * parts,
-        in_specs=[smem_spec] + [any_spec] * (parts + 4),
+        in_specs=[smem_spec] + [any_spec] * (parts + 3),
         out_specs=(vmem_spec,) * parts,
         scratch_shapes=[
             pltpu.VMEM((parts, slots, quarter), half),
-            pltpu.VMEM((slots, width), half),
             pltpu.VMEM((slots, width), half),
             pltpu.VMEM((depth, width), half),
             pltpu.VMEM((width, depth), half),
             pltpu.VMEM((slots, width), full),
             pltpu.VMEM((slots, 128), full),
             pltpu.VMEM((slots, width), half),
-            pltpu.SemaphoreType.DMA((2 * parts + 3,)),
+            pltpu.SemaphoreType.DMA((2 * parts + 2,)),
         ],
         compiler_params=PARAMS,
         name="backward",
-    )(me, *all_cots, *[in_hbm(x) for x in (hidden, slope, inner, outer)])
+    )(me, *all_cots, *[in_hbm(x) for x in (saved, inner, outer)])
     arrivals = sent_on(ins, "rep")
     out = pl.pallas_call(
         add_outs_kernel,

time: 151 us -> 151 us (level)
  no operation moved by 1% of the time
where the time goes in v7:
time: 151 us
  blocking collectives  55.3 us (37%)
  waiting for transfers between devices  43.4 us (29%)
  starting transfers between devices  34.5 us (23%)
  Pallas kernels  15.5 us (10%)
    all_to_all x1, blocking collectives, exchange(): lax.all_to_all(packed.reshape(peers, -1, 2 * quarter), 'expert', 0, 0, ti...  38.2 us
    all_to_all x1, waiting for transfers between devices, exchange(): lax.all_to_all(summed.reshape(peers, -1, 2 * quarter + 128), 'expert', 0,...  22.7 us
    ppermute x6, waiting for transfers between devices, shift_by(): lax.ppermute(x, axis, [(i, (i + shift) % peers) for i in range(peers)])  20.6 us
    ppermute x6, starting transfers between devices, shift_by(): lax.ppermute(x, axis, [(i, (i + shift) % peers) for i in range(peers)])  20.2 us
    all_to_all x1, blocking collectives, exchange(): all_rows = lax.all_to_all(copied, 'rep', 0, 0, tiled=True)  17.1 us
    all_to_all x1, starting transfers between devices, exchange(): lax.all_to_all(summed.reshape(peers, -1, 2 * quarter + 128), 'expert', 0,...  9.15 us
    pallas_call x1, Pallas kernels, exchange(): pl.pallas_call(lambda *refs: backward_kernel(parts, *refs), out_shape=(sh...  5.79 us
    all_to_all x1, starting transfers between devices, exchange(): outs = lax.all_to_all(outs, 'rep', 0, 0, tiled=True)  5.09 us
  transfers between devices with their start and end apart: 8, of which 7 were waited for; matrix products, arithmetic and copies ran while one was open for 0% of the time, Pallas kernels for 4%

profile of v7, /device:TPU:2, one launch (start us, length us, event | category | flops | bytes accessed | tf_op | source)
XLA Modules:
  0.0 150.9 jit_solution(12493812013040302864)
XLA Ops:
  0.6 1.5 pack.1
  2.1 0.1 reshape.21
  2.2 38.2 %all_to_all.20 = bf16[128,4,512]{2,1,0:T(4,128)(2,1)S(1)} all-to-all(bf16[128,4,512]{2,1,0:T(4,128)(2,1)S(1)} %reshape.21), channel_id=1, replica_groups=mesh['expert'=128,'rep'=4] {'expert'}, dimensions={0} | all-to-all | bytes 1048576 | tf_op jit(solution)/shard_map/all_to_all | solution.py:330
  40.4 0.0 copy-start
  40.4 0.1 reshape.22.arrived_ref
  40.6 1.2 spread.1
  41.7 17.1 %all_to_all.21.rows_ref = bf16[4,512,256]{2,1,0:T(8,128)(2,1)S(1)} all-to-all(bf16[4,512,256]{2,1,0:T(8,128)(2,1)} %get-tuple-element.14), channel_id=1, replica_groups=mesh['expert'=128,'rep'=4] {'rep'}, dimensions={0} | all-to-all | bytes 2097152 | tf_op jit(solution)/shard_map/all_to_all | solution.py:342
  58.8 0.0 copy-done
  58.8 4.8 %forward.1 = (bf16[4,512,256]{2,1,0:T(8,128)(2,1)}, bf16[512,1024]{1,0:T(8,128)(2,1)}) custom-call(bf16[4,512,256]{2,1,0:T(8,128)(2,1)S(1)} %all_to_all.21.rows_ref, bf16[1024,1024]{1,0:T(8,128)(2,1)S(1)} %bitcast.7, bf16[1024,1024]{1,0:T(8,128)(2,1)} %bitcast.12), custom_call_target="tpu_custom_call" | custom-call | tf_op jit(solution)/shard_map/forward/pallas_call | solution.py:356
  63.6 0.0 copy-start.1
  63.7 5.1 %all-to-all-start.2 = ((bf16[4,512,256]{2,1,0:T(8,128)(2,1)}), bf16[4,512,256]{2,1,0:T(8,128)(2,1)S(1)}, u32[]{:S(2)}, u32[]{:S(2)}) async-start(bf16[4,512,256]{2,1,0:T(8,128)(2,1)} %get-tuple-element.15), calls=%async_computation.2 | async-start | bytes 2097152 | tf_op jit(solution)/shard_map/all_to_all | solution.py:375
  68.7 0.0 copy-done.1
  68.7 3.4 %collective-permute-start = (bf16[512,256]{1,0:T(8,128)(2,1)S(1)}, bf16[512,256]{1,0:T(8,128)(2,1)S(1)}, u32[]{:S(2)}, u32[]{:S(2)}) collective-permute-start(bf16[512,256]{1,0:T(8,128)(2,1)S(1)} %copy-done.1), channel_id=1, source_target_pairs={{0,1},{1,2},{2,3},{3,0},{4,5},{5,6},{6,7},{7,4},{8,9},{9,10},{10,1... | collective-permute-start | bytes 786440 | tf_op jit(solution)/shard_map/ppermute | solution.py:285
  72.1 2.6 %collective-permute-start.1 = (bf16[512,256]{1,0:T(8,128)(2,1)S(1)}, bf16[512,256]{1,0:T(8,128)(2,1)S(1)}, u32[]{:S(2)}, u32[]{:S(2)}) collective-permute-start(bf16[512,256]{1,0:T(8,128)(2,1)S(1)} %copy-done.1), channel_id=1, source_target_pairs={{0,2},{1,3},{2,0},{3,1},{4,6},{5,7},{6,4},{7,5},{8,10},{9,11},{10,... | collective-permute-start | bytes 786440 | tf_op jit(solution)/shard_map/ppermute | solution.py:285
  74.7 4.5 %collective-permute-start.2 = (bf16[512,256]{1,0:T(8,128)(2,1)S(1)}, bf16[512,256]{1,0:T(8,128)(2,1)S(1)}, u32[]{:S(2)}, u32[]{:S(2)}) collective-permute-start(bf16[512,256]{1,0:T(8,128)(2,1)S(1)} %copy-done.1), channel_id=1, source_target_pairs={{0,3},{1,0},{2,1},{3,2},{4,7},{5,4},{6,5},{7,6},{8,11},{9,8},{10,9... | collective-permute-start | bytes 786440 | tf_op jit(solution)/shard_map/ppermute | solution.py:285
  79.2 7.6 %collective-permute-done.refs_2_ = bf16[512,256]{1,0:T(8,128)(2,1)S(1)} collective-permute-done((bf16[512,256]{1,0:T(8,128)(2,1)S(1)}, bf16[512,256]{1,0:T(8,128)(2,1)S(1)}, u32[]{:S(2)}, u32[]{:S(2)}) %collective-permute-start) | collective-permute-done | bytes 262176 | tf_op jit(solution)/shard_map/ppermute | solution.py:285
  86.8 1.7 %collective-permute-done.1.refs_3_ = bf16[512,256]{1,0:T(8,128)(2,1)S(1)} collective-permute-done((bf16[512,256]{1,0:T(8,128)(2,1)S(1)}, bf16[512,256]{1,0:T(8,128)(2,1)S(1)}, u32[]{:S(2)}, u32[]{:S(2)}) %collective-permute-start.1) | collective-permute-done | bytes 262176 | tf_op jit(solution)/shard_map/ppermute | solution.py:285
  88.5 2.8 %collective-permute-done.2.refs_4_ = bf16[512,256]{1,0:T(8,128)(2,1)S(1)} collective-permute-done((bf16[512,256]{1,0:T(8,128)(2,1)S(1)}, bf16[512,256]{1,0:T(8,128)(2,1)S(1)}, u32[]{:S(2)}, u32[]{:S(2)}) %collective-permute-start.2) | collective-permute-done | bytes 262176 | tf_op jit(solution)/shard_map/ppermute | solution.py:285
  91.3 5.8 %backward.1 = (bf16[528,256]{1,0:T(8,128)(2,1)S(1)}, bf16[528,256]{1,0:T(8,128)(2,1)S(1)}, bf16[528,256]{1,0:T(8,128)(2,1)S(1)}, bf16[528,256]{1,0:T(8,128)(2,1)S(1)}) custom-call(s32[1]{0:T(128)} %bitcast.4.refs_0_, bf16[512,256]{1,0:T(8,128)(2,1)S(1)} %copy-done.1, bf16[512,256]{1,0:T(8,128)(2,1)S(1)} %collective-permute-done.refs_2_, ...), custom_call_target="tpu_custom_call" | custom-call | tf_op jit(solution)/shard_map/backward/pallas_call | solution.py:376
  97.1 2.5 %collective-permute-start.3 = (bf16[528,256]{1,0:T(8,128)(2,1)S(1)}, bf16[528,256]{1,0:T(8,128)(2,1)S(1)}, u32[]{:S(2)}, u32[]{:S(2)}) collective-permute-start(bf16[528,256]{1,0:T(8,128)(2,1)S(1)} %get-tuple-element.19), channel_id=1, source_target_pairs={{0,1},{1,2},{2,3},{3,0},{4,5},{5,6},{6,7},{7,4},{8,9},{9,10},{10,1... | collective-permute-start | bytes 811016 | tf_op jit(solution)/shard_map/ppermute | solution.py:285
  99.6 4.9 %collective-permute-start.4 = (bf16[528,256]{1,0:T(8,128)(2,1)S(1)}, bf16[528,256]{1,0:T(8,128)(2,1)S(1)}, u32[]{:S(2)}, u32[]{:S(2)}) collective-permute-start(bf16[528,256]{1,0:T(8,128)(2,1)S(1)} %get-tuple-element.20), channel_id=1, source_target_pairs={{0,2},{1,3},{2,0},{3,1},{4,6},{5,7},{6,4},{7,5},{8,10},{9,11},{10,... | collective-permute-start | bytes 811016 | tf_op jit(solution)/shard_map/ppermute | solution.py:285
  104.6 2.4 %collective-permute-start.5 = (bf16[528,256]{1,0:T(8,128)(2,1)S(1)}, bf16[528,256]{1,0:T(8,128)(2,1)S(1)}, u32[]{:S(2)}, u32[]{:S(2)}) collective-permute-start(bf16[528,256]{1,0:T(8,128)(2,1)S(1)} %get-tuple-element.21), channel_id=1, source_target_pairs={{0,3},{1,0},{2,1},{3,2},{4,7},{5,4},{6,5},{7,6},{8,11},{9,8},{10,9... | collective-permute-start | bytes 811016 | tf_op jit(solution)/shard_map/ppermute | solution.py:285
  107.0 0.0 all-to-all-done.2.outs_ref
  107.0 0.1 add_outs.1.out_ref
  107.1 0.6 collective-permute-done.3.refs_1_
  107.7 4.7 %collective-permute-done.4.refs_2_ = bf16[528,256]{1,0:T(8,128)(2,1)S(1)} collective-permute-done((bf16[528,256]{1,0:T(8,128)(2,1)S(1)}, bf16[528,256]{1,0:T(8,128)(2,1)S(1)}, u32[]{:S(2)}, u32[]{:S(2)}) %collective-permute-start.4) | collective-permute-done | bytes 270368 | tf_op jit(solution)/shard_map/ppermute | solution.py:285
  112.4 3.2 %collective-permute-done.5.refs_3_ = bf16[528,256]{1,0:T(8,128)(2,1)S(1)} collective-permute-done((bf16[528,256]{1,0:T(8,128)(2,1)S(1)}, bf16[528,256]{1,0:T(8,128)(2,1)S(1)}, u32[]{:S(2)}, u32[]{:S(2)}) %collective-permute-start.5) | collective-permute-done | bytes 270368 | tf_op jit(solution)/shard_map/ppermute | solution.py:285
  115.6 0.0 copy-start.2
  115.6 0.4 add.1
  116.0 0.0 copy-start.3
  116.1 1.0 reshape.24
  117.1 9.2 %all-to-all-start.3 = ((bf16[128,4,640]{2,1,0:T(4,128)(2,1)}), bf16[128,4,640]{2,1,0:T(4,128)(2,1)S(1)}, u32[]{:S(2)}, u32[]{:S(2)}) async-start(bf16[128,4,640]{2,1,0:T(4,128)(2,1)} %reshape.24), calls=%async_computation.3 | async-start | bytes 1310720 | tf_op jit(solution)/shard_map/all_to_all | solution.py:407
  126.2 0.0 copy-done.2
  126.2 0.3 shard_map.85.refs_0_
  126.5 0.3 shard_map.86.refs_1_
  126.8 22.7 %all-to-all-done.3 = bf16[128,4,640]{2,1,0:T(4,128)(2,1)S(1)} async-done(((bf16[128,4,640]{2,1,0:T(4,128)(2,1)}), bf16[128,4,640]{2,1,0:T(4,128)(2,1)S(1)}, u32[]{:S(2)}, u32[]{:S(2)}) %all-to-all-start.3) | async-done | bytes 655392 | tf_op jit(solution)/shard_map/all_to_all | solution.py:407
  149.5 0.1 reshape.25.refs_3_
  149.7 0.0 copy-done.3
  149.7 1.2 combine.1
Async XLA Ops:
  40.4 18.4 %copy-start = (bf16[1,1024,1024]{2,1,0:T(8,128)(2,1)S(1)}, bf16[1,1024,1024]{2,1,0:T(8,128)(2,1)}, u32[]{:S(2)}) copy-start(bf16[1,1024,1024]{2,1,0:T(8,128)(2,1)} %param.10) | copy-start | bytes 6291460
  63.6 5.1 %copy-start.1 = (bf16[512,256]{1,0:T(8,128)(2,1)S(1)}, bf16[512,256]{1,0:T(8,128)(2,1)}, u32[]{:S(2)}) copy-start(bf16[512,256]{1,0:T(8,128)(2,1)} %get-tuple-element.16.refs_1_) | copy-start | bytes 786436
  63.7 43.3 %all-to-all-start.2 = ((bf16[4,512,256]{2,1,0:T(8,128)(2,1)}), bf16[4,512,256]{2,1,0:T(8,128)(2,1)S(1)}, u32[]{:S(2)}, u32[]{:S(2)}) async-start(bf16[4,512,256]{2,1,0:T(8,128)(2,1)} %get-tuple-element.15), calls=%async_computation.2 | async-start | bytes 2097152 | tf_op jit(solution)/shard_map/all_to_all | solution.py:375
  68.7 18.1 %collective-permute-start = (bf16[512,256]{1,0:T(8,128)(2,1)S(1)}, bf16[512,256]{1,0:T(8,128)(2,1)S(1)}, u32[]{:S(2)}, u32[]{:S(2)}) collective-permute-start(bf16[512,256]{1,0:T(8,128)(2,1)S(1)} %copy-done.1), channel_id=1, source_target_pairs={{0,1},{1,2},{2,3},{3,0},{4,5},{5,6},{6,7},{7,4},{8,9},{9,10},{10,1... | collective-permute-start | bytes 786440 | tf_op jit(solution)/shard_map/ppermute | solution.py:285
  72.1 16.4 %collective-permute-start.1 = (bf16[512,256]{1,0:T(8,128)(2,1)S(1)}, bf16[512,256]{1,0:T(8,128)(2,1)S(1)}, u32[]{:S(2)}, u32[]{:S(2)}) collective-permute-start(bf16[512,256]{1,0:T(8,128)(2,1)S(1)} %copy-done.1), channel_id=1, source_target_pairs={{0,2},{1,3},{2,0},{3,1},{4,6},{5,7},{6,4},{7,5},{8,10},{9,11},{10,... | collective-permute-start | bytes 786440 | tf_op jit(solution)/shard_map/ppermute | solution.py:285
  74.7 16.7 %collective-permute-start.2 = (bf16[512,256]{1,0:T(8,128)(2,1)S(1)}, bf16[512,256]{1,0:T(8,128)(2,1)S(1)}, u32[]{:S(2)}, u32[]{:S(2)}) collective-permute-start(bf16[512,256]{1,0:T(8,128)(2,1)S(1)} %copy-done.1), channel_id=1, source_target_pairs={{0,3},{1,0},{2,1},{3,2},{4,7},{5,4},{6,5},{7,6},{8,11},{9,8},{10,9... | collective-permute-start | bytes 786440 | tf_op jit(solution)/shard_map/ppermute | solution.py:285
  97.1 10.6 %collective-permute-start.3 = (bf16[528,256]{1,0:T(8,128)(2,1)S(1)}, bf16[528,256]{1,0:T(8,128)(2,1)S(1)}, u32[]{:S(2)}, u32[]{:S(2)}) collective-permute-start(bf16[528,256]{1,0:T(8,128)(2,1)S(1)} %get-tuple-element.19), channel_id=1, source_target_pairs={{0,1},{1,2},{2,3},{3,0},{4,5},{5,6},{6,7},{7,4},{8,9},{9,10},{10,1... | collective-permute-start | bytes 811016 | tf_op jit(solution)/shard_map/ppermute | solution.py:285
  99.6 12.7 %collective-permute-start.4 = (bf16[528,256]{1,0:T(8,128)(2,1)S(1)}, bf16[528,256]{1,0:T(8,128)(2,1)S(1)}, u32[]{:S(2)}, u32[]{:S(2)}) collective-permute-start(bf16[528,256]{1,0:T(8,128)(2,1)S(1)} %get-tuple-element.20), channel_id=1, source_target_pairs={{0,2},{1,3},{2,0},{3,1},{4,6},{5,7},{6,4},{7,5},{8,10},{9,11},{10,... | collective-permute-start | bytes 811016 | tf_op jit(solution)/shard_map/ppermute | solution.py:285
  104.6 11.1 %collective-permute-start.5 = (bf16[528,256]{1,0:T(8,128)(2,1)S(1)}, bf16[528,256]{1,0:T(8,128)(2,1)S(1)}, u32[]{:S(2)}, u32[]{:S(2)}) collective-permute-start(bf16[528,256]{1,0:T(8,128)(2,1)S(1)} %get-tuple-element.21), channel_id=1, source_target_pairs={{0,3},{1,0},{2,1},{3,2},{4,7},{5,4},{6,5},{7,6},{8,11},{9,8},{10,9... | collective-permute-start | bytes 811016 | tf_op jit(solution)/shard_map/ppermute | solution.py:285
  115.6 10.6 %copy-start.2 = (s32[128,2]{0,1:T(2,128)S(1)}, s32[128,2]{0,1:T(2,128)}, u32[]{:S(2)}) copy-start(s32[128,2]{0,1:T(2,128)} %param.8) | copy-start | bytes 3076
  116.0 33.6 %copy-start.3 = (f32[128,2]{0,1:T(2,128)S(1)}, f32[128,2]{0,1:T(2,128)}, u32[]{:S(2)}) copy-start(f32[128,2]{0,1:T(2,128)} %param.9) | copy-start | bytes 3076
  117.1 32.5 %all-to-all-start.3 = ((bf16[128,4,640]{2,1,0:T(4,128)(2,1)}), bf16[128,4,640]{2,1,0:T(4,128)(2,1)S(1)}, u32[]{:S(2)}, u32[]{:S(2)}) async-start(bf16[128,4,640]{2,1,0:T(4,128)(2,1)} %reshape.24), calls=%async_computation.3 | async-start | bytes 1310720 | tf_op jit(solution)/shard_map/all_to_all | solution.py:407
